TPU v7x, 256 devices: a whole 4x4x8 slice. The times are simulated.
256 devices in a mesh: row: 4 (over z_lo, core), col: 16 (over y, x), depth: 4 (over z_hi).
Axes of the slice: x: 4, y: 4, z: 8 (z_hi: 4, z_lo: 2; z = z_hi * 2 + z_lo), core: 2. Of those that a mesh axis runs over, the one named last changes fastest.
Arguments:
- diag_two: float32 [256, 256], replicated, may hold values from -3 to 3, as said below
- diag_one: float32 [256, 256], replicated, may hold values from -3 to 3, as said below
- cross_tile: float32 [256, 256], replicated, may hold values from -0.375 to 0.375
- left_two: float32 [256, 32768], P(None, ('col', 'depth')), may hold values from -0.375 to 0.375
- left_one: float32 [256, 32768], P(None, ('col', 'depth')), may hold values from -0.375 to 0.375
- below_left: float32 [4096, 32768], P('row', ('col', 'depth')), may hold values from -0.09375 to 0.09375
- panel_two: float32 [4096, 256], P('row', 'col'), may hold values from -0.09375 to 0.09375
- panel_one: float32 [4096, 256], P('row', 'col'), may hold values from -0.09375 to 0.09375
- grad_diag_two: float32 [256, 256], replicated, may hold values from -6 to 6
- grad_diag_one: float32 [256, 256], replicated, may hold values from -6 to 6
- grad_cross: float32 [256, 256], replicated, may hold values from -6 to 6
- grad_left_two: float32 [256, 32768], P('row', ('col', 'depth')), may hold values from -6 to 6
- grad_left_one: float32 [256, 32768], P('row', ('col', 'depth')), may hold values from -6 to 6
- grad_below: float32 [4096, 32768], P('row', ('col', 'depth')), may hold values from -6 to 6
- grad_panel_two: float32 [4096, 256], P('row', 'col'), may hold values from -6 to 6
- grad_panel_one: float32 [4096, 256], P('row', 'col'), may hold values from -6 to 6
Outputs:
- out_below: float32 [4096, 32768], P('row', ('col', 'depth'))
- out_left_two: float32 [256, 32768], P('row', ('col', 'depth'))
- out_left_one: float32 [256, 32768], P('row', ('col', 'depth'))
- out_diag_two: float32 [256, 256], replicated
- out_diag_one: float32 [256, 256], replicated
- out_cross: float32 [256, 256], replicated
- out_panel_two: float32 [4096, 256], P('row', 'col')
- out_panel_one: float32 [4096, 256], P('row', 'col')
Inputs may be any that keep to these rules, and one draw needn't show every extreme that they name: `diag_two`: lower triangular; its diagonal lies in 1 to 3. `diag_one`: lower triangular; its diagonal lies in 1 to 3.
All inputs are finite; a program needn't handle non-finite values.
Results may differ from a plain program's by a relative error of at most 0.000071.
Values sent between devices are 32-bit elements; how exact they have to be, the bound alone decides.
No kernel may reach another device: no remote copies, remote signals or barrier semaphores. Data moves between devices by JAX's collectives and lax.ppermute only.
A program may use at most 64 MiB of HBM per device.

v0:
```python
import jax
import jax.numpy as jnp
from jax import lax
from jax.sharding import PartitionSpec as P


def gather_turned(arrays, axis, dims):
    turned = [jnp.moveaxis(a, dim, 0) for a, dim in zip(arrays, dims)]
    both = jnp.concatenate([t.reshape(len(t), -1) for t in turned], axis=1)
    out, at, outs = (lax.all_gather(both, axis, axis=0, tiled=True), 0, [])
    for t, dim in zip(turned, dims):
        piece = out[:, at : at + t[0].size].reshape(-1, *t.shape[1:])
        outs.append(jnp.moveaxis(piece, 0, dim))
        at += t[0].size
    return tuple(outs)


def gathered_total(value, axis):
    blocks = lax.all_gather(value, axis)
    return blocks.sum(axis=0)


def sent_to_all(value, axis):
    count = lax.axis_size(axis)
    return lax.all_to_all(
        jnp.broadcast_to(value[None], (count, *value.shape)), axis, 0, 0, tiled=True
    )


def taken_together(value, axis):
    return sent_to_all(value, axis).sum(axis=0)


def in_blocks(value, dim, count):
    before, after = (value.shape[:dim], value.shape[dim + 1 :])
    return jnp.moveaxis(value.reshape(*before, count, -1, *after), dim, 0)


def sum_at_owner(value, axis, dim):
    count = lax.axis_size(axis)
    blocks = lax.all_to_all(in_blocks(value, dim, count), axis, 0, 0, tiled=True)
    return jnp.sum(blocks, axis=0)


def matmul(left, right):
    return jnp.dot(left, right, precision=lax.Precision.HIGHEST, preferred_element_type=jnp.float32)


def right_solve(factor, values):
    return lax.linalg.triangular_solve(factor, values, left_side=False, lower=True)


def halved(square):
    return jnp.tril(square) - 0.5 * jnp.diag(jnp.diag(square))


def reverse_block(factor, cotangent):
    inner = halved(matmul(factor.T, cotangent))
    leftward = lax.linalg.triangular_solve(
        factor, inner, left_side=True, lower=True, transpose_a=True
    )
    spread = right_solve(factor, leftward)
    return spread + spread.T


def body(
    diag_two,
    diag_one,
    cross_tile,
    left_two,
    left_one,
    below_left,
    panel_two,
    panel_one,
    grad_diag_two,
    grad_diag_one,
    grad_cross,
    grad_left_two,
    grad_left_one,
    grad_below,
    grad_panel_two,
    grad_panel_one,
):
    share = grad_left_two.shape[0]
    width = panel_two.shape[1]
    row_start = lax.axis_index("row") * share
    col_start = lax.axis_index("col") * width
    grad_two_all, panel_two_all, grad_one_all, panel_one_all = gather_turned(
        (grad_panel_two, panel_two, grad_panel_one, panel_one), "col", (1, 1, 1, 1)
    )
    solved_two = right_solve(diag_two, grad_two_all)
    gram_two, gram_cross = (
        gathered_total(matmul(solved_two.T, panel_two_all), "row"),
        gathered_total(matmul(solved_two.T, panel_one_all), "row"),
    )
    below_first = grad_below - matmul(solved_two, left_two)
    sym_two = reverse_block(diag_two, grad_diag_two - jnp.tril(gram_two))
    cross_next = grad_cross - gram_cross - matmul(sym_two, cross_tile)
    out_cross = right_solve(diag_one, cross_next)
    panel_next = grad_one_all - matmul(solved_two, cross_tile)
    out_panel_one = right_solve(diag_one, panel_next)
    gram_below = taken_together(matmul(out_panel_one.T, panel_one_all), "row")
    summed_both = sum_at_owner(
        jnp.concatenate(
            [matmul(solved_two.T, below_left), matmul(out_panel_one.T, below_left)], axis=1
        ),
        "row",
        0,
    )
    summed_two = summed_both[:, : left_two.shape[1]]
    summed_one = summed_both[:, left_two.shape[1] :]
    out_below = below_first - matmul(out_panel_one, left_one)
    gram_one = matmul(out_cross.T, cross_tile) + gram_below
    sym_one = reverse_block(diag_one, grad_diag_one - jnp.tril(gram_one))
    sym_two_rows = lax.dynamic_slice_in_dim(sym_two, row_start, share, 0)
    sym_one_rows = lax.dynamic_slice_in_dim(sym_one, row_start, share, 0)
    cross_rows = lax.dynamic_slice_in_dim(out_cross, row_start, share, 0)
    cross_cols = lax.dynamic_slice_in_dim(out_cross, row_start, share, 1)
    out_left_two = (
        grad_left_two - summed_two - matmul(sym_two_rows, left_two) - matmul(cross_rows, left_one)
    )
    out_left_one = (
        grad_left_one - matmul(cross_cols.T, left_two) - summed_one - matmul(sym_one_rows, left_one)
    )
    out_panel_two = lax.dynamic_slice_in_dim(solved_two, col_start, width, 1)
    panel_one_cols = lax.dynamic_slice_in_dim(out_panel_one, col_start, width, 1)
    return (
        out_below,
        out_left_two,
        out_left_one,
        halved(sym_two),
        halved(sym_one),
        out_cross,
        out_panel_two,
        panel_one_cols,
    )


def solution(mesh):
    return jax.shard_map(
        body,
        mesh=mesh,
        in_specs=(
            P(),
            P(),
            P(),
            P(None, ("col", "depth")),
            P(None, ("col", "depth")),
            P("row", ("col", "depth")),
            P("row", "col"),
            P("row", "col"),
            P(),
            P(),
            P(),
            P("row", ("col", "depth")),
            P("row", ("col", "depth")),
            P("row", ("col", "depth")),
            P("row", "col"),
            P("row", "col"),
        ),
        out_specs=(
            P("row", ("col", "depth")),
            P("row", ("col", "depth")),
            P("row", ("col", "depth")),
            P(),
            P(),
            P(),
            P("row", "col"),
            P("row", "col"),
        ),
        check_vma=False,
    )
```

profile of v0, /device:TPU:1, one launch (start us, length us, event | category | flops | bytes accessed | tf_op | source)
XLA Modules:
  0.0 182.9 jit_solution(14696959862518335248)
XLA Ops:
  7.3 1.8 pad_maximum_fusion.12
  9.2 1.0 fusion.17
  10.2 4.0 %while.14 = (s32[]{:T(128)}, f32[256,256]{1,0:T(8,128)S(1)}, s32[2,2]{1,0:T(2,128)S(1)}, f32[2,128,128]{2,1,0:T(8,128)S(1)}, s32[]{:T(128)}) while((s32[]{:T(128)}, f32[256,256]{1,0:T(8,128)S(1)}, s32[2,2]{1,0:T(2,128)S(1)}, f32[2,128,128]{2,1,0:T(8,128)S(1)}, s32[]{:T(128)}) %tuple.63), condition=%wide.while_cond, body=%wide.while_body.sunk | while | flops 2 | bytes 131181 | solution.py:50
  10.2 0.6 fusion.106
  10.8 1.4 bitcast_dynamic-update-slice_fusion.4
  12.2 0.6 fusion.106
  12.8 1.4 bitcast_dynamic-update-slice_fusion.4
  14.2 20.3 %custom-call.21 = f32[2,128,128]{1,2,0:T(8,128)} custom-call(f32[2,128,128]{2,1,0:T(8,128)S(1)} %get-tuple-element.59), custom_call_target="InvertDiagBlocksLowerTriangular" | custom-call | tf_op jit(solution)/shard_map/triangular_solve/custom-call.1 | solution.py:50
  34.5 0.8 copy.74
  35.4 4.0 %while.15 = (s32[]{:T(128)}, f32[256,256]{1,0:T(8,128)S(1)}, s32[2,2]{1,0:T(2,128)S(1)}, f32[2,128,128]{2,1,0:T(8,128)S(1)}, s32[]{:T(128)}) while((s32[]{:T(128)}, f32[256,256]{1,0:T(8,128)S(1)}, s32[2,2]{1,0:T(2,128)S(1)}, f32[2,128,128]{2,1,0:T(8,128)S(1)}, s32[]{:T(128)}) %tuple.75), condition=%wide.while_cond.clone, body=%wide.while_body.clone.sunk | while | flops 2 | bytes 131181 | solution.py:50
  35.4 0.6 fusion.107
  36.0 1.4 bitcast_dynamic-update-slice_fusion.5
  37.5 0.6 fusion.107
  38.0 1.4 bitcast_dynamic-update-slice_fusion.5
  39.4 19.9 %custom-call.22 = f32[2,128,128]{1,2,0:T(8,128)S(1)} custom-call(f32[2,128,128]{2,1,0:T(8,128)S(1)} %get-tuple-element.60), custom_call_target="InvertDiagBlocksLowerTriangular" | custom-call | tf_op jit(solution)/shard_map/triangular_solve/custom-call.1 | solution.py:50
  59.3 0.9 copy.81
  60.2 11.3 %all-gather.6.cloned.1.call-done = f32[256,4096]{1,0:T(8,128)} async-done(((f32[16,4096]{1,0:T(8,128)}), f32[256,4096]{1,0:T(8,128)}) %all-gather.6.cloned.1.call-update) | async-done | bytes 4194320 | tf_op jit(solution)/shard_map/all_gather | solution.py:10
  71.5 2.7 %fusion.74 = (f32[256,1024]{1,0:T(8,128)}, f32[256,1024]{1,0:T(8,128)S(1)}) fusion(f32[256,4096]{1,0:T(8,128)} %all-gather.6.cloned.1.call-done), kind=kLoop, calls=%fused_computation.134 | loop fusion | bytes 4194304 | tf_op jit(solution)/shard_map/slice | solution.py:12
  74.2 1.3 copy.94
  75.6 1.7 fusion.12
  77.3 2.1 %convolution_subtract_fusion.2 = f32[1024,128]{1,0:T(8,128)S(1)} fusion(f32[128,1024]{1,0:T(8,128)S(1)} %fusion.12, f32[1024,256]{1,0:T(8,128)} %bitcast.139, f32[256,256]{1,0:T(8,128)} %copy-done.11), kind=kOutput, calls=%fused_computation.17 | convolution fusion | flops 201457664 | bytes 1638400 | tf_op jit(solution)/shard_map/triangular_solve/dot.4 | solution.py:50
  79.4 0.6 fusion.43
  80.0 3.0 %fusion.3 = f32[256,256]{1,0:T(8,128)} fusion(f32[256,4096]{1,0:T(8,128)} %all-gather.6.cloned.1.call-done, f32[1024,128]{0,1:T(8,128)S(1)} %bitcast.124, f32[1024,128]{0,1:T(8,128)S(1)} %fusion.43), kind=kOutput, calls=%fused_computation.34 | convolution fusion | flops 805568512 | bytes 2359296 | tf_op jit(solution)/shard_map/dot_general | solution.py:46
  83.0 2.5 %copy.95 = f32[256,1024]{0,1:T(8,128)} copy(f32[256,1024]{1,0:T(8,128)} %get-tuple-element.118) | data formatting | bytes 2097152
  85.6 3.2 %convolution_subtract_fusion = f32[1024,256]{1,0:T(8,128)S(1)} fusion(f32[256,256]{1,0:T(8,128)} %param.24, f32[256,1024]{0,1:T(8,128)} %copy.95, f32[1024,128]{0,1:T(8,128)S(1)} %bitcast.125, f32[1024,128]{0,1:T(8,128)S(1)} %fusion.43), kind=kOutput, calls=%fused_computation.9 | convolution fusion | flops 805830656 | bytes 3407872 | tf_op jit(solution)/shard_map/dot_general | solution.py:46
  89.4 1.0 convolution_subtract_fusion.1
  90.4 0.6 fusion.50
  91.0 0.8 copy-done.3
  91.8 2.3 %fusion.5 = f32[256,256]{1,0:T(8,128)S(1)} fusion(f32[256,4096]{1,0:T(8,128)} %all-gather.6.cloned.1.call-done, f32[1024,128]{0,1:T(8,128)S(1)} %bitcast.130, f32[1024,128]{0,1:T(8,128)S(1)} %fusion.50), kind=kOutput, calls=%fused_computation.37 | convolution fusion | flops 805568512 | bytes 2359296 | tf_op jit(solution)/shard_map/dot_general | solution.py:46
  94.1 1.0 broadcast_in_dim.66
  95.2 5.0 %all-to-all-start.1 = ((f32[4,256,256]{2,1,0:T(8,128)}), f32[4,256,256]{2,1,0:T(8,128)}, u32[]{:S(2)}, u32[]{:S(2)}) async-start(f32[4,256,256]{2,1,0:T(8,128)} %broadcast_in_dim.66), calls=%async_computation.1 | async-start | bytes 2097152 | tf_op jit(solution)/shard_map/all_to_all | solution.py:25
  100.2 1.5 fusion.39
  101.7 0.6 fusion.40
  102.3 3.0 %fusion.7 = f32[256,256]{1,0:T(8,128)} fusion(f32[256,4096]{1,0:T(8,128)} %all-gather.6.cloned.1.call-done, f32[1024,128]{0,1:T(8,128)S(1)} %bitcast.127, f32[1024,128]{0,1:T(8,128)S(1)} %fusion.43), kind=kOutput, calls=%fused_computation.39 | convolution fusion | flops 805568512 | bytes 2359296 | tf_op jit(solution)/shard_map/dot_general | solution.py:46
  105.3 3.9 %fusion.9 = f32[256,512]{1,0:T(8,128)} fusion(f32[1024,512]{1,0:T(8,128)S(1)} %copy-done, f32[1024,128]{0,1:T(8,128)} %bitcast.132, f32[1024,128]{0,1:T(8,128)} %copy-done.3), kind=kOutput, calls=%fused_computation.41 | convolution fusion | flops 1610874880 | bytes 3670016 | tf_op jit(solution)/shard_map/dot_general | solution.py:46
  109.3 2.7 %fusion.14 = f32[256,512]{1,0:T(8,128)} fusion(f32[1024,512]{1,0:T(8,128)S(1)} %copy-done, f32[1024,128]{0,1:T(8,128)S(1)} %bitcast.128, f32[1024,128]{0,1:T(8,128)S(1)} %fusion.43), kind=kOutput, calls=%fused_computation.51 | convolution fusion | flops 1610874880 | bytes 3670016 | tf_op jit(solution)/shard_map/dot_general | solution.py:46
  112.0 3.2 %fusion.15 = f32[1024,512]{1,0:T(8,128)} fusion(f32[256,512]{1,0:T(8,128)S(1)} %copy-done.5, f32[1024,128]{0,1:T(8,128)S(1)} %bitcast.129, f32[1024,128]{0,1:T(8,128)S(1)} %fusion.43), kind=kOutput, calls=%fused_computation.52 | convolution fusion | flops 1610874880 | bytes 3670016 | tf_op jit(solution)/shard_map/dot_general | solution.py:46
  115.2 2.4 %pad_maximum_fusion.2 = f32[256,1024]{1,0:T(8,128)} fusion(f32[256,512]{1,0:T(8,128)} %fusion.9, f32[256,512]{1,0:T(8,128)} %fusion.14), kind=kLoop, calls=%fused_computation.36 | loop fusion | flops 262144 | bytes 2097152 | tf_op jit(solution)/shard_map/concatenate | solution.py:104
  117.6 5.5 %subtract_subtract_fusion = f32[1024,512]{1,0:T(8,128)} fusion(f32[1024,512]{1,0:T(8,128)} %param.35, f32[1024,512]{1,0:T(8,128)} %fusion.15, f32[256,512]{1,0:T(8,128)S(1)} %copy-done.7, f32[1024,128]{0,1:T(8,128)S(1)} %bitcast.133, f32[1024,128]{0,1:T(8,128)S(1)} %copy-done.4), kind=kOutput, calls=%fused_computation.8 | convolution fusion | flops 1611923456 | bytes 7864320 | tf_op jit(solution)/shard_map/dot_general | solution.py:46
  123.1 1.4 reduce_sum.37
  124.6 1.4 convolution_bitcast_fusion.1
  126.1 2.6 %gather_fusion = f32[256]{0:T(256)S(1)} fusion(f32[256,256]{0,1:T(8,128)S(1)} %convolution_bitcast_fusion.1, s32[256]{0:T(256)S(1)} %bitcast.120), kind=kCustom, calls=%fused_computation | custom fusion | bytes 4096 | tf_op jit(solution)/shard_map/jit(_diag)/jit(diagonal)/cond/branch_0_fun/gather | solution.py:54
  130.8 0.8 copy.78
  131.7 6.9 %all-gather.10.cloned.1.call-done = f32[1024,256]{1,0:T(8,128)} async-done(((f32[256,256]{1,0:T(8,128)}), f32[1024,256]{1,0:T(8,128)}) %all-gather.10.cloned.1.call-update) | async-done | bytes 1048592 | tf_op jit(solution)/shard_map/all_gather | solution.py:19
  138.6 2.0 %reduce_sum.38 = f32[256,256]{1,0:T(8,128)} reduce(f32[4,256,256]{2,1,0:T(8,128)} %bitcast.146, f32[]{:T(128)} %constant.53.clone.1), dimensions={0}, to_apply=%region_2.6 | reduce | flops 196608 | bytes 1310724 | tf_op jit(solution)/shard_map/reduce_sum | solution.py:20
  140.6 1.0 bitcast_add_fusion.1
  141.6 1.6 convolution_subtract_fusion.3
  144.2 4.4 %all-to-all-start = ((f32[4,64,1024]{2,1,0:T(8,128)}), f32[4,64,1024]{2,1,0:T(8,128)}, u32[]{:S(2)}, u32[]{:S(2)}) async-start(f32[4,64,1024]{2,1,0:T(8,128)} %bitcast.140), calls=%async_computation | async-start | bytes 2097152 | tf_op jit(solution)/shard_map/all_to_all | solution.py:41
  148.6 1.3 reduce_sum.39
  150.0 0.8 copy.80
  150.8 1.6 fusion.1
  152.4 1.3 convolution_bitcast_fusion
  153.8 2.4 %gather_fusion.1 = f32[256]{0:T(256)S(1)} fusion(f32[256,256]{0,1:T(8,128)S(1)} %convolution_bitcast_fusion, s32[256]{0:T(256)S(1)} %bitcast.121), kind=kCustom, calls=%fused_computation.1 | custom fusion | bytes 4096 | tf_op jit(solution)/shard_map/jit(_diag)/jit(diagonal)/cond/branch_0_fun/gather | solution.py:54
  157.2 2.4 %gather_fusion.2 = f32[256]{0:T(256)S(1)} fusion(f32[256,256]{0,1:T(8,128)S(1)} %bitcast_add_fusion.1, s32[256]{0:T(256)S(1)} %bitcast.122), kind=kCustom, calls=%fused_computation.2 | custom fusion | bytes 4096 | tf_op jit(solution)/shard_map/jit(_diag)/jit(diagonal)/cond/branch_0_fun/gather | solution.py:54
  159.6 0.8 copy.88
  161.7 2.4 %gather_fusion.3 = f32[256]{0:T(256)S(1)} fusion(f32[256,256]{0,1:T(8,128)S(1)} %bitcast_add_fusion, s32[256]{0:T(256)S(1)} %bitcast.123), kind=kCustom, calls=%fused_computation.3 | custom fusion | bytes 4096 | tf_op jit(solution)/shard_map/jit(_diag)/jit(diagonal)/cond/branch_0_fun/gather | solution.py:54
  164.1 0.7 multiply_subtract_fusion
  164.8 1.8 copy.87
  166.6 0.7 multiply_subtract_fusion.1
  167.3 1.8 copy.86
  169.1 2.0 %reduce_sum.36 = f32[64,1024]{1,0:T(8,128)} reduce(f32[4,64,1024]{2,1,0:T(8,128)} %all-to-all-done, f32[]{:T(128)} %constant.53.clone.1), dimensions={0}, to_apply=%region_0.2 | reduce | flops 196608 | bytes 1310724 | tf_op jit(solution)/shard_map/reduce_sum | solution.py:42
  171.2 1.4 fusion.2
  172.6 2.2 %convolution_subtract_fusion.4 = f32[64,512]{1,0:T(8,128)} fusion(f32[64,512]{1,0:T(8,128)S(1)} %fusion.2, f32[256,512]{1,0:T(8,128)} %param.26, f32[256,256]{0,1:T(8,128)S(1)} %bitcast_add_fusion, s32[]{:T(128)S(6)} %select_n.58), kind=kOutput, calls=%fused_computation.24 | convolution fusion | flops 100696064 | bytes 917508 | tf_op jit(solution)/shard_map/dot_general | solution.py:46
  175.2 1.1 convolution_subtract_fusion.6
  (97 shorter events, 6.7 us)
Async XLA Ops:
  7.2 98.2 %copy-start = (f32[1024,512]{1,0:T(8,128)S(1)}, f32[1024,512]{1,0:T(8,128)}, u32[]{:S(2)}) copy-start(f32[1024,512]{1,0:T(8,128)} %param.27) | copy-start | bytes 6291460
  7.2 27.4 %copy-start.22 = (f32[256,256]{1,0:T(8,128)S(1)}, f32[256,256]{1,0:T(8,128)}, u32[]{:S(2)}) copy-start(f32[256,256]{1,0:T(8,128)} %param.30) | copy-start | bytes 786436
  7.2 28.2 %copy-start.19 = (f32[256,256]{1,0:T(8,128)S(1)}, f32[256,256]{1,0:T(8,128)}, u32[]{:S(2)}) copy-start(f32[256,256]{1,0:T(8,128)} %param.23) | copy-start | bytes 786436
  7.2 64.3 %all-gather.6.cloned.1.call-start = ((), (), s32[]{:S(2)}) async-start(), calls=%async_computation.2 | async-start | bytes 4456448 | tf_op jit(solution)/shard_map/all_gather | solution.py:10
  7.3 52.1 %copy-start.23 = (f32[256,256]{1,0:T(8,128)S(1)}, f32[256,256]{1,0:T(8,128)}, u32[]{:S(2)}) copy-start(f32[256,256]{1,0:T(8,128)} %param.31) | copy-start | bytes 786436
  9.1 114.0 %all-gather.8.cloned.1.call-start = ((), (), s32[]{:S(2)}) async-start(), calls=%async_computation.3 | async-start | bytes 1310720 | tf_op jit(solution)/shard_map/all_gather | solution.py:19
  14.2 46.0 %copy-start.11 = (f32[256,256]{1,0:T(8,128)}, f32[256,256]{1,0:T(8,128)S(1)}, u32[]{:S(2)}) copy-start(f32[256,256]{1,0:T(8,128)S(1)} %get-tuple-element.217) | copy-start | bytes 786436
  39.4 104.1 %copy-start.9 = (f32[256,256]{1,0:T(8,128)}, f32[256,256]{1,0:T(8,128)S(1)}, u32[]{:S(2)}) copy-start(f32[256,256]{1,0:T(8,128)S(1)} %get-tuple-element.216) | copy-start | bytes 786436
  59.3 31.1 %copy-start.14 = (f32[2,128,128]{1,2,0:T(8,128)}, f32[2,128,128]{1,2,0:T(8,128)S(1)}, u32[]{:S(2)}) copy-start(f32[2,128,128]{1,2,0:T(8,128)S(1)} %custom-call.22) | copy-start | bytes 393220
  75.6 3.8 %copy-start.17 = (f32[2,128,128]{1,2,0:T(8,128)S(1)}, f32[2,128,128]{1,2,0:T(8,128)}, u32[]{:S(2)}) copy-start(f32[2,128,128]{1,2,0:T(8,128)} %custom-call.21) | copy-start | bytes 393220
  89.4 4.8 %copy-start.1 = (f32[128,1024]{1,0:T(8,128)}, f32[128,1024]{1,0:T(8,128)S(1)}, u32[]{:S(2)}) copy-start(f32[128,1024]{1,0:T(8,128)S(1)} %fusion.10) | copy-start | bytes 1572868
  91.0 0.8 copy-start.3
  95.2 49.0 %all-to-all-start.1 = ((f32[4,256,256]{2,1,0:T(8,128)}), f32[4,256,256]{2,1,0:T(8,128)}, u32[]{:S(2)}, u32[]{:S(2)}) async-start(f32[4,256,256]{2,1,0:T(8,128)} %broadcast_in_dim.66), calls=%async_computation.1 | async-start | bytes 2097152 | tf_op jit(solution)/shard_map/all_to_all | solution.py:25
  100.2 38.3 %all-gather.10.cloned.1.call-start = ((), (), s32[]{:S(2)}) async-start(), calls=%async_computation.4 | async-start | bytes 1310720 | tf_op jit(solution)/shard_map/all_gather | solution.py:19
  109.3 2.7 %copy-start.5 = (f32[256,512]{1,0:T(8,128)S(1)}, f32[256,512]{1,0:T(8,128)}, u32[]{:S(2)}) copy-start(f32[256,512]{1,0:T(8,128)} %param.25) | copy-start | bytes 1572868
  115.2 2.4 %copy-start.2 = (f32[128,1024]{1,0:T(8,128)S(1)}, f32[128,1024]{1,0:T(8,128)}, u32[]{:S(2)}) copy-start(f32[128,1024]{1,0:T(8,128)} %copy-done.1) | copy-start | bytes 1572868
  115.2 2.4 %copy-start.4 = (f32[1024,128]{0,1:T(8,128)S(1)}, f32[1024,128]{0,1:T(8,128)}, u32[]{:S(2)}) copy-start(f32[1024,128]{0,1:T(8,128)} %copy-done.3) | copy-start | bytes 1572868
  115.2 2.4 %copy-start.7 = (f32[256,512]{1,0:T(8,128)S(1)}, f32[256,512]{1,0:T(8,128)}, u32[]{:S(2)}) copy-start(f32[256,512]{1,0:T(8,128)} %param.26) | copy-start | bytes 1572868
  123.1 5.6 %copy-start.18 = (f32[2,128,128]{1,2,0:T(8,128)S(1)}, f32[2,128,128]{1,2,0:T(8,128)}, u32[]{:S(2)}) copy-start(f32[2,128,128]{1,2,0:T(8,128)} %custom-call.21) | copy-start | bytes 393220
  124.5 4.6 %copy-start.12 = (f32[256,256]{1,0:T(8,128)S(1)}, f32[256,256]{1,0:T(8,128)}, u32[]{:S(2)}) copy-start(f32[256,256]{1,0:T(8,128)} %copy-done.11) | copy-start | bytes 786436
  130.0 11.5 %copy-start.13 = (f32[256,256]{1,0:T(8,128)S(1)}, f32[256,256]{1,0:T(8,128)}, u32[]{:S(2)}) copy-start(f32[256,256]{1,0:T(8,128)} %param.24) | copy-start | bytes 786436
  130.8 12.4 %copy-start.15 = (f32[2,128,128]{1,2,0:T(8,128)S(1)}, f32[2,128,128]{1,2,0:T(8,128)}, u32[]{:S(2)}) copy-start(f32[2,128,128]{1,2,0:T(8,128)} %copy-done.14) | copy-start | bytes 393220
  144.2 6.6 %copy-start.20 = (f32[256,256]{0,1:T(8,128)S(1)}, f32[256,256]{0,1:T(8,128)}, u32[]{:S(2)}) copy-start(f32[256,256]{0,1:T(8,128)} %copy.81) | copy-start | bytes 786436
  144.2 24.9 %all-to-all-start = ((f32[4,64,1024]{2,1,0:T(8,128)}), f32[4,64,1024]{2,1,0:T(8,128)}, u32[]{:S(2)}, u32[]{:S(2)}) async-start(f32[4,64,1024]{2,1,0:T(8,128)} %bitcast.140), calls=%async_computation | async-start | bytes 2097152 | tf_op jit(solution)/shard_map/all_to_all | solution.py:41
  150.0 6.2 %copy-start.16 = (f32[2,128,128]{1,2,0:T(8,128)S(1)}, f32[2,128,128]{1,2,0:T(8,128)}, u32[]{:S(2)}) copy-start(f32[2,128,128]{1,2,0:T(8,128)} %copy-done.14) | copy-start | bytes 393220
  150.8 5.7 %copy-start.10 = (f32[256,256]{1,0:T(8,128)S(1)}, f32[256,256]{1,0:T(8,128)}, u32[]{:S(2)}) copy-start(f32[256,256]{1,0:T(8,128)} %copy-done.9) | copy-start | bytes 786436
  161.7 9.5 %copy-start.6 = (f32[256,512]{1,0:T(8,128)S(1)}, f32[256,512]{1,0:T(8,128)}, u32[]{:S(2)}) copy-start(f32[256,512]{1,0:T(8,128)} %param.25) | copy-start | bytes 1572868
  161.7 9.5 %copy-start.24 = (f32[64,512]{1,0:T(8,128)S(1)}, f32[64,512]{1,0:T(8,128)}, u32[]{:S(2)}) copy-start(f32[64,512]{1,0:T(8,128)} %param.34) | copy-start | bytes 393220
  171.1 3.6 %copy-start.21 = (f32[64,1024]{1,0:T(8,128)S(1)}, f32[64,1024]{1,0:T(8,128)}, u32[]{:S(2)}) copy-start(f32[64,1024]{1,0:T(8,128)} %reduce_sum.36) | copy-start | bytes 786436
  171.1 3.6 %copy-start.25 = (f32[64,512]{1,0:T(8,128)S(1)}, f32[64,512]{1,0:T(8,128)}, u32[]{:S(2)}) copy-start(f32[64,512]{1,0:T(8,128)} %param.33) | copy-start | bytes 393220
  171.1 4.1 %copy-start.8 = (f32[256,512]{1,0:T(8,128)S(1)}, f32[256,512]{1,0:T(8,128)}, u32[]{:S(2)}) copy-start(f32[256,512]{1,0:T(8,128)} %param.26) | copy-start | bytes 1572868
Sparse Core Ops, SparseCore 0:
  11.0 60.4 all-gather.5
  83.1 27.1 all-gather.7
  115.3 23.1 all-gather.9
where the time goes:
time: 184 us; the launch traced here: 183 us
  other arithmetic  56.8 us (31%)
  matrix products  49.2 us (27%)
  local copies, waits for them, and re-layouts  34.6 us (19%)
  waiting for transfers between devices  18.3 us (10%)
  between operations  14.4 us (8%)
  starting transfers between devices  9.55 us (5%)
    another operation x10, other arithmetic, right_solve(): lax.linalg.triangular_solve(factor, values, left_side=False, lower=True)  43.3 us
    dot_general x16, matrix products, matmul(): jnp.dot(left, right, precision=lax.Precision.HIGHEST, preferred_element_t...  37.9 us
    all_gather x1, waiting for transfers between devices, gather_turned(): out, at, outs = (lax.all_gather(both, axis, axis=0, tiled=True), 0, [])  11.3 us
    unnamed x59, local copies, waits for them, and re-layouts  11 us
    gather x4, local copies, waits for them, and re-layouts, halved(): return jnp.tril(square) - 0.5 * jnp.diag(jnp.diag(square))  9.74 us
    another operation x15, matrix products, right_solve(): lax.linalg.triangular_solve(factor, values, left_side=False, lower=True)  9.4 us
    another operation x19, local copies, waits for them, and re-layouts, right_solve(): lax.linalg.triangular_solve(factor, values, left_side=False, lower=True)  9.14 us
    all_gather x2, waiting for transfers between devices, gathered_total(): blocks = lax.all_gather(value, axis)  6.87 us
  transfers between devices with their start and end apart: 5, of which 2 were waited for; matrix products, arithmetic and copies ran while one was open for 65% of the time, Pallas kernels for 0%

commit v1 on v0

v1 whole, which is shorter than its diff:
```python
import jax
import jax.numpy as jnp
from jax import lax
from jax.experimental import pallas as pl
from jax.experimental.pallas import tpu as pltpu
from jax.sharding import Mesh, PartitionSpec as P

F32 = jnp.float32
BF16 = jnp.bfloat16
VMEM = pl.BlockSpec(memory_space=pltpu.VMEM)
SMEM = pl.BlockSpec(memory_space=pltpu.SMEM)
NN = (((1,), (0,)), ((), ()))
NT = (((1,), (1,)), ((), ()))
TN = (((0,), (0,)), ((), ()))


def full(a, b, dims=NN):
    return lax.dot_general(a, b, dims, precision=lax.Precision.HIGHEST, preferred_element_type=F32)


def one(a, b, dims=NN):
    return lax.dot_general(a, b, dims, preferred_element_type=F32)


def split(a):
    hi = a.astype(BF16)
    return hi, (a - hi.astype(F32)).astype(BF16)


def dot3(a, b, dims=NN):
    return one(a[0], b[0], dims) + (one(a[0], b[1], dims) + one(a[1], b[0], dims))


def shaped(*shape, dtype=F32):
    return jax.ShapeDtypeStruct(shape, dtype)


def params():
    return pltpu.CompilerParams(vmem_limit_bytes=56 * 2**20)


def positions(n):
    return (
        lax.broadcasted_iota(jnp.int32, (n, n), 0),
        lax.broadcasted_iota(jnp.int32, (n, n), 1),
    )


def halved(square):
    row, col = positions(square.shape[0])
    return jnp.where(row > col, square, jnp.where(row == col, 0.5 * square, 0.0))


def inverse_kernel(d2, d1, c, l2, l1, a2, a2t, a1, a1t, d2t, d1t, vt, w_hi, w_lo):
    n = d2.shape[0]
    row, col = positions(n)
    factors = (d2[...], d1[...])
    xs = [jnp.where(row == col, 1.0 / f, 0.0) for f in factors]
    step = 0
    while (1 << step) < n:
        inside = (
            ((row >> (step + 1)) == (col >> (step + 1)))
            & ((row >> step) != (col >> step))
            & (row > col)
        )
        parts = [full(jnp.where(inside, f, 0.0), x) for f, x in zip(factors, xs)]
        xs = [x - full(x, p) for x, p in zip(xs, parts)]
        step += 1
    x2, x1 = xs
    a2[...] = x2
    a1[...] = x1
    x2t, x1t = (x2.T, x1.T)
    a2t[...] = x2t
    a1t[...] = x1t
    d2t[...] = factors[0].T
    d1t[...] = factors[1].T
    vt[0, :, :n] = x2t
    vt[0, :, n:] = jnp.zeros((n, n), F32)
    vt[1, :, :n] = -full(x2, full(c[...], x1)).T
    vt[1, :, n:] = x1t
    w1 = full(x1, l1[...])
    w2 = full(x2, l2[...] - full(c[...], w1))
    hi, lo = split(w1)
    w_hi[n:] = hi
    w_lo[n:] = lo
    hi, lo = split(w2)
    w_hi[:n] = hi
    w_lo[:n] = lo


def inverses(d2, d1, c, l2, l1):
    n, width = l2.shape
    square = shaped(n, n)
    return pl.pallas_call(
        inverse_kernel,
        out_shape=(square,) * 6
        + (shaped(2, n, 2 * n), shaped(2 * n, width, dtype=BF16), shaped(2 * n, width, dtype=BF16)),
        in_specs=[VMEM] * 5,
        out_specs=[VMEM] * 9,
        compiler_params=params(),
        name="inverses",
    )(d2, d1, c, l2, l1)


def split_kernel(a, hi, lo):
    hi[...], lo[...] = split(a[...])


def split_rows(a):
    rows, cols = a.shape
    spec = pl.BlockSpec((rows // 4, cols), lambda i: (i, 0))
    return pl.pallas_call(
        split_kernel,
        grid=(4,),
        out_shape=(shaped(rows, cols, dtype=BF16),) * 2,
        in_specs=[spec],
        out_specs=[spec] * 2,
        compiler_params=params(),
        name="split_rows",
    )(a)


def gram_kernel(place, p2, p1, own, x1, x2, x3, y1, y2, y3, dy1, dy2, dy3, dx1, dx2, dx3, hi, lo, gram):
    x, y = (place[0], place[1])
    n = hi.shape[0] // 2
    w = p2.shape[0]

    def put(values, half, xx, yy):
        at = pl.multiple_of(half * n + ((yy & 3) * 4 + (xx & 3)) * w, w)
        h, l = split(values)
        hi[pl.ds(at, w)] = h
        lo[pl.ds(at, w)] = l

    for half in range(2):
        rows = pl.ds(half * w, w)
        put(own[rows], half, x, y)
        for k, ref in enumerate((x1, x2, x3)):
            put(ref[rows], half, x + 3 - k, y)
        for k, ref in enumerate((y1, y2, y3)):
            put(ref[rows], half, x, y + 3 - k)
    for k, ref in enumerate((dy1, dy2, dy3)):
        for j in range(3):
            put(ref[pl.ds(j * w, w)], 0, x + 3 - j, y + 3 - k)
    for k, ref in enumerate((dx1, dx2, dx3)):
        for j in range(3):
            put(ref[pl.ds(j * w, w)], 1, x + 3 - k, y + 3 - j)
    p2s, p1s = (split(p2[...]), split(p1[...]))
    both = tuple(jnp.concatenate(pair, axis=0) for pair in zip(p2s, p1s))
    gram[: 2 * w] = dot3(both, (hi[:n], lo[:n]), NT)
    gram[2 * w :] = dot3(p1s, (hi[n:], lo[n:]), NT)


def grams(place, p2, p1, pieces, n):
    rows = p2.shape[1]
    w = p2.shape[0]
    return pl.pallas_call(
        gram_kernel,
        out_shape=(
            shaped(2 * n, rows, dtype=BF16),
            shaped(2 * n, rows, dtype=BF16),
            shaped(3 * w, n),
        ),
        in_specs=[SMEM] + [VMEM] * (2 + len(pieces)),
        out_specs=[VMEM] * 3,
        compiler_params=params(),
        name="grams",
    )(place, p2, p1, *pieces)


def below_sum_kernel(place, hi, lo, bl_hi, bl_lo, a2t, a1t, c, keep, send):
    n = a2t.shape[0]
    share = n // 4
    below = (bl_hi[...], bl_lo[...])
    q2 = dot3((hi[:n], lo[:n]), below)
    u2 = dot3(split(a2t[...]), split(q2))
    q1 = dot3((hi[n:], lo[n:]), below)
    q1 = q1 - dot3(split(c[...].T), split(u2))
    u1 = dot3(split(a1t[...]), split(q1))
    for core in range(2):

        @pl.when(place[2] == core)
        def _():
            for r in range(4):
                ref = keep if r % 2 == core else send
                ref[r // 2, :share] = u2[r * share : (r + 1) * share]
                ref[r // 2, share:] = u1[r * share : (r + 1) * share]


def below_sums(place, hi, lo, bl_hi, bl_lo, a2t, a1t, c):
    n = a2t.shape[0]
    width = bl_hi.shape[1]
    return pl.pallas_call(
        below_sum_kernel,
        out_shape=(shaped(2, n // 2, width),) * 2,
        in_specs=[SMEM] + [VMEM] * 7,
        out_specs=[VMEM] * 2,
        compiler_params=params(),
        name="below_sums",
    )(place, hi, lo, bl_hi, bl_lo, a2t, a1t, c)


def pair_kernel(place, keep, got, mine, send):
    z = place[3]
    mine[...] = (keep[pl.ds(z, 1)] + got[pl.ds(z, 1)])[0]
    send[...] = (keep[pl.ds(1 - z, 1)] + got[pl.ds(1 - z, 1)])[0]


def pair_sums(place, keep, got):
    return pl.pallas_call(
        pair_kernel,
        out_shape=(shaped(*keep.shape[1:]),) * 2,
        in_specs=[SMEM] + [VMEM] * 2,
        out_specs=[VMEM] * 2,
        compiler_params=params(),
        name="pair_sums",
    )(place, keep, got)


def below_kernel(place, hi, lo, w_hi, w_lo, vt, grad, out, s2t, s1t):
    w = s2t.shape[0]
    g = (hi[...], lo[...])
    out[...] = grad[...] - dot3(g, (w_hi[...], w_lo[...]), TN)
    at = pl.multiple_of((place[1] * 4 + place[0]) * w, w)
    v = jnp.concatenate([vt[0, pl.ds(at, w)], vt[1, pl.ds(at, w)]], axis=0)
    solved = dot3(split(v), g)
    s2t[...] = solved[:w]
    s1t[...] = solved[w:]


def below_outputs(place, hi, lo, w_hi, w_lo, vt, grad, w):
    rows, width = grad.shape
    steps = 4
    tall = rows // steps
    whole = lambda a: pl.BlockSpec(a.shape, lambda i: (0,) * a.ndim)
    across = pl.BlockSpec((hi.shape[0], tall), lambda i: (0, i))
    thin = pl.BlockSpec((w, tall), lambda i: (0, i))
    block = pl.BlockSpec((tall, width), lambda i: (i, 0))
    return pl.pallas_call(
        below_kernel,
        grid=(steps,),
        out_shape=(shaped(rows, width), shaped(w, rows), shaped(w, rows)),
        in_specs=[SMEM, across, across, whole(w_hi), whole(w_lo), whole(vt), block],
        out_specs=[block, thin, thin],
        compiler_params=params(),
        name="below_outputs",
    )(place, hi, lo, w_hi, w_lo, vt, grad)


def chain_kernel(
    place, mine, other, a2, a2t, a1, a1t, d2t, d1t, c, gd2, gd1, gc, l2, l1, gl2, gl1, part, got,
    o_left2, o_left1, o_diag2, o_diag1, o_cross, rows2, rows1, rowsx, rowsxt,
):
    n = a2.shape[0]
    w = mine.shape[1] // 3
    first = place[2] == 0
    a, b = (mine[...], other[...])
    low = jnp.where(first, a, b)
    high = jnp.where(first, b, a)

    def gathered(k):
        return jnp.concatenate(
            [half[:, k * w : (k + 1) * w].reshape(n, n // 2) for half in (low, high)], axis=1
        )

    row, col = positions(n)
    lower = row >= col
    gram2 = full(gathered(0), a2[...]).T
    cross_t = full(gathered(1), a2[...])
    below_t = full(gathered(2) - full(cross_t, c[...]), a1[...])
    inner = halved(full(d2t[...], gd2[...] - jnp.where(lower, gram2, 0.0)))
    spread = full(full(a2t[...], inner), a2[...])
    sym2 = spread + spread.T
    rows2[...] = sym2
    o_diag2[...] = halved(sym2)
    cross = full(gc[...] - cross_t.T - full(sym2, c[...]), a1[...])
    o_cross[...] = cross
    rowsx[...] = cross
    cross_turned = cross.T
    rowsxt[...] = cross_turned
    gram1 = full(cross_turned, c[...]) + below_t.T
    inner = halved(full(d1t[...], gd1[...] - jnp.where(lower, gram1, 0.0)))
    spread = full(full(a1t[...], inner), a1[...])
    sym1 = spread + spread.T
    rows1[...] = sym1
    o_diag1[...] = halved(sym1)
    share = gl2.shape[0]
    at = pl.ds(pl.multiple_of((place[3] * 2 + place[2]) * share, share), share)
    l2s, l1s = (split(l2[...]), split(l1[...]))
    o_left2[...] = (
        gl2[...]
        - (part[:share] + got[:share])
        - dot3(split(rows2[at]), l2s)
        - dot3(split(rowsx[at]), l1s)
    )
    o_left1[...] = (
        gl1[...]
        - dot3(split(rowsxt[at]), l2s)
        - (part[share:] + got[share:])
        - dot3(split(rows1[at]), l1s)
    )


def chain(place, *operands):
    n = operands[2].shape[0]
    left = operands[14].shape
    return pl.pallas_call(
        chain_kernel,
        out_shape=(shaped(*left), shaped(*left), shaped(n, n), shaped(n, n), shaped(n, n)),
        in_specs=[SMEM] + [VMEM] * len(operands),
        out_specs=[VMEM] * 5,
        scratch_shapes=[pltpu.VMEM((n, n), F32)] * 4,
        compiler_params=params(),
        name="chain",
    )(place, *operands)


def shifted(value, axis, by):
    count = lax.axis_size(axis)
    return lax.ppermute(value, axis, [(i, (i + by) % count) for i in range(count)])


def shared(value, axes):
    count = lax.axis_size(axes)
    return lax.all_to_all(
        jnp.broadcast_to(value[None], (count, *value.shape)), axes, 0, 0, tiled=True
    )


def body(d2, d1, c, l2, l1, bl, p2, p1, gd2, gd1, gc, gl2, gl1, gb, g2, g1):
    n = d2.shape[0]
    w = p2.shape[1]
    core = lax.axis_index("core")
    place = jnp.stack(
        [lax.axis_index("x"), lax.axis_index("y"), core, lax.axis_index("zlo")]
    ).astype(jnp.int32)
    own = jnp.concatenate([g2.T, g1.T], axis=0)
    xs = [shifted(own, "x", k) for k in (1, 2, 3)]
    ys = [shifted(own, "y", k) for k in (1, 2, 3)]
    a2, a2t, a1, a1t, d2t, d1t, vt, w_hi, w_lo = inverses(d2, d1, c, l2, l1)
    bl_hi, bl_lo = split_rows(bl)
    from_x = jnp.concatenate([v[:w] for v in xs], axis=0)
    from_y = jnp.concatenate([v[w:] for v in ys], axis=0)
    dys = [shifted(from_x, "y", k) for k in (1, 2, 3)]
    dxs = [shifted(from_y, "x", k) for k in (1, 2, 3)]
    hi, lo, gram = grams(place, p2.T, p1.T, [own, *xs, *ys, *dys, *dxs], n)
    gram = shared(gram, ("zlo", "core")).sum(axis=0)
    gram = shared(lax.dynamic_slice_in_dim(gram, core * (n // 2), n // 2, 1), ("y", "x"))
    other = shifted(gram, "core", 1)
    keep, send = below_sums(place, hi, lo, bl_hi, bl_lo, a2t, a1t, c)
    part, send = pair_sums(place, keep, shifted(send, "core", 1))
    got = shifted(send, "zlo", 1)
    out_below, s2t, s1t = below_outputs(place, hi, lo, w_hi, w_lo, vt, gb, w)
    left2, left1, diag2, diag1, cross = chain(
        place, gram, other, a2, a2t, a1, a1t, d2t, d1t, c, gd2, gd1, gc, l2, l1, gl2, gl1, part, got
    )
    return out_below, left2, left1, diag2, diag1, cross, s2t.T, s1t.T


def solution(mesh):
    fine = Mesh(
        mesh.devices.reshape(2, 2, 4, 4, 4), ("zlo", "core", "y", "x", "dep")
    )
    row, col, deep = (("zlo", "core"), ("y", "x"), ("y", "x", "dep"))
    return jax.shard_map(
        body,
        mesh=fine,
        in_specs=(
            P(),
            P(),
            P(),
            P(None, deep),
            P(None, deep),
            P(row, deep),
            P(row, col),
            P(row, col),
            P(),
            P(),
            P(),
            P(row, deep),
            P(row, deep),
            P(row, deep),
            P(row, col),
            P(row, col),
        ),
        out_specs=(
            P(row, deep),
            P(row, deep),
            P(row, deep),
            P(),
            P(),
            P(),
            P(row, col),
            P(row, col),
        ),
        check_vma=False,
    )
```

time: 184 us -> 107 us (0.58)
  other arithmetic: 56.8 us -> 1.54 us
  matrix products: 49.2 us -> 0 us
  Pallas kernels: 0 us -> 47 us
  local copies, waits for them, and re-layouts: 34.6 us -> 3.84 us
  starting transfers between devices: 9.55 us -> 34.6 us
  between operations: 14.4 us -> 0.89 us
  blocking collectives: 0 us -> 13.4 us
  waiting for transfers between devices: 18.3 us -> 5.35 us
    pallas_call x0 -> x7, Pallas kernels: none -> 47 us  [the longest x1 15.7 us: inverses(): pl.pallas_call(inverse_kernel, out_shape=(square,) * 6 + (shaped(2, n, 2...]
    another operation x10 -> x1, other arithmetic: 43.3 us -> 0.61 us  [body(): jnp.stack([lax.axis_index('x'), lax.axis_index('y'), core, lax.axis_index...]
    dot_general x16 -> x0, matrix products: 37.9 us -> none  [matmul(): jnp.dot(left, right, precision=lax.Precision.HIGHEST, preferred_element_t...]
    ppermute x0 -> x15, starting transfers between devices: none -> 22.9 us  [shifted(): lax.ppermute(value, axis, [(i, (i + by) % count) for i in range(count)])]
    all_gather x3 -> x0, waiting for transfers between devices: 18.2 us -> none  [the longest x1 11.3 us: gather_turned(): out, at, outs = (lax.all_gather(both, axis, axis=0, tiled=True), 0, [])]
    all_to_all x0 -> x1, blocking collectives: none -> 13.4 us  [shared(): lax.all_to_all(jnp.broadcast_to(value[None], (count, *value.shape)), axes...]
    another operation x21 -> x0, matrix products: 11.3 us -> none  [the longest x15 9.4 us: right_solve(): lax.linalg.triangular_solve(factor, values, left_side=False, lower=True)]
    gather x4 -> x0, local copies, waits for them, and re-layouts: 9.74 us -> none  [halved(): return jnp.tril(square) - 0.5 * jnp.diag(jnp.diag(square))]
  transfers between devices with their start and end apart: 5 -> 16, of which waited for: 2 -> 6; matrix products, arithmetic and copies ran while one was open for 65% -> 1% of each run, Pallas kernels for 0% -> 32%
where the time goes in v1:
time: 107 us
  Pallas kernels  47 us (44%)
  starting transfers between devices  34.6 us (32%)
  blocking collectives  13.4 us (13%)
  waiting for transfers between devices  5.35 us (5%)
  local copies, waits for them, and re-layouts  3.84 us (4%)
  other arithmetic  1.54 us (1%)
    ppermute x15, starting transfers between devices, shifted(): lax.ppermute(value, axis, [(i, (i + by) % count) for i in range(count)])  22.9 us
    pallas_call x1, Pallas kernels, inverses(): pl.pallas_call(inverse_kernel, out_shape=(square,) * 6 + (shaped(2, n, 2...  15.7 us
    all_to_all x1, blocking collectives, shared(): lax.all_to_all(jnp.broadcast_to(value[None], (count, *value.shape)), axes...  13.4 us
    all_to_all x1, starting transfers between devices, shared(): lax.all_to_all(jnp.broadcast_to(value[None], (count, *value.shape)), axes...  11.7 us
    pallas_call x1, Pallas kernels, chain(): pl.pallas_call(chain_kernel, out_shape=(shaped(*left), shaped(*left), sha...  9.26 us
    pallas_call x1, Pallas kernels, below_sums(): pl.pallas_call(below_sum_kernel, out_shape=(shaped(2, n // 2, width),) *...  6.36 us
    pallas_call x1, Pallas kernels, below_outputs(): pl.pallas_call(below_kernel, grid=(steps,), out_shape=(shaped(rows, width...  6.31 us
    ppermute x15, waiting for transfers between devices, shifted(): lax.ppermute(value, axis, [(i, (i + by) % count) for i in range(count)])  5.35 us
  transfers between devices with their start and end apart: 16, of which 6 were waited for; matrix products, arithmetic and copies ran while one was open for 1% of the time, Pallas kernels for 32%

profile of v1, /device:TPU:1, one launch (start us, length us, event | category | flops | bytes accessed | tf_op | source)
XLA Modules:
  0.0 106.6 jit_solution(13950191397916757934)
XLA Ops:
  0.6 0.9 pad_maximum_fusion.2.own
  1.5 0.0 copy-start.1
  1.5 2.2 %collective-permute-start.3 = (f32[32,1024]{1,0:T(8,128)S(1)}, f32[32,1024]{1,0:T(8,128)S(1)}, u32[]{:S(2)}, u32[]{:S(2)}) collective-permute-start(f32[32,1024]{1,0:T(8,128)S(1)} %pad_maximum_fusion.2.own), channel_id=1, source_target_pairs={{0,16},{16,32},{32,48},{48,0},{1,17},{17,33},{33,49},{49,1},{2,18}... | collective-permute-start | bytes 393224 | tf_op jit(solution)/shard_map/ppermute | solution.py:319
  3.7 2.6 %collective-permute-start.4 = (f32[32,1024]{1,0:T(8,128)S(1)}, f32[32,1024]{1,0:T(8,128)S(1)}, u32[]{:S(2)}, u32[]{:S(2)}) collective-permute-start(f32[32,1024]{1,0:T(8,128)S(1)} %pad_maximum_fusion.2.own), channel_id=1, source_target_pairs={{0,32},{16,48},{32,0},{48,16},{1,33},{17,49},{33,1},{49,17},{2,34}... | collective-permute-start | bytes 393224 | tf_op jit(solution)/shard_map/ppermute | solution.py:319
  6.4 1.1 %collective-permute-start.5 = (f32[32,1024]{1,0:T(8,128)S(1)}, f32[32,1024]{1,0:T(8,128)S(1)}, u32[]{:S(2)}, u32[]{:S(2)}) collective-permute-start(f32[32,1024]{1,0:T(8,128)S(1)} %pad_maximum_fusion.2.own), channel_id=1, source_target_pairs={{0,48},{16,0},{32,16},{48,32},{1,49},{17,1},{33,17},{49,33},{2,50}... | collective-permute-start | bytes 393224 | tf_op jit(solution)/shard_map/ppermute | solution.py:319
  7.4 1.2 %collective-permute-start = (f32[32,1024]{1,0:T(8,128)S(1)}, f32[32,1024]{1,0:T(8,128)S(1)}, u32[]{:S(2)}, u32[]{:S(2)}) collective-permute-start(f32[32,1024]{1,0:T(8,128)S(1)} %pad_maximum_fusion.2.own), channel_id=1, source_target_pairs={{0,4},{4,8},{8,12},{12,0},{1,5},{5,9},{9,13},{13,1},{2,6},{6,10},{... | collective-permute-start | bytes 393224 | tf_op jit(solution)/shard_map/ppermute | solution.py:319
  8.6 2.5 %collective-permute-start.1 = (f32[32,1024]{1,0:T(8,128)S(1)}, f32[32,1024]{1,0:T(8,128)S(1)}, u32[]{:S(2)}, u32[]{:S(2)}) collective-permute-start(f32[32,1024]{1,0:T(8,128)S(1)} %pad_maximum_fusion.2.own), channel_id=1, source_target_pairs={{0,8},{4,12},{8,0},{12,4},{1,9},{5,13},{9,1},{13,5},{2,10},{6,14},... | collective-permute-start | bytes 393224 | tf_op jit(solution)/shard_map/ppermute | solution.py:319
  11.1 0.0 collective-permute-done.3.y1
  11.1 1.2 %collective-permute-start.2 = (f32[32,1024]{1,0:T(8,128)S(1)}, f32[32,1024]{1,0:T(8,128)S(1)}, u32[]{:S(2)}, u32[]{:S(2)}) collective-permute-start(f32[32,1024]{1,0:T(8,128)S(1)} %pad_maximum_fusion.2.own), channel_id=1, source_target_pairs={{0,12},{4,0},{8,4},{12,8},{1,13},{5,1},{9,5},{13,9},{2,14},{6,2},{... | collective-permute-start | bytes 393224 | tf_op jit(solution)/shard_map/ppermute | solution.py:319
  12.3 0.0 collective-permute-done.4.y2
  12.3 0.0 copy-start.5
  12.3 0.0 collective-permute-done.5.y3
  12.3 0.0 copy-start.6
  12.3 2.6 %collective-permute-start.10 = (f32[48,1024]{1,0:T(8,128)S(1)}, f32[48,1024]{1,0:T(8,128)S(1)}, u32[]{:S(2)}, u32[]{:S(2)}) collective-permute-start(f32[48,1024]{1,0:T(8,128)S(1)} %pad_maximum_fusion.1), channel_id=1, source_target_pairs={{0,8},{4,12},{8,0},{12,4},{1,9},{5,13},{9,1},{13,5},{2,10},{6,14},... | collective-permute-start | bytes 589832 | tf_op jit(solution)/shard_map/ppermute | solution.py:319
  15.0 0.9 collective-permute-start.11
  15.8 0.0 collective-permute-done.x1
  15.8 0.0 collective-permute-done.1.x2
  15.8 0.0 copy-start.8
  15.9 0.3 collective-permute-done.2.x3
  16.2 0.9 collective-permute-start.6
  17.0 2.3 %collective-permute-start.7 = (f32[48,1024]{1,0:T(8,128)S(1)}, f32[48,1024]{1,0:T(8,128)S(1)}, u32[]{:S(2)}, u32[]{:S(2)}) collective-permute-start(f32[48,1024]{1,0:T(8,128)S(1)} %pad_maximum_fusion), channel_id=1, source_target_pairs={{0,32},{16,48},{32,0},{48,16},{1,33},{17,49},{33,1},{49,17},{2,34}... | collective-permute-start | bytes 589832 | tf_op jit(solution)/shard_map/ppermute | solution.py:319
  19.3 0.7 collective-permute-start.8
  20.1 0.5 collective-permute-done.10.dx2
  20.6 1.4 %collective-permute-start.9 = (f32[48,1024]{1,0:T(8,128)S(1)}, f32[48,1024]{1,0:T(8,128)S(1)}, u32[]{:S(2)}, u32[]{:S(2)}) collective-permute-start(f32[48,1024]{1,0:T(8,128)S(1)} %pad_maximum_fusion.1), channel_id=1, source_target_pairs={{0,4},{4,8},{8,12},{12,0},{1,5},{5,9},{9,13},{13,1},{2,6},{6,10},{... | collective-permute-start | bytes 589832 | tf_op jit(solution)/shard_map/ppermute | solution.py:319
  21.9 0.6 pad_add_fusion.place
  22.6 2.2 %collective-permute-done.11.dx3 = f32[48,1024]{1,0:T(8,128)S(1)} collective-permute-done((f32[48,1024]{1,0:T(8,128)S(1)}, f32[48,1024]{1,0:T(8,128)S(1)}, u32[]{:S(2)}, u32[]{:S(2)}) %collective-permute-start.11) | collective-permute-done | bytes 196640 | tf_op jit(solution)/shard_map/ppermute | solution.py:319
  24.7 0.0 collective-permute-done.6.dy1
  24.7 0.0 collective-permute-done.7.dy2
  24.7 0.0 copy-start.14
  24.7 0.2 collective-permute-done.8.dy3
  25.0 1.7 %collective-permute-done.9.dx1 = f32[48,1024]{1,0:T(8,128)S(1)} collective-permute-done((f32[48,1024]{1,0:T(8,128)S(1)}, f32[48,1024]{1,0:T(8,128)S(1)}, u32[]{:S(2)}, u32[]{:S(2)}) %collective-permute-start.9) | collective-permute-done | bytes 196640 | tf_op jit(solution)/shard_map/ppermute | solution.py:319
  26.6 0.0 copy-done.1
  26.6 0.0 copy-done.4
  26.6 0.0 copy-done.5
  26.6 0.0 copy-done.6
  26.6 0.0 copy-done.7
  26.6 0.0 copy-done.8
  26.7 0.0 copy-done.9
  26.7 0.0 copy-done.11
  26.7 0.0 copy-done.12
  26.7 0.0 copy-done.13
  26.7 0.0 copy-done.14
  26.7 0.6 copy-done.16
  27.3 3.5 %grams.1 = (bf16[512,1024]{1,0:T(8,128)(2,1)}, bf16[512,1024]{1,0:T(8,128)(2,1)}, f32[48,256]{1,0:T(8,128)}) custom-call(s32[4]{0:T(128)} %pad_add_fusion.place, f32[16,1024]{1,0:T(8,128)} %bitcast.10, f32[16,1024]{1,0:T(8,128)} %bitcast.11, f32[32,1024]{1,0:T(8,128)} %copy-done.1, f32[32,1024]{1,0:T(8,128)} %copy-done.7, f32[32,1024]{1,0:T(8,128)} %copy-done.8, ...), custom_call_target="tpu_custom_call" | custom-call | tf_op jit(solution)/shard_map/grams/pallas_call | solution.py:156
  30.8 1.5 %broadcast_in_dim.4 = f32[4,48,256]{2,1,0:T(8,128)} broadcast(f32[48,256]{1,0:T(8,128)} %get-tuple-element.40), dimensions={1,2} | broadcast | bytes 245760 | tf_op jit(solution)/shard_map/broadcast_in_dim | solution.py:325
  32.3 11.7 %all-to-all-start = ((f32[4,48,256]{2,1,0:T(8,128)}), f32[4,48,256]{2,1,0:T(8,128)S(1)}, u32[]{:S(2)}, u32[]{:S(2)}) async-start(f32[4,48,256]{2,1,0:T(8,128)} %broadcast_in_dim.4), calls=%async_computation | async-start | bytes 393216 | tf_op jit(solution)/shard_map/all_to_all | solution.py:324
  44.0 3.8 %split_rows.1 = (bf16[1024,512]{1,0:T(8,128)(2,1)}, bf16[1024,512]{1,0:T(8,128)(2,1)}) custom-call(f32[1024,512]{1,0:T(8,128)} %a.1), custom_call_target="tpu_custom_call" | custom-call | tf_op jit(solution)/shard_map/split_rows/pallas_call | solution.py:112
  47.8 15.7 %inverses.1 = (f32[256,256]{1,0:T(8,128)}, f32[256,256]{1,0:T(8,128)}, f32[256,256]{1,0:T(8,128)}, f32[256,256]{1,0:T(8,128)}, f32[256,256]{1,0:T(8,128)}, /*ind...) custom-call(f32[256,256]{1,0:T(8,128)} %d2.1, f32[256,256]{1,0:T(8,128)} %d1.1, ...), custom_call_target="tpu_custom_call" | custom-call | tf_op jit(solution)/shard_map/inverses/pallas_call | solution.py:94
  63.5 6.4 %below_sums.1 = (f32[2,128,512]{2,1,0:T(8,128)}, f32[2,128,512]{2,1,0:T(8,128)}) custom-call(s32[4]{0:T(128)} %pad_add_fusion.place, bf16[512,1024]{1,0:T(8,128)(2,1)} %get-tuple-element.34.hi, bf16[512,1024]{1,0:T(8,128)(2,1)} %get-tuple-element.35.lo, bf16[1024,512]{1,0:T(8,128)(2,1)} %get-tuple-element.47.bl_hi, ...), custom_call_target="tpu_custom_call" | custom-call | tf_op jit(solution)/shard_map/below_sums/pallas_call | solution.py:192
  69.8 0.0 collective-permute-start.13
  69.9 0.0 all-to-all-done
  69.9 13.4 %all_to_all.10.mine = f32[16,48,128]{2,1,0:T(8,128)S(1)} all-to-all(f32[16,48,128]{2,1,0:T(8,128)S(1)} %broadcast_in_dim.5), channel_id=1, replica_groups=mesh['zlo'=2,'core'=2,'y'=4,'x'=4,'dep'=4] {'y','x'}, dimensions={0} | all-to-all | bytes 786432 | tf_op jit(solution)/shard_map/all_to_all | solution.py:324
  83.4 1.6 %collective-permute-start.12 = (f32[16,48,128]{2,1,0:T(8,128)S(1)}, f32[16,48,128]{2,1,0:T(8,128)S(1)}, u32[]{:S(2)}, u32[]{:S(2)}) collective-permute-start(f32[16,48,128]{2,1,0:T(8,128)S(1)} %all_to_all.10.mine), channel_id=1, source_target_pairs={{0,64},{64,0},{1,65},{65,1},{2,66},{66,2},{3,67},{67,3},{4,68},{68... | collective-permute-start | bytes 1179656 | tf_op jit(solution)/shard_map/ppermute | solution.py:319
  85.0 0.0 collective-permute-done.13.got
  85.0 0.8 copy-done.2
  85.8 2.1 %pair_sums.1 = (f32[128,512]{1,0:T(8,128)}, f32[128,512]{1,0:T(8,128)}) custom-call(s32[4]{0:T(128)} %pad_add_fusion.place, f32[2,128,512]{2,1,0:T(8,128)} %get-tuple-element.49.keep, f32[2,128,512]{2,1,0:T(8,128)} %copy-done.2), custom_call_target="tpu_custom_call" | custom-call | tf_op jit(solution)/shard_map/pair_sums/pallas_call | solution.py:209
  87.9 1.8 %collective-permute-start.14 = (f32[128,512]{1,0:T(8,128)}, f32[128,512]{1,0:T(8,128)S(1)}, u32[]{:S(2)}, u32[]{:S(2)}) collective-permute-start(f32[128,512]{1,0:T(8,128)} %get-tuple-element.52), channel_id=1, source_target_pairs={{0,128},{128,0},{1,129},{129,1},{2,130},{130,2},{3,131},{131,3},{4... | collective-permute-start | bytes 786440 | tf_op jit(solution)/shard_map/ppermute | solution.py:319
  89.6 6.3 %below_outputs.1 = (f32[1024,512]{1,0:T(8,128)}, f32[16,1024]{1,0:T(8,128)}, f32[16,1024]{1,0:T(8,128)}) custom-call(s32[4]{0:T(128)} %pad_add_fusion.place, bf16[512,1024]{1,0:T(8,128)(2,1)} %get-tuple-element.34.hi, bf16[512,1024]{1,0:T(8,128)(2,1)} %get-tuple-element.35.lo, bf16[512,512]{1,0:T(8,128)(2,1)} %get-tuple-element.36.w_hi, ...), custom_call_target="tpu_custom_call" | custom-call | tf_op jit(solution)/shard_map/below_outputs/pallas_call | solution.py:238
  95.9 0.0 copy-done
  95.9 0.5 collective-permute-done.14.got
  96.5 0.0 collective-permute-done.12.other
  96.5 0.7 copy-done.10
  97.2 0.1 copy-done.3
  97.3 9.3 %chain.1 = (f32[64,512]{1,0:T(8,128)}, f32[64,512]{1,0:T(8,128)}, f32[256,256]{1,0:T(8,128)}, f32[256,256]{1,0:T(8,128)}, f32[256,256]{1,0:T(8,128)}) custom-call(s32[4]{0:T(128)} %pad_add_fusion.place, f32[16,48,128]{2,1,0:T(8,128)} %copy-done, f32[16,48,128]{2,1,0:T(8,128)} %copy-done.3, f32[256,256]{1,0:T(8,128)} %get-tuple-element.41.a2, ...), custom_call_target="tpu_custom_call" | custom-call | tf_op jit(solution)/shard_map/chain/pallas_call | solution.py:306
  (24 shorter events, 0.1 us)
Async XLA Ops:
  1.5 25.1 %copy-start.1 = (f32[32,1024]{1,0:T(8,128)}, f32[32,1024]{1,0:T(8,128)S(1)}, u32[]{:S(2)}) copy-start(f32[32,1024]{1,0:T(8,128)S(1)} %pad_maximum_fusion.2.own) | copy-start | bytes 393220
  1.5 9.6 %collective-permute-start.3 = (f32[32,1024]{1,0:T(8,128)S(1)}, f32[32,1024]{1,0:T(8,128)S(1)}, u32[]{:S(2)}, u32[]{:S(2)}) collective-permute-start(f32[32,1024]{1,0:T(8,128)S(1)} %pad_maximum_fusion.2.own), channel_id=1, source_target_pairs={{0,16},{16,32},{32,48},{48,0},{1,17},{17,33},{33,49},{49,1},{2,18}... | collective-permute-start | bytes 393224 | tf_op jit(solution)/shard_map/ppermute | solution.py:319
  3.7 8.5 %collective-permute-start.4 = (f32[32,1024]{1,0:T(8,128)S(1)}, f32[32,1024]{1,0:T(8,128)S(1)}, u32[]{:S(2)}, u32[]{:S(2)}) collective-permute-start(f32[32,1024]{1,0:T(8,128)S(1)} %pad_maximum_fusion.2.own), channel_id=1, source_target_pairs={{0,32},{16,48},{32,0},{48,16},{1,33},{17,49},{33,1},{49,17},{2,34}... | collective-permute-start | bytes 393224 | tf_op jit(solution)/shard_map/ppermute | solution.py:319
  6.4 5.9 %collective-permute-start.5 = (f32[32,1024]{1,0:T(8,128)S(1)}, f32[32,1024]{1,0:T(8,128)S(1)}, u32[]{:S(2)}, u32[]{:S(2)}) collective-permute-start(f32[32,1024]{1,0:T(8,128)S(1)} %pad_maximum_fusion.2.own), channel_id=1, source_target_pairs={{0,48},{16,0},{32,16},{48,32},{1,49},{17,1},{33,17},{49,33},{2,50}... | collective-permute-start | bytes 393224 | tf_op jit(solution)/shard_map/ppermute | solution.py:319
  7.4 8.4 %collective-permute-start = (f32[32,1024]{1,0:T(8,128)S(1)}, f32[32,1024]{1,0:T(8,128)S(1)}, u32[]{:S(2)}, u32[]{:S(2)}) collective-permute-start(f32[32,1024]{1,0:T(8,128)S(1)} %pad_maximum_fusion.2.own), channel_id=1, source_target_pairs={{0,4},{4,8},{8,12},{12,0},{1,5},{5,9},{9,13},{13,1},{2,6},{6,10},{... | collective-permute-start | bytes 393224 | tf_op jit(solution)/shard_map/ppermute | solution.py:319
  8.6 7.2 %collective-permute-start.1 = (f32[32,1024]{1,0:T(8,128)S(1)}, f32[32,1024]{1,0:T(8,128)S(1)}, u32[]{:S(2)}, u32[]{:S(2)}) collective-permute-start(f32[32,1024]{1,0:T(8,128)S(1)} %pad_maximum_fusion.2.own), channel_id=1, source_target_pairs={{0,8},{4,12},{8,0},{12,4},{1,9},{5,13},{9,1},{13,5},{2,10},{6,14},... | collective-permute-start | bytes 393224 | tf_op jit(solution)/shard_map/ppermute | solution.py:319
  11.1 15.5 %copy-start.4 = (f32[32,1024]{1,0:T(8,128)}, f32[32,1024]{1,0:T(8,128)S(1)}, u32[]{:S(2)}) copy-start(f32[32,1024]{1,0:T(8,128)S(1)} %collective-permute-done.3.y1) | copy-start | bytes 393220
  11.1 5.0 %collective-permute-start.2 = (f32[32,1024]{1,0:T(8,128)S(1)}, f32[32,1024]{1,0:T(8,128)S(1)}, u32[]{:S(2)}, u32[]{:S(2)}) collective-permute-start(f32[32,1024]{1,0:T(8,128)S(1)} %pad_maximum_fusion.2.own), channel_id=1, source_target_pairs={{0,12},{4,0},{8,4},{12,8},{1,13},{5,1},{9,5},{13,9},{2,14},{6,2},{... | collective-permute-start | bytes 393224 | tf_op jit(solution)/shard_map/ppermute | solution.py:319
  12.3 14.4 %copy-start.5 = (f32[32,1024]{1,0:T(8,128)}, f32[32,1024]{1,0:T(8,128)S(1)}, u32[]{:S(2)}) copy-start(f32[32,1024]{1,0:T(8,128)S(1)} %collective-permute-done.4.y2) | copy-start | bytes 393220
  12.3 14.3 %copy-start.6 = (f32[32,1024]{1,0:T(8,128)}, f32[32,1024]{1,0:T(8,128)S(1)}, u32[]{:S(2)}) copy-start(f32[32,1024]{1,0:T(8,128)S(1)} %collective-permute-done.5.y3) | copy-start | bytes 393220
  12.3 8.2 %collective-permute-start.10 = (f32[48,1024]{1,0:T(8,128)S(1)}, f32[48,1024]{1,0:T(8,128)S(1)}, u32[]{:S(2)}, u32[]{:S(2)}) collective-permute-start(f32[48,1024]{1,0:T(8,128)S(1)} %pad_maximum_fusion.1), channel_id=1, source_target_pairs={{0,8},{4,12},{8,0},{12,4},{1,9},{5,13},{9,1},{13,5},{2,10},{6,14},... | collective-permute-start | bytes 589832 | tf_op jit(solution)/shard_map/ppermute | solution.py:319
  15.0 9.7 %collective-permute-start.11 = (f32[48,1024]{1,0:T(8,128)S(1)}, f32[48,1024]{1,0:T(8,128)S(1)}, u32[]{:S(2)}, u32[]{:S(2)}) collective-permute-start(f32[48,1024]{1,0:T(8,128)S(1)} %pad_maximum_fusion.1), channel_id=1, source_target_pairs={{0,12},{4,0},{8,4},{12,8},{1,13},{5,1},{9,5},{13,9},{2,14},{6,2},{... | collective-permute-start | bytes 589832 | tf_op jit(solution)/shard_map/ppermute | solution.py:319
  15.8 10.8 %copy-start.7 = (f32[32,1024]{1,0:T(8,128)}, f32[32,1024]{1,0:T(8,128)S(1)}, u32[]{:S(2)}) copy-start(f32[32,1024]{1,0:T(8,128)S(1)} %collective-permute-done.x1) | copy-start | bytes 393220
  15.8 10.8 %copy-start.8 = (f32[32,1024]{1,0:T(8,128)}, f32[32,1024]{1,0:T(8,128)S(1)}, u32[]{:S(2)}) copy-start(f32[32,1024]{1,0:T(8,128)S(1)} %collective-permute-done.1.x2) | copy-start | bytes 393220
  16.1 10.5 %copy-start.9 = (f32[32,1024]{1,0:T(8,128)}, f32[32,1024]{1,0:T(8,128)S(1)}, u32[]{:S(2)}) copy-start(f32[32,1024]{1,0:T(8,128)S(1)} %collective-permute-done.2.x3) | copy-start | bytes 393220
  16.2 8.6 %collective-permute-start.6 = (f32[48,1024]{1,0:T(8,128)S(1)}, f32[48,1024]{1,0:T(8,128)S(1)}, u32[]{:S(2)}, u32[]{:S(2)}) collective-permute-start(f32[48,1024]{1,0:T(8,128)S(1)} %pad_maximum_fusion), channel_id=1, source_target_pairs={{0,16},{16,32},{32,48},{48,0},{1,17},{17,33},{33,49},{49,1},{2,18}... | collective-permute-start | bytes 589832 | tf_op jit(solution)/shard_map/ppermute | solution.py:319
  17.0 7.7 %collective-permute-start.7 = (f32[48,1024]{1,0:T(8,128)S(1)}, f32[48,1024]{1,0:T(8,128)S(1)}, u32[]{:S(2)}, u32[]{:S(2)}) collective-permute-start(f32[48,1024]{1,0:T(8,128)S(1)} %pad_maximum_fusion), channel_id=1, source_target_pairs={{0,32},{16,48},{32,0},{48,16},{1,33},{17,49},{33,1},{49,17},{2,34}... | collective-permute-start | bytes 589832 | tf_op jit(solution)/shard_map/ppermute | solution.py:319
  19.3 5.6 %collective-permute-start.8 = (f32[48,1024]{1,0:T(8,128)S(1)}, f32[48,1024]{1,0:T(8,128)S(1)}, u32[]{:S(2)}, u32[]{:S(2)}) collective-permute-start(f32[48,1024]{1,0:T(8,128)S(1)} %pad_maximum_fusion), channel_id=1, source_target_pairs={{0,48},{16,0},{32,16},{48,32},{1,49},{17,1},{33,17},{49,33},{2,50}... | collective-permute-start | bytes 589832 | tf_op jit(solution)/shard_map/ppermute | solution.py:319
  20.6 6.1 %copy-start.11 = (f32[48,1024]{1,0:T(8,128)}, f32[48,1024]{1,0:T(8,128)S(1)}, u32[]{:S(2)}) copy-start(f32[48,1024]{1,0:T(8,128)S(1)} %collective-permute-done.10.dx2) | copy-start | bytes 589828
  20.6 6.0 %collective-permute-start.9 = (f32[48,1024]{1,0:T(8,128)S(1)}, f32[48,1024]{1,0:T(8,128)S(1)}, u32[]{:S(2)}, u32[]{:S(2)}) collective-permute-start(f32[48,1024]{1,0:T(8,128)S(1)} %pad_maximum_fusion.1), channel_id=1, source_target_pairs={{0,4},{4,8},{8,12},{12,0},{1,5},{5,9},{9,13},{13,1},{2,6},{6,10},{... | collective-permute-start | bytes 589832 | tf_op jit(solution)/shard_map/ppermute | solution.py:319
  24.7 2.0 %copy-start.12 = (f32[48,1024]{1,0:T(8,128)}, f32[48,1024]{1,0:T(8,128)S(1)}, u32[]{:S(2)}) copy-start(f32[48,1024]{1,0:T(8,128)S(1)} %collective-permute-done.11.dx3) | copy-start | bytes 589828
  24.7 2.0 %copy-start.13 = (f32[48,1024]{1,0:T(8,128)}, f32[48,1024]{1,0:T(8,128)S(1)}, u32[]{:S(2)}) copy-start(f32[48,1024]{1,0:T(8,128)S(1)} %collective-permute-done.6.dy1) | copy-start | bytes 589828
  24.7 2.0 %copy-start.14 = (f32[48,1024]{1,0:T(8,128)}, f32[48,1024]{1,0:T(8,128)S(1)}, u32[]{:S(2)}) copy-start(f32[48,1024]{1,0:T(8,128)S(1)} %collective-permute-done.7.dy2) | copy-start | bytes 589828
  24.9 1.8 %copy-start.15 = (f32[48,1024]{1,0:T(8,128)}, f32[48,1024]{1,0:T(8,128)S(1)}, u32[]{:S(2)}) copy-start(f32[48,1024]{1,0:T(8,128)S(1)} %collective-permute-done.8.dy3) | copy-start | bytes 589828
  26.6 0.7 copy-start.16
  32.3 37.6 %all-to-all-start = ((f32[4,48,256]{2,1,0:T(8,128)}), f32[4,48,256]{2,1,0:T(8,128)S(1)}, u32[]{:S(2)}, u32[]{:S(2)}) async-start(f32[4,48,256]{2,1,0:T(8,128)} %broadcast_in_dim.4), calls=%async_computation | async-start | bytes 393216 | tf_op jit(solution)/shard_map/all_to_all | solution.py:324
  69.8 15.2 %collective-permute-start.13 = (f32[2,128,512]{2,1,0:T(8,128)}, f32[2,128,512]{2,1,0:T(8,128)S(1)}, u32[]{:S(2)}, u32[]{:S(2)}) collective-permute-start(f32[2,128,512]{2,1,0:T(8,128)} %get-tuple-element.50), channel_id=1, source_target_pairs={{0,64},{64,0},{1,65},{65,1},{2,66},{66,2},{3,67},{67,3},{4,68},{68... | collective-permute-start | bytes 1572872 | tf_op jit(solution)/shard_map/ppermute | solution.py:319
  83.4 12.6 %copy-start = (f32[16,48,128]{2,1,0:T(8,128)}, f32[16,48,128]{2,1,0:T(8,128)S(1)}, u32[]{:S(2)}) copy-start(f32[16,48,128]{2,1,0:T(8,128)S(1)} %all_to_all.10.mine) | copy-start | bytes 1179652
  83.4 13.1 %collective-permute-start.12 = (f32[16,48,128]{2,1,0:T(8,128)S(1)}, f32[16,48,128]{2,1,0:T(8,128)S(1)}, u32[]{:S(2)}, u32[]{:S(2)}) collective-permute-start(f32[16,48,128]{2,1,0:T(8,128)S(1)} %all_to_all.10.mine), channel_id=1, source_target_pairs={{0,64},{64,0},{1,65},{65,1},{2,66},{66,2},{3,67},{67,3},{4,68},{68... | collective-permute-start | bytes 1179656 | tf_op jit(solution)/shard_map/ppermute | solution.py:319
  85.0 0.8 copy-start.2
  87.9 8.6 %collective-permute-start.14 = (f32[128,512]{1,0:T(8,128)}, f32[128,512]{1,0:T(8,128)S(1)}, u32[]{:S(2)}, u32[]{:S(2)}) collective-permute-start(f32[128,512]{1,0:T(8,128)} %get-tuple-element.52), channel_id=1, source_target_pairs={{0,128},{128,0},{1,129},{129,1},{2,130},{130,2},{3,131},{131,3},{4... | collective-permute-start | bytes 786440 | tf_op jit(solution)/shard_map/ppermute | solution.py:319
  96.5 0.7 copy-start.10
  96.5 0.8 copy-start.3

commit v2 on v1

v2 whole, which is shorter than its diff:
```python
import jax
import jax.numpy as jnp
from jax import lax
from jax.experimental import pallas as pl
from jax.experimental.pallas import tpu as pltpu
from jax.sharding import Mesh, PartitionSpec as P

F32 = jnp.float32
BF16 = jnp.bfloat16
VMEM = pl.BlockSpec(memory_space=pltpu.VMEM)
SMEM = pl.BlockSpec(memory_space=pltpu.SMEM)
NN = (((1,), (0,)), ((), ()))
NT = (((1,), (1,)), ((), ()))
TN = (((0,), (0,)), ((), ()))


def full(a, b, dims=NN):
    return lax.dot_general(a, b, dims, precision=lax.Precision.HIGHEST, preferred_element_type=F32)


def one(a, b, dims=NN):
    return lax.dot_general(a, b, dims, preferred_element_type=F32)


def split(a):
    hi = a.astype(BF16)
    return hi, (a - hi.astype(F32)).astype(BF16)


def dot3(a, b, dims=NN):
    return one(a[0], b[0], dims) + (one(a[0], b[1], dims) + one(a[1], b[0], dims))


def shaped(*shape, dtype=F32):
    return jax.ShapeDtypeStruct(shape, dtype)


def near(*shape, dtype=F32):
    return pltpu.VMEM(shape, dtype)


def call(kernel, name, outs, operands, scratch=(), micros=2.0, loads=0, space=pltpu.VMEM, out_specs=None):
    kept = len(operands) - loads
    held = [pltpu.with_memory_space_constraint(v, pltpu.VMEM) for v in operands[1:kept]]
    far = [pltpu.with_memory_space_constraint(v, pltpu.HBM) for v in operands[kept:]]
    return pl.pallas_call(
        kernel,
        out_shape=tuple(outs),
        in_specs=[SMEM] + [VMEM] * len(held) + [pl.BlockSpec(memory_space=space)] * loads,
        out_specs=out_specs or [VMEM] * len(outs),
        scratch_shapes=list(scratch),
        compiler_params=pltpu.CompilerParams(vmem_limit_bytes=20 * 2**20),
        cost_estimate=pl.CostEstimate(
            flops=int(micros * 1e9), transcendentals=0, bytes_accessed=int(micros * 3e6)
        ),
        name=name,
    )(operands[0], *held, *far)


def positions(n):
    return (
        lax.broadcasted_iota(jnp.int32, (n, n), 0),
        lax.broadcasted_iota(jnp.int32, (n, n), 1),
    )


def halved(square):
    row, col = positions(square.shape[0])
    return jnp.where(row > col, square, jnp.where(row == col, 0.5 * square, 0.0))


def three(a):
    hi = a.astype(BF16)
    rest = a - hi.astype(F32)
    mid = rest.astype(BF16)
    return hi, mid, (rest - mid.astype(F32)).astype(BF16)


def dot3f(a, b, dims=NN):
    return dot3(split(a), split(b), dims)


def block_inverses(factor, size):
    n = factor.shape[0]
    row, col = positions(n)
    same = (row // size) == (col // size)
    lower = jnp.where(same & (row >= col), factor, 0.0)
    packed = lower[:size]
    for k in range(1, n // size):
        packed = packed + lower[k * size : (k + 1) * size]
    line = lax.broadcasted_iota(jnp.int32, (size, n), 0)
    lane = lax.broadcasted_iota(jnp.int32, (size, n), 1) % size
    columns = jnp.concatenate([jnp.where(lane == j, packed, 0.0) for j in range(size)], axis=0)
    ones = jnp.where(same, 1.0, 0.0).astype(BF16)
    hi, mid, lo = three(columns)
    spread = one(hi, ones) + (one(mid, ones) + one(lo, ones))
    x = jnp.where(line == lane, 1.0, 0.0)
    for j in range(size):
        column = spread[j * size : (j + 1) * size]
        solved = x[j : j + 1] / column[j : j + 1]
        x = jnp.where(line == j, solved, x - jnp.where(line > j, column, 0.0) * solved)
    return jnp.where(same, jnp.concatenate([x] * (n // size), axis=0), 0.0)


def inverses_of(factors):
    n = factors[0].shape[0]
    half = n // 2
    size = 16
    xs = [block_inverses(f, size) for f in factors]
    blocks = [(f, x, at) for f, x in zip(factors, xs) for at in (0, half)]
    corners = [x[at : at + half, at : at + half] for f, x, at in blocks]
    belows = [f[at : at + half, at : at + half] for f, x, at in blocks]
    row, col = positions(half)
    while size < half:
        inside = (row // (2 * size) == col // (2 * size)) & (row // size > col // size)
        parts = [full(jnp.where(inside, f, 0.0), x) for f, x in zip(belows, corners)]
        corners = [x - full(x, p) for x, p in zip(corners, parts)]
        size *= 2
    outs = []
    parts = [full(f[half:, :half], corners[2 * k]) for k, f in enumerate(factors)]
    parts = [full(corners[2 * k + 1], p) for k, p in enumerate(parts)]
    for k, p in enumerate(parts):
        top = jnp.concatenate([corners[2 * k], jnp.zeros((half, half), F32)], axis=1)
        low = jnp.concatenate([-p, corners[2 * k + 1]], axis=1)
        outs.append(jnp.concatenate([top, low], axis=0))
    return outs


def inverse_kernel(place, *refs):
    count = (len(refs) - 5) // 2
    sources, (a2, a2t, a1, a1t), targets, sems = (
        refs[:count],
        refs[count : count + 4],
        refs[count + 4 : -1],
        refs[-1],
    )
    copies = [
        pltpu.make_async_copy(source, target, sems.at[k])
        for k, (source, target) in enumerate(zip(sources, targets))
    ]
    for copy in copies:
        copy.start()
    copies[0].wait()
    copies[1].wait()
    x2, x1 = inverses_of([targets[0][...], targets[1][...]])
    a2[...] = x2
    a1[...] = x1
    a2t[...] = x2.T
    a1t[...] = x1.T
    for copy in copies[2:]:
        copy.wait()


def weight_kernel(place, a2, a2t, a1, a1t, d2, d1, c, l2, l1, bl, d2t, d1t, vt, w_hi, w_lo, bl_hi, bl_lo):
    n = d2.shape[0]
    d2t[...] = d2[...].T
    d1t[...] = d1[...].T
    x1 = split(a1[...])
    x2 = split(a2[...])
    cs = split(c[...])
    vt[0, :, :n] = a2t[...]
    vt[0, :, n:] = jnp.zeros((n, n), F32)
    vt[1, :, :n] = -dot3(x2, split(dot3(cs, x1))).T
    vt[1, :, n:] = a1t[...]
    w1 = dot3(x1, split(l1[...]))
    hi, lo = split(w1)
    w_hi[n:] = hi
    w_lo[n:] = lo
    hi, lo = split(dot3(x2, split(l2[...] - dot3(cs, (hi, lo)))))
    w_hi[:n] = hi
    w_lo[:n] = lo
    bl_hi[...], bl_lo[...] = split(bl[...])


def first_kernel(place, g2, g1, p2, p1, along_x, along_y):
    w = g2.shape[0]
    along_x[:w] = g1[...]
    along_x[w : 2 * w] = p2[...]
    along_x[2 * w :] = p1[...]
    along_y[...] = g2[...]


def far_kernel(place, x0, y0, x1, x3, x2, y1, y3, y2, far_x, far_y):
    w = y0.shape[0]
    for k, (fx, fy) in enumerate(((x0, y0), (x1, y1), (x2, y2), (x3, y3))):
        far_x[k * w : (k + 1) * w] = fy[...]
        far_y[k * w : (k + 1) * w] = fx[:w]


def gram_kernel(
    place, x0, y0, x1, x3, x2, y1, y3, y2, dx1, dx3, dx2, dy1, dy3, dy2, hi, lo, keep, send, p,
):
    x, y, core = (place[0], place[1], place[2])
    n = hi.shape[0] // 2
    w = y0.shape[0]

    def put(values, half, xx, yy):
        at = pl.multiple_of(half * n + ((yy & 3) * 4 + (xx & 3)) * w, w)
        h, l = split(values)
        hi[pl.ds(at, w)] = h
        lo[pl.ds(at, w)] = l

    for k, (fx, fy) in enumerate(((x0, y0), (x1, y1), (x2, y2), (x3, y3))):
        put(fy[...], 0, x, y + 4 - k)
        put(fx[:w], 1, x + 4 - k, y)
        rows = pl.ds(pl.multiple_of(((x + 4 - k) & 3) * w, w), w)
        p[0, rows] = fx[w : 2 * w]
        p[1, rows] = fx[2 * w :]
    for k, (fx, fy) in enumerate(((dx1, dy1), (dx2, dy2), (dx3, dy3))):
        for j in range(4):
            rows = slice(j * w, (j + 1) * w)
            put(fx[rows], 0, x + 3 - k, y + 4 - j)
            put(fy[rows], 1, x + 4 - j, y + 3 - k)
    both = split(jnp.concatenate([p[0], p[1]], axis=0))
    wide = dot3((hi[:n], lo[:n]), both, NT)
    tall = dot3((hi[n:], lo[n:]), split(p[1]), NT)
    half = n // 2
    packed = jnp.concatenate([wide, jnp.concatenate([tall[:half], tall[half:]], axis=1)], axis=0)
    part = packed.shape[0] // 2

    @pl.when(core == 0)
    def _():
        keep[...] = packed[:part]
        send[...] = packed[part:]

    @pl.when(core == 1)
    def _():
        keep[...] = packed[part:]
        send[...] = packed[:part]


def add_kernel(place, a, b, out):
    out[...] = a[...] + b[...]


def stack_kernel(place, a, b, c, d, out):
    out[0] = a[...]
    out[1] = b[...]
    out[2] = c[...]
    out[3] = d[...]


def below_sum_kernel(place, hi, lo, bl_hi, bl_lo, a2t, a1t, c, keep, send):
    core = place[2]
    n = a2t.shape[0]
    share = n // 4
    below = (bl_hi[...], bl_lo[...])
    q2 = dot3((hi[:n], lo[:n]), below)
    u2 = dot3f(a2t[...], q2)
    q1 = dot3((hi[n:], lo[n:]), below)
    u1 = dot3f(a1t[...], q1 - dot3f(c[...].T, u2))
    for k in range(2):

        @pl.when(core == k)
        def _():
            for r in range(4):
                ref = keep if r % 2 == k else send
                ref[r // 2, :share] = u2[r * share : (r + 1) * share]
                ref[r // 2, share:] = u1[r * share : (r + 1) * share]


def pair_kernel(place, keep, got, mine, send):
    z = place[3]
    mine[...] = (keep[pl.ds(z, 1)] + got[pl.ds(z, 1)])[0]
    send[...] = (keep[pl.ds(1 - z, 1)] + got[pl.ds(1 - z, 1)])[0]


def below_kernel(place, hi, lo, w_hi, w_lo, vt, grad, out, s2t, s1t, held, sems):
    w = s2t.shape[0]
    weights = (w_hi[...], w_lo[...])
    steps = sems.shape[0]
    tall = held.shape[0] // steps
    copies = []
    for k in range(steps):
        rows = pl.ds(k * tall, tall)
        held[rows] = grad[rows] - dot3((hi[:, rows], lo[:, rows]), weights, TN)
        copies.append(pltpu.make_async_copy(held.at[rows], out.at[rows], sems.at[k]))
        copies[-1].start()
    at = pl.multiple_of((place[1] * 4 + place[0]) * w, w)
    v = jnp.concatenate([vt[0, pl.ds(at, w)], vt[1, pl.ds(at, w)]], axis=0)
    solved = dot3(split(v), (hi[...], lo[...]))
    s2t[...] = solved[:w]
    s1t[...] = solved[w:]
    for copy in copies:
        copy.wait()


def chain_kernel(
    place, mine, other, a2, a2t, a1, a1t, d2t, d1t, c, gd2, gd1, gc, l2, l1, gl2, gl1,
    left2, left1, o_diag2, o_diag1, o_cross, whole, tall, rows2, rows1, rowsx, rowsxt,
):
    n = a2.shape[0]
    first = place[2] == 0
    quarter = n // 4
    half = n // 2
    for k, by in enumerate((0, 1, 3, 2)):
        y = (place[1] + 4 - by) & 3
        a, b = (mine[k], other[k])
        block = jnp.concatenate([jnp.where(first, a, b), jnp.where(first, b, a)], axis=0)
        whole[y] = block[:n]
        tall[y, :half] = block[n:, :quarter]
        tall[y, half:] = block[n:, quarter:]
    row, col = positions(n)
    lower = row >= col
    both = [dot3f(a2t[...], whole[y]) for y in range(4)]
    gram2 = jnp.concatenate([b[:, :quarter] for b in both], axis=1)
    gram_cross = jnp.concatenate([b[:, quarter:] for b in both], axis=1)
    tall = jnp.concatenate([tall[y] for y in range(4)], axis=1)
    below = dot3f(a1t[...], tall - dot3f(c[...].T, gram_cross))
    inner = halved(dot3f(d2t[...], gd2[...] - jnp.where(lower, gram2, 0.0)))
    spread = dot3f(dot3f(a2t[...], inner), a2[...])
    sym2 = spread + spread.T
    rows2[...] = sym2
    o_diag2[...] = halved(sym2)
    cross = dot3f(gc[...] - gram_cross - dot3f(sym2, c[...]), a1[...])
    o_cross[...] = cross
    rowsx[...] = cross
    cross_turned = cross.T
    rowsxt[...] = cross_turned
    gram1 = dot3f(cross_turned, c[...]) + below
    inner = halved(dot3f(d1t[...], gd1[...] - jnp.where(lower, gram1, 0.0)))
    spread = dot3f(dot3f(a1t[...], inner), a1[...])
    sym1 = spread + spread.T
    rows1[...] = sym1
    o_diag1[...] = halved(sym1)
    share = gl2.shape[0]
    at = pl.ds(pl.multiple_of((place[3] * 2 + place[2]) * share, share), share)
    l2s, l1s = (split(l2[...]), split(l1[...]))
    left2[...] = gl2[...] - dot3(split(rows2[at]), l2s) - dot3(split(rowsx[at]), l1s)
    left1[...] = gl1[...] - dot3(split(rowsxt[at]), l2s) - dot3(split(rows1[at]), l1s)


def left_kernel(place, left2, left1, part, got, o_left2, o_left1):
    share = left2.shape[0]
    o_left2[...] = left2[...] - (part[:share] + got[:share])
    o_left1[...] = left1[...] - (part[share:] + got[share:])


def shifted(value, axis, by):
    count = lax.axis_size(axis)
    return lax.ppermute(value, axis, [(i, (i + by) % count) for i in range(count)])


def shifts(value, axis):
    return [shifted(value, axis, k) for k in (1, 3, 2)]


def after(values, first):
    return lax.optimization_barrier((tuple(values), first))[0]


def body(d2, d1, c, l2, l1, bl, p2, p1, gd2, gd1, gc, gl2, gl1, gb, g2, g1):
    n = d2.shape[0]
    width = l2.shape[1]
    rows, w = p2.shape
    core = lax.axis_index("core")
    place = jnp.stack(
        [lax.axis_index("x"), lax.axis_index("y"), core, lax.axis_index("zlo")]
    ).astype(jnp.int32)
    along_x, along_y = call(
        first_kernel,
        "first",
        (near(3 * w, rows), near(w, rows)),
        (place, g2.T, g1.T, p2.T, p1.T),
        (),
        1.0,
        4,
    )
    xs = shifts(along_x, "x")
    ys = shifts(along_y, "y")
    square = near(n, n)
    given = after((d2, d1, c, l2, l1, bl, gd2, gd1, gc, gl2, gl1, gb), along_x)
    a2, a2t, a1, a1t, d2, d1, c, l2, l1, bl, gd2, gd1, gc, gl2, gl1, gb = call(
        inverse_kernel,
        "inverses",
        (square,) * 4 + tuple(near(*v.shape) for v in given),
        (place, *given),
        (pltpu.SemaphoreType.DMA((len(given),)),),
        4.0,
        len(given),
        pltpu.HBM,
    )
    pieces = (along_x, along_y, *xs, *ys)
    (x0,) = after((along_x,), a2)
    far_x, far_y = call(
        far_kernel, "far", (near(4 * w, rows),) * 2, (place, x0, *pieces[1:]), (), 0.6
    )
    dxs = shifts(far_x, "x")
    dys = shifts(far_y, "y")
    halves = (near(rows, width, dtype=BF16),) * 2
    thick = (near(2 * n, width, dtype=BF16),) * 2
    (bl,) = after((bl,), far_x)
    d2t, d1t, vt, w_hi, w_lo, bl_hi, bl_lo = call(
        weight_kernel,
        "weights",
        (square, square, near(2, n, 2 * n), *thick, *halves),
        (place, a2, a2t, a1, a1t, d2, d1, c, l2, l1, bl),
        (),
        2.7,
    )
    half = near(6 * n // 8, n // 2)
    (x0,) = after((along_x,), w_hi)
    hi, lo, keep, send = call(
        gram_kernel,
        "grams",
        (near(2 * n, rows, dtype=BF16),) * 2 + (half, half),
        (place, x0, *pieces[1:], *dxs, *dys),
        (pltpu.VMEM((2, 4 * w, rows), F32),),
        2.0,
    )
    (gram,) = call(
        add_kernel, "pair_gram", (half,), (place, keep, shifted(send, "core", 1)), (), 0.5
    )
    (below_hi,) = after((bl_hi,), gram)
    keep, send = call(
        below_sum_kernel,
        "below_sums",
        (near(2, n // 2, width),) * 2,
        (place, hi, lo, below_hi, bl_lo, a2t, a1t, c),
        (),
        3.0,
    )
    (gram,) = call(
        add_kernel,
        "row_gram",
        (half,),
        (place, *after((gram,), keep), shifted(gram, "zlo", 1)),
        (),
        0.6,
    )
    part, send = call(
        pair_kernel,
        "pair_sums",
        (near(n // 2, width),) * 2,
        (place, keep, shifted(send, "core", 1)),
        (),
        0.6,
    )
    got = shifted(send, "zlo", 1)
    (gb,) = after((gb,), (send, gram))
    out_below, s2t, s1t = call(
        below_kernel,
        "below_outputs",
        (shaped(rows, width), shaped(w, rows), shaped(w, rows)),
        (place, hi, lo, w_hi, w_lo, vt, gb),
        (pltpu.VMEM(gb.shape, F32), pltpu.SemaphoreType.DMA((4,))),
        3.8,
        out_specs=[pl.BlockSpec(memory_space=pltpu.HBM), VMEM, VMEM],
    )
    (mine,) = call(
        stack_kernel,
        "stack",
        (near(4, *half.shape),),
        (place, *after((gram,), s2t), *shifts(gram, "y")),
        (),
        0.8,
    )
    left2, left1, diag2, diag1, cross = call(
        chain_kernel,
        "chain",
        (near(*gl2.shape), near(*gl2.shape), shaped(n, n), shaped(n, n), shaped(n, n)),
        (place, mine, shifted(mine, "core", 1), a2, a2t, a1, a1t, d2t, d1t, c, gd2, gd1, gc, l2, l1, gl2, gl1),
        (pltpu.VMEM((4, n, n // 2), F32), pltpu.VMEM((4, n, n // 4), F32))
        + (pltpu.VMEM((n, n), F32),) * 4,
        5.2,
    )
    left2, left1 = call(
        left_kernel, "left", (shaped(*gl2.shape),) * 2, (place, left2, left1, part, got), (), 1.0
    )
    return out_below, left2, left1, diag2, diag1, cross, s2t.T, s1t.T


def solution(mesh):
    fine = Mesh(
        mesh.devices.reshape(2, 2, 4, 4, 4), ("zlo", "core", "y", "x", "dep")
    )
    row, col, deep = (("zlo", "core"), ("y", "x"), ("y", "x", "dep"))
    return jax.shard_map(
        body,
        mesh=fine,
        in_specs=(
            P(),
            P(),
            P(),
            P(None, deep),
            P(None, deep),
            P(row, deep),
            P(row, col),
            P(row, col),
            P(),
            P(),
            P(),
            P(row, deep),
            P(row, deep),
            P(row, deep),
            P(row, col),
            P(row, col),
        ),
        out_specs=(
            P(row, deep),
            P(row, deep),
            P(row, deep),
            P(),
            P(),
            P(),
            P(row, col),
            P(row, col),
        ),
        check_vma=False,
    )
```

time: 107 us -> 70.6 us (0.66)
  Pallas kernels: 47 us -> 26.8 us
  blocking collectives: 13.4 us -> 0 us
  waiting for transfers between devices: 5.35 us -> 10.2 us
  local copies, waits for them, and re-layouts: 3.84 us -> 0 us
  starting transfers between devices: 34.6 us -> 32.5 us
  other arithmetic: 1.54 us -> 0.08 us
    pallas_call x7 -> x13, Pallas kernels: 47 us -> 26.8 us  [call(): pl.pallas_call(kernel, out_shape=tuple(outs), in_specs=[SMEM] + [VMEM] *...]
    all_to_all x1 -> x0, blocking collectives: 13.4 us -> none  [shared(): lax.all_to_all(jnp.broadcast_to(value[None], (count, *value.shape)), axes...]
    all_to_all x1 -> x0, starting transfers between devices: 11.7 us -> none  [shared(): lax.all_to_all(jnp.broadcast_to(value[None], (count, *value.shape)), axes...]
    ppermute x15 -> x20, starting transfers between devices: 22.9 us -> 32.5 us  [shifted(): lax.ppermute(value, axis, [(i, (i + by) % count) for i in range(count)])]
    ppermute x15 -> x20, waiting for transfers between devices: 5.35 us -> 10.2 us  [shifted(): lax.ppermute(value, axis, [(i, (i + by) % count) for i in range(count)])]
    unnamed x34 -> x0, local copies, waits for them, and re-layouts: 2.27 us -> none
    broadcast_in_dim x2 -> x0, local copies, waits for them, and re-layouts: 1.52 us -> none  [shared(): jnp.broadcast_to(value[None], (count, *value.shape))]
  transfers between devices with their start and end apart: 16 -> 20, of which waited for: 6 -> 6; matrix products, arithmetic and copies ran while one was open for 1% -> 0% of each run, Pallas kernels for 32% -> 25%
where the time goes in v2:
time: 70.6 us; the launch traced here: 70.5 us
  starting transfers between devices  32.5 us (46%)
  Pallas kernels  26.8 us (38%)
  waiting for transfers between devices  10.2 us (14%)
  between operations  0.82 us (1%)
    ppermute x20, starting transfers between devices, shifted(): lax.ppermute(value, axis, [(i, (i + by) % count) for i in range(count)])  32.5 us
    pallas_call x13, Pallas kernels, call(): pl.pallas_call(kernel, out_shape=tuple(outs), in_specs=[SMEM] + [VMEM] *...  26.8 us
    ppermute x20, waiting for transfers between devices, shifted(): lax.ppermute(value, axis, [(i, (i + by) % count) for i in range(count)])  10.2 us
  transfers between devices with their start and end apart: 20, of which 6 were waited for; matrix products, arithmetic and copies ran while one was open for 0% of the time, Pallas kernels for 25%

profile of v2, /device:TPU:1, one launch (start us, length us, event | category | flops | bytes accessed | tf_op | source)
XLA Modules:
  0.0 70.5 jit_solution(12296887384007309602)
XLA Ops:
  0.6 0.1 pad_add_fusion.place
  0.7 1.0 %first.1 = (f32[48,1024]{1,0:T(8,128)S(1)}, f32[16,1024]{1,0:T(8,128)S(1)}) custom-call(s32[4]{0:T(128)S(1)} %pad_add_fusion.place, f32[16,1024]{1,0:T(8,128)} %bitcast.10, f32[16,1024]{1,0:T(8,128)} %bitcast.11, f32[16,1024]{1,0:T(8,128)} %bitcast.12, f32[16,1024]{1,0:T(8,128)} %bitcast.13), custom_call_target="tpu_custom_call" | custom-call | flops 1000000000 | bytes 3000000 | tf_op jit(solution)/shard_map/first/pallas_call | solution.py:46
  1.7 2.2 %collective-permute-start.3 = (f32[16,1024]{1,0:T(8,128)S(1)}, f32[16,1024]{1,0:T(8,128)S(1)}, u32[]{:S(2)}, u32[]{:S(2)}) collective-permute-start(f32[16,1024]{1,0:T(8,128)S(1)} %get-tuple-element.96.y0), channel_id=1, source_target_pairs={{0,16},{16,32},{32,48},{48,0},{1,17},{17,33},{33,49},{49,1},{2,18}... | collective-permute-start | bytes 196616 | tf_op jit(solution)/shard_map/ppermute | solution.py:341
  3.9 1.2 %collective-permute-start = (f32[48,1024]{1,0:T(8,128)S(1)}, f32[48,1024]{1,0:T(8,128)S(1)}, u32[]{:S(2)}, u32[]{:S(2)}) collective-permute-start(f32[48,1024]{1,0:T(8,128)S(1)} %get-tuple-element.100.x0), channel_id=1, source_target_pairs={{0,4},{4,8},{8,12},{12,0},{1,5},{5,9},{9,13},{13,1},{2,6},{6,10},{... | collective-permute-start | bytes 589832 | tf_op jit(solution)/shard_map/ppermute | solution.py:341
  5.1 1.5 %collective-permute-start.1 = (f32[48,1024]{1,0:T(8,128)S(1)}, f32[48,1024]{1,0:T(8,128)S(1)}, u32[]{:S(2)}, u32[]{:S(2)}) collective-permute-start(f32[48,1024]{1,0:T(8,128)S(1)} %get-tuple-element.100.x0), channel_id=1, source_target_pairs={{0,12},{4,0},{8,4},{12,8},{1,13},{5,1},{9,5},{13,9},{2,14},{6,2},{... | collective-permute-start | bytes 589832 | tf_op jit(solution)/shard_map/ppermute | solution.py:341
  6.6 1.5 %collective-permute-start.2 = (f32[48,1024]{1,0:T(8,128)S(1)}, f32[48,1024]{1,0:T(8,128)S(1)}, u32[]{:S(2)}, u32[]{:S(2)}) collective-permute-start(f32[48,1024]{1,0:T(8,128)S(1)} %get-tuple-element.100.x0), channel_id=1, source_target_pairs={{0,8},{4,12},{8,0},{12,4},{1,9},{5,13},{9,1},{13,5},{2,10},{6,14},... | collective-permute-start | bytes 589832 | tf_op jit(solution)/shard_map/ppermute | solution.py:341
  8.1 1.5 %collective-permute-start.4 = (f32[16,1024]{1,0:T(8,128)S(1)}, f32[16,1024]{1,0:T(8,128)S(1)}, u32[]{:S(2)}, u32[]{:S(2)}) collective-permute-start(f32[16,1024]{1,0:T(8,128)S(1)} %get-tuple-element.96.y0), channel_id=1, source_target_pairs={{0,48},{16,0},{32,16},{48,32},{1,49},{17,1},{33,17},{49,33},{2,50}... | collective-permute-start | bytes 196616 | tf_op jit(solution)/shard_map/ppermute | solution.py:341
  9.6 0.0 collective-permute-done.3.y1
  9.6 1.6 %collective-permute-start.5 = (f32[16,1024]{1,0:T(8,128)S(1)}, f32[16,1024]{1,0:T(8,128)S(1)}, u32[]{:S(2)}, u32[]{:S(2)}) collective-permute-start(f32[16,1024]{1,0:T(8,128)S(1)} %get-tuple-element.96.y0), channel_id=1, source_target_pairs={{0,32},{16,48},{32,0},{48,16},{1,33},{17,49},{33,1},{49,17},{2,34}... | collective-permute-start | bytes 196616 | tf_op jit(solution)/shard_map/ppermute | solution.py:341
  11.2 4.4 %inverses.1 = (f32[256,256]{1,0:T(8,128)S(1)}, f32[256,256]{1,0:T(8,128)S(1)}, f32[256,256]{1,0:T(8,128)S(1)}, f32[256,256]{1,0:T(8,128)S(1)}, f32[256,256]{1,0:...) custom-call(s32[4]{0:T(128)S(1)} %pad_add_fusion.place, ...), custom_call_target="tpu_custom_call" | custom-call | flops 4000000000 | bytes 12000000 | tf_op jit(solution)/shard_map/inverses/pallas_call | solution.py:46
  15.6 0.0 collective-permute-done.4.y3
  15.6 0.0 collective-permute-done.5.y2
  15.6 0.0 collective-permute-done.x1
  15.6 0.0 collective-permute-done.1.x3
  15.6 0.1 collective-permute-done.2.x2
  15.8 0.6 far.1
  16.3 1.7 %collective-permute-start.10 = (f32[64,1024]{1,0:T(8,128)S(1)}, f32[64,1024]{1,0:T(8,128)S(1)}, u32[]{:S(2)}, u32[]{:S(2)}) collective-permute-start(f32[64,1024]{1,0:T(8,128)S(1)} %get-tuple-element.101), channel_id=1, source_target_pairs={{0,48},{16,0},{32,16},{48,32},{1,49},{17,1},{33,17},{49,33},{2,50}... | collective-permute-start | bytes 786440 | tf_op jit(solution)/shard_map/ppermute | solution.py:341
  18.0 1.5 %collective-permute-start.11 = (f32[64,1024]{1,0:T(8,128)S(1)}, f32[64,1024]{1,0:T(8,128)S(1)}, u32[]{:S(2)}, u32[]{:S(2)}) collective-permute-start(f32[64,1024]{1,0:T(8,128)S(1)} %get-tuple-element.101), channel_id=1, source_target_pairs={{0,32},{16,48},{32,0},{48,16},{1,33},{17,49},{33,1},{49,17},{2,34}... | collective-permute-start | bytes 786440 | tf_op jit(solution)/shard_map/ppermute | solution.py:341
  19.5 0.6 collective-permute-start.6
  20.1 2.1 %collective-permute-start.7 = (f32[64,1024]{1,0:T(8,128)S(1)}, f32[64,1024]{1,0:T(8,128)S(1)}, u32[]{:S(2)}, u32[]{:S(2)}) collective-permute-start(f32[64,1024]{1,0:T(8,128)S(1)} %get-tuple-element.97), channel_id=1, source_target_pairs={{0,12},{4,0},{8,4},{12,8},{1,13},{5,1},{9,5},{13,9},{2,14},{6,2},{... | collective-permute-start | bytes 786440 | tf_op jit(solution)/shard_map/ppermute | solution.py:341
  22.2 0.0 collective-permute-start.8
  22.2 0.0 collective-permute-done.10.dy3
  22.2 1.5 %collective-permute-start.9 = (f32[64,1024]{1,0:T(8,128)S(1)}, f32[64,1024]{1,0:T(8,128)S(1)}, u32[]{:S(2)}, u32[]{:S(2)}) collective-permute-start(f32[64,1024]{1,0:T(8,128)S(1)} %get-tuple-element.101), channel_id=1, source_target_pairs={{0,16},{16,32},{32,48},{48,0},{1,17},{17,33},{33,49},{49,1},{2,18}... | collective-permute-start | bytes 786440 | tf_op jit(solution)/shard_map/ppermute | solution.py:341
  23.6 2.7 %weights.1 = (f32[256,256]{1,0:T(8,128)S(1)}, f32[256,256]{1,0:T(8,128)S(1)}, f32[2,256,512]{2,1,0:T(8,128)S(1)}, bf16[512,512]{1,0:T(8,128)(2,1)S(1)}, bf16[512...) custom-call(s32[4]{0:T(128)S(1)} %pad_add_fusion.place, ...), custom_call_target="tpu_custom_call" | custom-call | flops 2700000000 | bytes 8100000 | tf_op jit(solution)/shard_map/weights/pallas_call | solution.py:46
  26.3 0.0 collective-permute-done.11.dy2
  26.3 0.0 collective-permute-done.6.dx1
  26.4 1.4 %collective-permute-done.7.dx3 = f32[64,1024]{1,0:T(8,128)S(1)} collective-permute-done((f32[64,1024]{1,0:T(8,128)S(1)}, f32[64,1024]{1,0:T(8,128)S(1)}, u32[]{:S(2)}, u32[]{:S(2)}) %collective-permute-start.7) | collective-permute-done | bytes 262176 | tf_op jit(solution)/shard_map/ppermute | solution.py:341
  27.8 3.8 %collective-permute-done.8.dx2 = f32[64,1024]{1,0:T(8,128)S(1)} collective-permute-done((f32[64,1024]{1,0:T(8,128)S(1)}, f32[64,1024]{1,0:T(8,128)S(1)}, u32[]{:S(2)}, u32[]{:S(2)}) %collective-permute-start.8) | collective-permute-done | bytes 262176 | tf_op jit(solution)/shard_map/ppermute | solution.py:341
  31.6 0.0 collective-permute-done.9.dy1
  31.6 1.9 %grams.1 = (bf16[512,1024]{1,0:T(8,128)(2,1)S(1)}, bf16[512,1024]{1,0:T(8,128)(2,1)S(1)}, f32[192,128]{1,0:T(8,128)S(1)}, f32[192,128]{1,0:T(8,128)S(1)}) custom-call(s32[4]{0:T(128)S(1)} %pad_add_fusion.place, f32[48,1024]{1,0:T(8,128)S(1)} %get-tuple-element.100.x0, f32[16,1024]{1,0:T(8,128)S(1)} %get-tuple-element.96.y0, ...), custom_call_target="tpu_custom_call" | custom-call | flops 2000000000 | bytes 6000000 | tf_op jit(solution)/shard_map/grams/pallas_call | solution.py:46
  33.5 6.7 %collective-permute-start.12 = (f32[192,128]{1,0:T(8,128)S(1)}, f32[192,128]{1,0:T(8,128)S(1)}, u32[]{:S(2)}, u32[]{:S(2)}) collective-permute-start(f32[192,128]{1,0:T(8,128)S(1)} %get-tuple-element.109), channel_id=1, source_target_pairs={{0,64},{64,0},{1,65},{65,1},{2,66},{66,2},{3,67},{67,3},{4,68},{68... | collective-permute-start | bytes 294920 | tf_op jit(solution)/shard_map/ppermute | solution.py:341
  40.2 0.9 %collective-permute-done.12.b = f32[192,128]{1,0:T(8,128)S(1)} collective-permute-done((f32[192,128]{1,0:T(8,128)S(1)}, f32[192,128]{1,0:T(8,128)S(1)}, u32[]{:S(2)}, u32[]{:S(2)}) %collective-permute-start.12) | collective-permute-done | bytes 98336 | tf_op jit(solution)/shard_map/ppermute | solution.py:341
  41.1 0.6 pair_gram.1.a
  41.7 3.3 %below_sums.1 = (f32[2,128,512]{2,1,0:T(8,128)S(1)}, f32[2,128,512]{2,1,0:T(8,128)S(1)}) custom-call(s32[4]{0:T(128)S(1)} %pad_add_fusion.place, bf16[512,1024]{1,0:T(8,128)(2,1)S(1)} %get-tuple-element.102.hi, bf16[512,1024]{1,0:T(8,128)(2,1)S(1)} %get-tuple-element.103.lo, bf16[1024,512]{1,0:T(8,128)(2,1)S(1)} %get-tuple-element.110.bl_hi, ...), custom_call_target="tpu_custom_call" | custom-call | flops 3000000000 | bytes 9000000 | tf_op jit(solution)/shard_map/below_sums/pallas_call | solution.py:46
  45.0 0.4 collective-permute-start.13
  45.5 1.7 %collective-permute-start.14 = (f32[192,128]{1,0:T(8,128)S(1)}, f32[192,128]{1,0:T(8,128)S(1)}, u32[]{:S(2)}, u32[]{:S(2)}) collective-permute-start(f32[192,128]{1,0:T(8,128)S(1)} %pair_gram.1.a), channel_id=1, source_target_pairs={{0,128},{128,0},{1,129},{129,1},{2,130},{130,2},{3,131},{131,3},{4... | collective-permute-start | bytes 294920 | tf_op jit(solution)/shard_map/ppermute | solution.py:341
  47.2 3.1 %collective-permute-done.14.b = f32[192,128]{1,0:T(8,128)S(1)} collective-permute-done((f32[192,128]{1,0:T(8,128)S(1)}, f32[192,128]{1,0:T(8,128)S(1)}, u32[]{:S(2)}, u32[]{:S(2)}) %collective-permute-start.14) | collective-permute-done | bytes 98336 | tf_op jit(solution)/shard_map/ppermute | solution.py:341
  50.3 0.6 row_gram.1.a
  50.9 0.1 collective-permute-start.15
  50.9 2.7 %collective-permute-start.16 = (f32[192,128]{1,0:T(8,128)S(1)}, f32[192,128]{1,0:T(8,128)S(1)}, u32[]{:S(2)}, u32[]{:S(2)}) collective-permute-start(f32[192,128]{1,0:T(8,128)S(1)} %row_gram.1.a), channel_id=1, source_target_pairs={{0,48},{16,0},{32,16},{48,32},{1,49},{17,1},{33,17},{49,33},{2,50}... | collective-permute-start | bytes 294920 | tf_op jit(solution)/shard_map/ppermute | solution.py:341
  53.6 0.3 collective-permute-start.17
  53.9 0.0 collective-permute-done.13.got
  53.9 0.6 pair_sums.1
  54.5 4.1 %below_outputs.1 = (f32[1024,512]{1,0:T(8,128)}, f32[16,1024]{1,0:T(8,128)}, f32[16,1024]{1,0:T(8,128)}) custom-call(s32[4]{0:T(128)S(1)} %pad_add_fusion.place, bf16[512,1024]{1,0:T(8,128)(2,1)S(1)} %get-tuple-element.102.hi, bf16[512,1024]{1,0:T(8,128)(2,1)S(1)} %get-tuple-element.103.lo, bf16[512,512]{1,0:T(8,128)(2,1)S(1)} %get-tuple-element.99.w_hi, ...), custom_call_target="tpu_custom_call" | custom-call | flops 3800000000 | bytes 11400000 | tf_op jit(solution)/shard_map/below_outputs/pallas_call | solution.py:46
  58.6 0.0 collective-permute-done.15.b
  58.6 0.0 collective-permute-done.16.c
  58.6 0.0 collective-permute-done.17.d
  58.6 0.6 stack.21.mine
  59.2 2.4 %collective-permute-start.18 = (f32[4,192,128]{2,1,0:T(8,128)S(1)}, f32[4,192,128]{2,1,0:T(8,128)S(1)}, u32[]{:S(2)}, u32[]{:S(2)}) collective-permute-start(f32[4,192,128]{2,1,0:T(8,128)S(1)} %stack.21.mine), channel_id=1, source_target_pairs={{0,64},{64,0},{1,65},{65,1},{2,66},{66,2},{3,67},{67,3},{4,68},{68... | collective-permute-start | bytes 1179656 | tf_op jit(solution)/shard_map/ppermute | solution.py:341
  61.6 1.5 %collective-permute-start.19 = (f32[128,512]{1,0:T(8,128)S(1)}, f32[128,512]{1,0:T(8,128)S(1)}, u32[]{:S(2)}, u32[]{:S(2)}) collective-permute-start(f32[128,512]{1,0:T(8,128)S(1)} %get-tuple-element.114), channel_id=1, source_target_pairs={{0,128},{128,0},{1,129},{129,1},{2,130},{130,2},{3,131},{131,3},{4... | collective-permute-start | bytes 786440 | tf_op jit(solution)/shard_map/ppermute | solution.py:341
  63.1 0.0 collective-permute-done.18.other
  63.1 5.3 %chain.1 = (f32[64,512]{1,0:T(8,128)S(1)}, f32[64,512]{1,0:T(8,128)S(1)}, f32[256,256]{1,0:T(8,128)}, f32[256,256]{1,0:T(8,128)}, f32[256,256]{1,0:T(8,128)}) custom-call(s32[4]{0:T(128)S(1)} %pad_add_fusion.place, f32[4,192,128]{2,1,0:T(8,128)S(1)} %stack.21.mine, f32[4,192,128]{2,1,0:T(8,128)S(1)} %collective-permute-done.18.other, ...), custom_call_target="tpu_custom_call" | custom-call | flops 5200000000 | bytes 15600000 | tf_op jit(solution)/shard_map/chain/pallas_call | solution.py:46
  68.4 0.8 %collective-permute-done.19.got = f32[128,512]{1,0:T(8,128)S(1)} collective-permute-done((f32[128,512]{1,0:T(8,128)S(1)}, f32[128,512]{1,0:T(8,128)S(1)}, u32[]{:S(2)}, u32[]{:S(2)}) %collective-permute-start.19) | collective-permute-done | bytes 262176 | tf_op jit(solution)/shard_map/ppermute | solution.py:341
  69.2 1.3 %left.1 = (f32[64,512]{1,0:T(8,128)}, f32[64,512]{1,0:T(8,128)}) custom-call(s32[4]{0:T(128)S(1)} %pad_add_fusion.place, f32[64,512]{1,0:T(8,128)S(1)} %get-tuple-element.127.left2, f32[64,512]{1,0:T(8,128)S(1)} %get-tuple-element.128.left1, f32[128,512]{1,0:T(8,128)S(1)} %get-tuple-element.129.part, f32[128,512]{1,0:T(8,128)S(1)} %collective-permute-done.19.got), custom_call_target="tpu_custom_call" | custom-call | flops 1000000000 | bytes 3000000 | tf_op jit(solution)/shard_map/left/pallas_call | solution.py:46
Async XLA Ops:
  1.7 7.9 %collective-permute-start.3 = (f32[16,1024]{1,0:T(8,128)S(1)}, f32[16,1024]{1,0:T(8,128)S(1)}, u32[]{:S(2)}, u32[]{:S(2)}) collective-permute-start(f32[16,1024]{1,0:T(8,128)S(1)} %get-tuple-element.96.y0), channel_id=1, source_target_pairs={{0,16},{16,32},{32,48},{48,0},{1,17},{17,33},{33,49},{49,1},{2,18}... | collective-permute-start | bytes 196616 | tf_op jit(solution)/shard_map/ppermute | solution.py:341
  3.9 11.7 %collective-permute-start = (f32[48,1024]{1,0:T(8,128)S(1)}, f32[48,1024]{1,0:T(8,128)S(1)}, u32[]{:S(2)}, u32[]{:S(2)}) collective-permute-start(f32[48,1024]{1,0:T(8,128)S(1)} %get-tuple-element.100.x0), channel_id=1, source_target_pairs={{0,4},{4,8},{8,12},{12,0},{1,5},{5,9},{9,13},{13,1},{2,6},{6,10},{... | collective-permute-start | bytes 589832 | tf_op jit(solution)/shard_map/ppermute | solution.py:341
  5.1 10.5 %collective-permute-start.1 = (f32[48,1024]{1,0:T(8,128)S(1)}, f32[48,1024]{1,0:T(8,128)S(1)}, u32[]{:S(2)}, u32[]{:S(2)}) collective-permute-start(f32[48,1024]{1,0:T(8,128)S(1)} %get-tuple-element.100.x0), channel_id=1, source_target_pairs={{0,12},{4,0},{8,4},{12,8},{1,13},{5,1},{9,5},{13,9},{2,14},{6,2},{... | collective-permute-start | bytes 589832 | tf_op jit(solution)/shard_map/ppermute | solution.py:341
  6.6 9.2 %collective-permute-start.2 = (f32[48,1024]{1,0:T(8,128)S(1)}, f32[48,1024]{1,0:T(8,128)S(1)}, u32[]{:S(2)}, u32[]{:S(2)}) collective-permute-start(f32[48,1024]{1,0:T(8,128)S(1)} %get-tuple-element.100.x0), channel_id=1, source_target_pairs={{0,8},{4,12},{8,0},{12,4},{1,9},{5,13},{9,1},{13,5},{2,10},{6,14},... | collective-permute-start | bytes 589832 | tf_op jit(solution)/shard_map/ppermute | solution.py:341
  8.1 7.5 %collective-permute-start.4 = (f32[16,1024]{1,0:T(8,128)S(1)}, f32[16,1024]{1,0:T(8,128)S(1)}, u32[]{:S(2)}, u32[]{:S(2)}) collective-permute-start(f32[16,1024]{1,0:T(8,128)S(1)} %get-tuple-element.96.y0), channel_id=1, source_target_pairs={{0,48},{16,0},{32,16},{48,32},{1,49},{17,1},{33,17},{49,33},{2,50}... | collective-permute-start | bytes 196616 | tf_op jit(solution)/shard_map/ppermute | solution.py:341
  9.6 6.0 %collective-permute-start.5 = (f32[16,1024]{1,0:T(8,128)S(1)}, f32[16,1024]{1,0:T(8,128)S(1)}, u32[]{:S(2)}, u32[]{:S(2)}) collective-permute-start(f32[16,1024]{1,0:T(8,128)S(1)} %get-tuple-element.96.y0), channel_id=1, source_target_pairs={{0,32},{16,48},{32,0},{48,16},{1,33},{17,49},{33,1},{49,17},{2,34}... | collective-permute-start | bytes 196616 | tf_op jit(solution)/shard_map/ppermute | solution.py:341
  16.3 5.8 %collective-permute-start.10 = (f32[64,1024]{1,0:T(8,128)S(1)}, f32[64,1024]{1,0:T(8,128)S(1)}, u32[]{:S(2)}, u32[]{:S(2)}) collective-permute-start(f32[64,1024]{1,0:T(8,128)S(1)} %get-tuple-element.101), channel_id=1, source_target_pairs={{0,48},{16,0},{32,16},{48,32},{1,49},{17,1},{33,17},{49,33},{2,50}... | collective-permute-start | bytes 786440 | tf_op jit(solution)/shard_map/ppermute | solution.py:341
  18.0 8.3 %collective-permute-start.11 = (f32[64,1024]{1,0:T(8,128)S(1)}, f32[64,1024]{1,0:T(8,128)S(1)}, u32[]{:S(2)}, u32[]{:S(2)}) collective-permute-start(f32[64,1024]{1,0:T(8,128)S(1)} %get-tuple-element.101), channel_id=1, source_target_pairs={{0,32},{16,48},{32,0},{48,16},{1,33},{17,49},{33,1},{49,17},{2,34}... | collective-permute-start | bytes 786440 | tf_op jit(solution)/shard_map/ppermute | solution.py:341
  19.5 6.9 %collective-permute-start.6 = (f32[64,1024]{1,0:T(8,128)S(1)}, f32[64,1024]{1,0:T(8,128)S(1)}, u32[]{:S(2)}, u32[]{:S(2)}) collective-permute-start(f32[64,1024]{1,0:T(8,128)S(1)} %get-tuple-element.97), channel_id=1, source_target_pairs={{0,4},{4,8},{8,12},{12,0},{1,5},{5,9},{9,13},{13,1},{2,6},{6,10},{... | collective-permute-start | bytes 786440 | tf_op jit(solution)/shard_map/ppermute | solution.py:341
  20.1 7.7 %collective-permute-start.7 = (f32[64,1024]{1,0:T(8,128)S(1)}, f32[64,1024]{1,0:T(8,128)S(1)}, u32[]{:S(2)}, u32[]{:S(2)}) collective-permute-start(f32[64,1024]{1,0:T(8,128)S(1)} %get-tuple-element.97), channel_id=1, source_target_pairs={{0,12},{4,0},{8,4},{12,8},{1,13},{5,1},{9,5},{13,9},{2,14},{6,2},{... | collective-permute-start | bytes 786440 | tf_op jit(solution)/shard_map/ppermute | solution.py:341
  22.2 9.4 %collective-permute-start.8 = (f32[64,1024]{1,0:T(8,128)S(1)}, f32[64,1024]{1,0:T(8,128)S(1)}, u32[]{:S(2)}, u32[]{:S(2)}) collective-permute-start(f32[64,1024]{1,0:T(8,128)S(1)} %get-tuple-element.97), channel_id=1, source_target_pairs={{0,8},{4,12},{8,0},{12,4},{1,9},{5,13},{9,1},{13,5},{2,10},{6,14},... | collective-permute-start | bytes 786440 | tf_op jit(solution)/shard_map/ppermute | solution.py:341
  22.2 9.4 %collective-permute-start.9 = (f32[64,1024]{1,0:T(8,128)S(1)}, f32[64,1024]{1,0:T(8,128)S(1)}, u32[]{:S(2)}, u32[]{:S(2)}) collective-permute-start(f32[64,1024]{1,0:T(8,128)S(1)} %get-tuple-element.101), channel_id=1, source_target_pairs={{0,16},{16,32},{32,48},{48,0},{1,17},{17,33},{33,49},{49,1},{2,18}... | collective-permute-start | bytes 786440 | tf_op jit(solution)/shard_map/ppermute | solution.py:341
  33.5 7.6 %collective-permute-start.12 = (f32[192,128]{1,0:T(8,128)S(1)}, f32[192,128]{1,0:T(8,128)S(1)}, u32[]{:S(2)}, u32[]{:S(2)}) collective-permute-start(f32[192,128]{1,0:T(8,128)S(1)} %get-tuple-element.109), channel_id=1, source_target_pairs={{0,64},{64,0},{1,65},{65,1},{2,66},{66,2},{3,67},{67,3},{4,68},{68... | collective-permute-start | bytes 294920 | tf_op jit(solution)/shard_map/ppermute | solution.py:341
  45.0 8.8 %collective-permute-start.13 = (f32[2,128,512]{2,1,0:T(8,128)S(1)}, f32[2,128,512]{2,1,0:T(8,128)S(1)}, u32[]{:S(2)}, u32[]{:S(2)}) collective-permute-start(f32[2,128,512]{2,1,0:T(8,128)S(1)} %get-tuple-element.113), channel_id=1, source_target_pairs={{0,64},{64,0},{1,65},{65,1},{2,66},{66,2},{3,67},{67,3},{4,68},{68... | collective-permute-start | bytes 1572872 | tf_op jit(solution)/shard_map/ppermute | solution.py:341
  45.5 4.8 %collective-permute-start.14 = (f32[192,128]{1,0:T(8,128)S(1)}, f32[192,128]{1,0:T(8,128)S(1)}, u32[]{:S(2)}, u32[]{:S(2)}) collective-permute-start(f32[192,128]{1,0:T(8,128)S(1)} %pair_gram.1.a), channel_id=1, source_target_pairs={{0,128},{128,0},{1,129},{129,1},{2,130},{130,2},{3,131},{131,3},{4... | collective-permute-start | bytes 294920 | tf_op jit(solution)/shard_map/ppermute | solution.py:341
  50.9 7.7 %collective-permute-start.15 = (f32[192,128]{1,0:T(8,128)S(1)}, f32[192,128]{1,0:T(8,128)S(1)}, u32[]{:S(2)}, u32[]{:S(2)}) collective-permute-start(f32[192,128]{1,0:T(8,128)S(1)} %row_gram.1.a), channel_id=1, source_target_pairs={{0,16},{16,32},{32,48},{48,0},{1,17},{17,33},{33,49},{49,1},{2,18}... | collective-permute-start | bytes 294920 | tf_op jit(solution)/shard_map/ppermute | solution.py:341
  50.9 7.6 %collective-permute-start.16 = (f32[192,128]{1,0:T(8,128)S(1)}, f32[192,128]{1,0:T(8,128)S(1)}, u32[]{:S(2)}, u32[]{:S(2)}) collective-permute-start(f32[192,128]{1,0:T(8,128)S(1)} %row_gram.1.a), channel_id=1, source_target_pairs={{0,48},{16,0},{32,16},{48,32},{1,49},{17,1},{33,17},{49,33},{2,50}... | collective-permute-start | bytes 294920 | tf_op jit(solution)/shard_map/ppermute | solution.py:341
  53.6 5.0 %collective-permute-start.17 = (f32[192,128]{1,0:T(8,128)S(1)}, f32[192,128]{1,0:T(8,128)S(1)}, u32[]{:S(2)}, u32[]{:S(2)}) collective-permute-start(f32[192,128]{1,0:T(8,128)S(1)} %row_gram.1.a), channel_id=1, source_target_pairs={{0,32},{16,48},{32,0},{48,16},{1,33},{17,49},{33,1},{49,17},{2,34}... | collective-permute-start | bytes 294920 | tf_op jit(solution)/shard_map/ppermute | solution.py:341
  59.2 3.9 %collective-permute-start.18 = (f32[4,192,128]{2,1,0:T(8,128)S(1)}, f32[4,192,128]{2,1,0:T(8,128)S(1)}, u32[]{:S(2)}, u32[]{:S(2)}) collective-permute-start(f32[4,192,128]{2,1,0:T(8,128)S(1)} %stack.21.mine), channel_id=1, source_target_pairs={{0,64},{64,0},{1,65},{65,1},{2,66},{66,2},{3,67},{67,3},{4,68},{68... | collective-permute-start | bytes 1179656 | tf_op jit(solution)/shard_map/ppermute | solution.py:341
  61.6 7.6 %collective-permute-start.19 = (f32[128,512]{1,0:T(8,128)S(1)}, f32[128,512]{1,0:T(8,128)S(1)}, u32[]{:S(2)}, u32[]{:S(2)}) collective-permute-start(f32[128,512]{1,0:T(8,128)S(1)} %get-tuple-element.114), channel_id=1, source_target_pairs={{0,128},{128,0},{1,129},{129,1},{2,130},{130,2},{3,131},{131,3},{4... | collective-permute-start | bytes 786440 | tf_op jit(solution)/shard_map/ppermute | solution.py:341

commit v3 on v2

--- a/solution.py
+++ b/solution.py
@@ -51,7 +51,7 @@
         scratch_shapes=list(scratch),
         compiler_params=pltpu.CompilerParams(vmem_limit_bytes=20 * 2**20),
         cost_estimate=pl.CostEstimate(
-            flops=int(micros * 1e9), transcendentals=0, bytes_accessed=int(micros * 3e6)
+            flops=int(micros * 1e7), transcendentals=0, bytes_accessed=int(micros * 3e4)
         ),
         name=name,
     )(operands[0], *held, *far)
@@ -385,11 +385,10 @@
     far_x, far_y = call(
         far_kernel, "far", (near(4 * w, rows),) * 2, (place, x0, *pieces[1:]), (), 0.6
     )
-    dxs = shifts(far_x, "x")
-    dys = shifts(far_y, "y")
+    dxs = [shifted(far_x, "x", k) for k in (1, 3)]
+    dys = [shifted(far_y, "y", k) for k in (1, 3)]
     halves = (near(rows, width, dtype=BF16),) * 2
     thick = (near(2 * n, width, dtype=BF16),) * 2
-    (bl,) = after((bl,), far_x)
     d2t, d1t, vt, w_hi, w_lo, bl_hi, bl_lo = call(
         weight_kernel,
         "weights",
@@ -398,6 +397,8 @@
         (),
         2.7,
     )
+    dxs.append(shifted(after(dxs[:1], w_hi)[0], "x", 1))
+    dys.append(shifted(after(dys[1:2], w_hi)[0], "y", 3))
     half = near(6 * n // 8, n // 2)
     (x0,) = after((along_x,), w_hi)
     hi, lo, keep, send = call(
@@ -428,6 +429,7 @@
         (),
         0.6,
     )
+    (send,) = after((send,), gram)
     part, send = call(
         pair_kernel,
         "pair_sums",

time: 70.6 us -> 66.2 us (0.938)
  starting transfers between devices: 32.5 us -> 29.6 us
  waiting for transfers between devices: 10.2 us -> 8.81 us
    ppermute x20, starting transfers between devices: 32.5 us -> 29.6 us  [shifted(): lax.ppermute(value, axis, [(i, (i + by) % count) for i in range(count)])]
    ppermute x20, waiting for transfers between devices: 10.2 us -> 8.81 us  [shifted(): lax.ppermute(value, axis, [(i, (i + by) % count) for i in range(count)])]
  transfers between devices with their start and end apart: 20 -> 20, of which waited for: 6 -> 8; matrix products, arithmetic and copies ran while one was open for 0% -> 0% of each run, Pallas kernels for 25% -> 31%
where the time goes in v3:
time: 66.2 us; the launch traced here: 66.1 us
  starting transfers between devices  29.6 us (45%)
  Pallas kernels  26.7 us (40%)
  waiting for transfers between devices  8.81 us (13%)
  between operations  0.81 us (1%)
    ppermute x20, starting transfers between devices, shifted(): lax.ppermute(value, axis, [(i, (i + by) % count) for i in range(count)])  29.6 us
    pallas_call x13, Pallas kernels, call(): pl.pallas_call(kernel, out_shape=tuple(outs), in_specs=[SMEM] + [VMEM] *...  26.7 us
    ppermute x20, waiting for transfers between devices, shifted(): lax.ppermute(value, axis, [(i, (i + by) % count) for i in range(count)])  8.81 us
  transfers between devices with their start and end apart: 20, of which 8 were waited for; matrix products, arithmetic and copies ran while one was open for 0% of the time, Pallas kernels for 31%

profile of v3, /device:TPU:1, one launch (start us, length us, event | category | flops | bytes accessed | tf_op | source)
XLA Modules:
  0.0 66.1 jit_solution(8350757950129498503)
XLA Ops:
  0.6 0.1 pad_add_fusion.place
  0.7 1.0 %first.1 = (f32[48,1024]{1,0:T(8,128)S(1)}, f32[16,1024]{1,0:T(8,128)S(1)}) custom-call(s32[4]{0:T(128)S(1)} %pad_add_fusion.place, f32[16,1024]{1,0:T(8,128)} %bitcast.10, f32[16,1024]{1,0:T(8,128)} %bitcast.11, f32[16,1024]{1,0:T(8,128)} %bitcast.12, f32[16,1024]{1,0:T(8,128)} %bitcast.13), custom_call_target="tpu_custom_call" | custom-call | flops 10000000 | bytes 30000 | tf_op jit(solution)/shard_map/first/pallas_call | solution.py:46
  1.7 3.7 %collective-permute-start.2 = (f32[48,1024]{1,0:T(8,128)S(1)}, f32[48,1024]{1,0:T(8,128)S(1)}, u32[]{:S(2)}, u32[]{:S(2)}) collective-permute-start(f32[48,1024]{1,0:T(8,128)S(1)} %get-tuple-element.100.x0), channel_id=1, source_target_pairs={{0,8},{4,12},{8,0},{12,4},{1,9},{5,13},{9,1},{13,5},{2,10},{6,14},... | collective-permute-start | bytes 589832 | tf_op jit(solution)/shard_map/ppermute | solution.py:341
  5.3 0.9 %collective-permute-start.1 = (f32[48,1024]{1,0:T(8,128)S(1)}, f32[48,1024]{1,0:T(8,128)S(1)}, u32[]{:S(2)}, u32[]{:S(2)}) collective-permute-start(f32[48,1024]{1,0:T(8,128)S(1)} %get-tuple-element.100.x0), channel_id=1, source_target_pairs={{0,12},{4,0},{8,4},{12,8},{1,13},{5,1},{9,5},{13,9},{2,14},{6,2},{... | collective-permute-start | bytes 589832 | tf_op jit(solution)/shard_map/ppermute | solution.py:341
  6.2 0.6 collective-permute-start
  6.8 2.9 %collective-permute-start.5 = (f32[16,1024]{1,0:T(8,128)S(1)}, f32[16,1024]{1,0:T(8,128)S(1)}, u32[]{:S(2)}, u32[]{:S(2)}) collective-permute-start(f32[16,1024]{1,0:T(8,128)S(1)} %get-tuple-element.99.y0), channel_id=1, source_target_pairs={{0,32},{16,48},{32,0},{48,16},{1,33},{17,49},{33,1},{49,17},{2,34}... | collective-permute-start | bytes 196616 | tf_op jit(solution)/shard_map/ppermute | solution.py:341
  9.7 0.8 %collective-permute-start.4 = (f32[16,1024]{1,0:T(8,128)S(1)}, f32[16,1024]{1,0:T(8,128)S(1)}, u32[]{:S(2)}, u32[]{:S(2)}) collective-permute-start(f32[16,1024]{1,0:T(8,128)S(1)} %get-tuple-element.99.y0), channel_id=1, source_target_pairs={{0,48},{16,0},{32,16},{48,32},{1,49},{17,1},{33,17},{49,33},{2,50}... | collective-permute-start | bytes 196616 | tf_op jit(solution)/shard_map/ppermute | solution.py:341
  10.5 1.2 %collective-permute-done.5.y2 = f32[16,1024]{1,0:T(8,128)S(1)} collective-permute-done((f32[16,1024]{1,0:T(8,128)S(1)}, f32[16,1024]{1,0:T(8,128)S(1)}, u32[]{:S(2)}, u32[]{:S(2)}) %collective-permute-start.5) | collective-permute-done | bytes 65568 | tf_op jit(solution)/shard_map/ppermute | solution.py:341
  11.7 1.3 %collective-permute-start.3 = (f32[16,1024]{1,0:T(8,128)S(1)}, f32[16,1024]{1,0:T(8,128)S(1)}, u32[]{:S(2)}, u32[]{:S(2)}) collective-permute-start(f32[16,1024]{1,0:T(8,128)S(1)} %get-tuple-element.99.y0), channel_id=1, source_target_pairs={{0,16},{16,32},{32,48},{48,0},{1,17},{17,33},{33,49},{49,1},{2,18}... | collective-permute-start | bytes 196616 | tf_op jit(solution)/shard_map/ppermute | solution.py:341
  13.0 4.4 %inverses.1 = (f32[256,256]{1,0:T(8,128)S(1)}, f32[256,256]{1,0:T(8,128)S(1)}, f32[256,256]{1,0:T(8,128)S(1)}, f32[256,256]{1,0:T(8,128)S(1)}, f32[256,256]{1,0:...) custom-call(s32[4]{0:T(128)S(1)} %pad_add_fusion.place, ...), custom_call_target="tpu_custom_call" | custom-call | flops 40000000 | bytes 120000 | tf_op jit(solution)/shard_map/inverses/pallas_call | solution.py:46
  17.4 0.0 collective-permute-done.4.y3
  17.4 0.0 collective-permute-done.3.y1
  17.4 0.0 collective-permute-done.2.x2
  17.5 0.0 collective-permute-done.1.x3
  17.5 0.0 collective-permute-done.x1
  17.5 0.6 far.1
  18.1 1.5 %collective-permute-start.10 = (f32[64,1024]{1,0:T(8,128)S(1)}, f32[64,1024]{1,0:T(8,128)S(1)}, u32[]{:S(2)}, u32[]{:S(2)}) collective-permute-start(f32[64,1024]{1,0:T(8,128)S(1)} %get-tuple-element.103), channel_id=1, source_target_pairs={{0,48},{16,0},{32,16},{48,32},{1,49},{17,1},{33,17},{49,33},{2,50}... | collective-permute-start | bytes 786440 | tf_op jit(solution)/shard_map/ppermute | solution.py:341
  19.6 0.2 collective-permute-start.6
  19.8 2.7 %weights.1 = (f32[256,256]{1,0:T(8,128)S(1)}, f32[256,256]{1,0:T(8,128)S(1)}, f32[2,256,512]{2,1,0:T(8,128)S(1)}, bf16[512,512]{1,0:T(8,128)(2,1)S(1)}, bf16[512...) custom-call(s32[4]{0:T(128)S(1)} %pad_add_fusion.place, ...), custom_call_target="tpu_custom_call" | custom-call | flops 27000000 | bytes 81000 | tf_op jit(solution)/shard_map/weights/pallas_call | solution.py:46
  22.4 2.6 %collective-permute-start.7 = (f32[64,1024]{1,0:T(8,128)S(1)}, f32[64,1024]{1,0:T(8,128)S(1)}, u32[]{:S(2)}, u32[]{:S(2)}) collective-permute-start(f32[64,1024]{1,0:T(8,128)S(1)} %get-tuple-element.101), channel_id=1, source_target_pairs={{0,12},{4,0},{8,4},{12,8},{1,13},{5,1},{9,5},{13,9},{2,14},{6,2},{... | collective-permute-start | bytes 786440 | tf_op jit(solution)/shard_map/ppermute | solution.py:341
  25.0 0.0 collective-permute-start.9
  25.0 0.0 collective-permute-done.10.dy3
  25.1 1.0 %collective-permute-done.6.dx1 = f32[64,1024]{1,0:T(8,128)S(1)} collective-permute-done((f32[64,1024]{1,0:T(8,128)S(1)}, f32[64,1024]{1,0:T(8,128)S(1)}, u32[]{:S(2)}, u32[]{:S(2)}) %collective-permute-start.6) | collective-permute-done | bytes 262176 | tf_op jit(solution)/shard_map/ppermute | solution.py:341
  26.0 0.0 collective-permute-start.8
  26.0 1.8 %collective-permute-start.11 = (f32[64,1024]{1,0:T(8,128)S(1)}, f32[64,1024]{1,0:T(8,128)S(1)}, u32[]{:S(2)}, u32[]{:S(2)}) collective-permute-start(f32[64,1024]{1,0:T(8,128)S(1)} %collective-permute-done.10.dy3), channel_id=1, source_target_pairs={{0,48},{16,0},{32,16},{48,32},{1,49},{17,1},{33,17},{49,33},{2,50}... | collective-permute-start | bytes 786440 | tf_op jit(solution)/shard_map/ppermute | solution.py:341
  27.8 0.5 collective-permute-done.7.dx3
  28.3 3.1 %collective-permute-done.9.dy1 = f32[64,1024]{1,0:T(8,128)S(1)} collective-permute-done((f32[64,1024]{1,0:T(8,128)S(1)}, f32[64,1024]{1,0:T(8,128)S(1)}, u32[]{:S(2)}, u32[]{:S(2)}) %collective-permute-start.9) | collective-permute-done | bytes 262176 | tf_op jit(solution)/shard_map/ppermute | solution.py:341
  31.5 1.0 %collective-permute-done.8.dx2 = f32[64,1024]{1,0:T(8,128)S(1)} collective-permute-done((f32[64,1024]{1,0:T(8,128)S(1)}, f32[64,1024]{1,0:T(8,128)S(1)}, u32[]{:S(2)}, u32[]{:S(2)}) %collective-permute-start.8) | collective-permute-done | bytes 262176 | tf_op jit(solution)/shard_map/ppermute | solution.py:341
  32.5 0.0 collective-permute-done.11.dy2
  32.5 1.9 %grams.1 = (bf16[512,1024]{1,0:T(8,128)(2,1)S(1)}, bf16[512,1024]{1,0:T(8,128)(2,1)S(1)}, f32[192,128]{1,0:T(8,128)S(1)}, f32[192,128]{1,0:T(8,128)S(1)}) custom-call(s32[4]{0:T(128)S(1)} %pad_add_fusion.place, f32[48,1024]{1,0:T(8,128)S(1)} %get-tuple-element.100.x0, f32[16,1024]{1,0:T(8,128)S(1)} %get-tuple-element.99.y0, ...), custom_call_target="tpu_custom_call" | custom-call | flops 20000000 | bytes 60000 | tf_op jit(solution)/shard_map/grams/pallas_call | solution.py:46
  34.4 5.2 %collective-permute-start.12 = (f32[192,128]{1,0:T(8,128)S(1)}, f32[192,128]{1,0:T(8,128)S(1)}, u32[]{:S(2)}, u32[]{:S(2)}) collective-permute-start(f32[192,128]{1,0:T(8,128)S(1)} %get-tuple-element.112), channel_id=1, source_target_pairs={{0,64},{64,0},{1,65},{65,1},{2,66},{66,2},{3,67},{67,3},{4,68},{68... | collective-permute-start | bytes 294920 | tf_op jit(solution)/shard_map/ppermute | solution.py:341
  39.6 0.9 %collective-permute-done.12.b = f32[192,128]{1,0:T(8,128)S(1)} collective-permute-done((f32[192,128]{1,0:T(8,128)S(1)}, f32[192,128]{1,0:T(8,128)S(1)}, u32[]{:S(2)}, u32[]{:S(2)}) %collective-permute-start.12) | collective-permute-done | bytes 98336 | tf_op jit(solution)/shard_map/ppermute | solution.py:341
  40.6 0.6 pair_gram.1.a
  41.1 1.7 %collective-permute-start.13 = (f32[192,128]{1,0:T(8,128)S(1)}, f32[192,128]{1,0:T(8,128)S(1)}, u32[]{:S(2)}, u32[]{:S(2)}) collective-permute-start(f32[192,128]{1,0:T(8,128)S(1)} %pair_gram.1.a), channel_id=1, source_target_pairs={{0,128},{128,0},{1,129},{129,1},{2,130},{130,2},{3,131},{131,3},{4... | collective-permute-start | bytes 294920 | tf_op jit(solution)/shard_map/ppermute | solution.py:341
  42.8 3.3 %below_sums.1 = (f32[2,128,512]{2,1,0:T(8,128)S(1)}, f32[2,128,512]{2,1,0:T(8,128)S(1)}) custom-call(s32[4]{0:T(128)S(1)} %pad_add_fusion.place, bf16[512,1024]{1,0:T(8,128)(2,1)S(1)} %get-tuple-element.105.hi, bf16[512,1024]{1,0:T(8,128)(2,1)S(1)} %get-tuple-element.106.lo, bf16[1024,512]{1,0:T(8,128)(2,1)S(1)} %get-tuple-element.113.bl_hi, ...), custom_call_target="tpu_custom_call" | custom-call | flops 30000000 | bytes 90000 | tf_op jit(solution)/shard_map/below_sums/pallas_call | solution.py:46
  46.2 0.0 collective-permute-done.13.b
  46.2 0.6 row_gram.1.a
  46.7 0.7 %collective-permute-start.14 = (f32[2,128,512]{2,1,0:T(8,128)S(1)}, f32[2,128,512]{2,1,0:T(8,128)S(1)}, u32[]{:S(2)}, u32[]{:S(2)}) collective-permute-start(f32[2,128,512]{2,1,0:T(8,128)S(1)} %get-tuple-element.118), channel_id=1, source_target_pairs={{0,64},{64,0},{1,65},{65,1},{2,66},{66,2},{3,67},{67,3},{4,68},{68... | collective-permute-start | bytes 1572872 | tf_op jit(solution)/shard_map/ppermute | solution.py:341
  47.4 1.7 %collective-permute-start.17 = (f32[192,128]{1,0:T(8,128)S(1)}, f32[192,128]{1,0:T(8,128)S(1)}, u32[]{:S(2)}, u32[]{:S(2)}) collective-permute-start(f32[192,128]{1,0:T(8,128)S(1)} %row_gram.1.a), channel_id=1, source_target_pairs={{0,32},{16,48},{32,0},{48,16},{1,33},{17,49},{33,1},{49,17},{2,34}... | collective-permute-start | bytes 294920 | tf_op jit(solution)/shard_map/ppermute | solution.py:341
  49.2 0.8 %collective-permute-start.16 = (f32[192,128]{1,0:T(8,128)S(1)}, f32[192,128]{1,0:T(8,128)S(1)}, u32[]{:S(2)}, u32[]{:S(2)}) collective-permute-start(f32[192,128]{1,0:T(8,128)S(1)} %row_gram.1.a), channel_id=1, source_target_pairs={{0,48},{16,0},{32,16},{48,32},{1,49},{17,1},{33,17},{49,33},{2,50}... | collective-permute-start | bytes 294920 | tf_op jit(solution)/shard_map/ppermute | solution.py:341
  49.9 0.7 %collective-permute-start.15 = (f32[192,128]{1,0:T(8,128)S(1)}, f32[192,128]{1,0:T(8,128)S(1)}, u32[]{:S(2)}, u32[]{:S(2)}) collective-permute-start(f32[192,128]{1,0:T(8,128)S(1)} %row_gram.1.a), channel_id=1, source_target_pairs={{0,16},{16,32},{32,48},{48,0},{1,17},{17,33},{33,49},{49,1},{2,18}... | collective-permute-start | bytes 294920 | tf_op jit(solution)/shard_map/ppermute | solution.py:341
  50.6 0.0 collective-permute-done.14.got
  50.6 0.6 pair_sums.1
  51.2 4.0 %below_outputs.1 = (f32[1024,512]{1,0:T(8,128)}, f32[16,1024]{1,0:T(8,128)}, f32[16,1024]{1,0:T(8,128)}) custom-call(s32[4]{0:T(128)S(1)} %pad_add_fusion.place, bf16[512,1024]{1,0:T(8,128)(2,1)S(1)} %get-tuple-element.105.hi, bf16[512,1024]{1,0:T(8,128)(2,1)S(1)} %get-tuple-element.106.lo, bf16[512,512]{1,0:T(8,128)(2,1)S(1)} %get-tuple-element.97.w_hi, ...), custom_call_target="tpu_custom_call" | custom-call | flops 38000000 | bytes 114000 | tf_op jit(solution)/shard_map/below_outputs/pallas_call | solution.py:46
  55.3 0.0 collective-permute-done.17.d
  55.3 0.0 collective-permute-done.16.c
  55.3 0.0 collective-permute-done.15.b
  55.3 0.6 stack.21.mine
  55.9 1.3 %collective-permute-start.18 = (f32[4,192,128]{2,1,0:T(8,128)S(1)}, f32[4,192,128]{2,1,0:T(8,128)S(1)}, u32[]{:S(2)}, u32[]{:S(2)}) collective-permute-start(f32[4,192,128]{2,1,0:T(8,128)S(1)} %stack.21.mine), channel_id=1, source_target_pairs={{0,64},{64,0},{1,65},{65,1},{2,66},{66,2},{3,67},{67,3},{4,68},{68... | collective-permute-start | bytes 1179656 | tf_op jit(solution)/shard_map/ppermute | solution.py:341
  57.2 1.3 %collective-permute-start.19 = (f32[128,512]{1,0:T(8,128)S(1)}, f32[128,512]{1,0:T(8,128)S(1)}, u32[]{:S(2)}, u32[]{:S(2)}) collective-permute-start(f32[128,512]{1,0:T(8,128)S(1)} %get-tuple-element.119), channel_id=1, source_target_pairs={{0,128},{128,0},{1,129},{129,1},{2,130},{130,2},{3,131},{131,3},{4... | collective-permute-start | bytes 786440 | tf_op jit(solution)/shard_map/ppermute | solution.py:341
  58.5 0.1 collective-permute-done.18.other
  58.6 5.3 %chain.1 = (f32[64,512]{1,0:T(8,128)S(1)}, f32[64,512]{1,0:T(8,128)S(1)}, f32[256,256]{1,0:T(8,128)}, f32[256,256]{1,0:T(8,128)}, f32[256,256]{1,0:T(8,128)}) custom-call(s32[4]{0:T(128)S(1)} %pad_add_fusion.place, f32[4,192,128]{2,1,0:T(8,128)S(1)} %stack.21.mine, f32[4,192,128]{2,1,0:T(8,128)S(1)} %collective-permute-done.18.other, ...), custom_call_target="tpu_custom_call" | custom-call | flops 52000000 | bytes 156000 | tf_op jit(solution)/shard_map/chain/pallas_call | solution.py:46
  63.9 0.9 %collective-permute-done.19.got = f32[128,512]{1,0:T(8,128)S(1)} collective-permute-done((f32[128,512]{1,0:T(8,128)S(1)}, f32[128,512]{1,0:T(8,128)S(1)}, u32[]{:S(2)}, u32[]{:S(2)}) %collective-permute-start.19) | collective-permute-done | bytes 262176 | tf_op jit(solution)/shard_map/ppermute | solution.py:341
  64.8 1.3 %left.1 = (f32[64,512]{1,0:T(8,128)}, f32[64,512]{1,0:T(8,128)}) custom-call(s32[4]{0:T(128)S(1)} %pad_add_fusion.place, f32[64,512]{1,0:T(8,128)S(1)} %get-tuple-element.131.left2, f32[64,512]{1,0:T(8,128)S(1)} %get-tuple-element.132.left1, f32[128,512]{1,0:T(8,128)S(1)} %get-tuple-element.133.part, f32[128,512]{1,0:T(8,128)S(1)} %collective-permute-done.19.got), custom_call_target="tpu_custom_call" | custom-call | flops 10000000 | bytes 30000 | tf_op jit(solution)/shard_map/left/pallas_call | solution.py:46
Async XLA Ops:
  1.7 15.8 %collective-permute-start.2 = (f32[48,1024]{1,0:T(8,128)S(1)}, f32[48,1024]{1,0:T(8,128)S(1)}, u32[]{:S(2)}, u32[]{:S(2)}) collective-permute-start(f32[48,1024]{1,0:T(8,128)S(1)} %get-tuple-element.100.x0), channel_id=1, source_target_pairs={{0,8},{4,12},{8,0},{12,4},{1,9},{5,13},{9,1},{13,5},{2,10},{6,14},... | collective-permute-start | bytes 589832 | tf_op jit(solution)/shard_map/ppermute | solution.py:341
  5.3 12.1 %collective-permute-start.1 = (f32[48,1024]{1,0:T(8,128)S(1)}, f32[48,1024]{1,0:T(8,128)S(1)}, u32[]{:S(2)}, u32[]{:S(2)}) collective-permute-start(f32[48,1024]{1,0:T(8,128)S(1)} %get-tuple-element.100.x0), channel_id=1, source_target_pairs={{0,12},{4,0},{8,4},{12,8},{1,13},{5,1},{9,5},{13,9},{2,14},{6,2},{... | collective-permute-start | bytes 589832 | tf_op jit(solution)/shard_map/ppermute | solution.py:341
  6.2 11.3 %collective-permute-start = (f32[48,1024]{1,0:T(8,128)S(1)}, f32[48,1024]{1,0:T(8,128)S(1)}, u32[]{:S(2)}, u32[]{:S(2)}) collective-permute-start(f32[48,1024]{1,0:T(8,128)S(1)} %get-tuple-element.100.x0), channel_id=1, source_target_pairs={{0,4},{4,8},{8,12},{12,0},{1,5},{5,9},{9,13},{13,1},{2,6},{6,10},{... | collective-permute-start | bytes 589832 | tf_op jit(solution)/shard_map/ppermute | solution.py:341
  6.8 4.9 %collective-permute-start.5 = (f32[16,1024]{1,0:T(8,128)S(1)}, f32[16,1024]{1,0:T(8,128)S(1)}, u32[]{:S(2)}, u32[]{:S(2)}) collective-permute-start(f32[16,1024]{1,0:T(8,128)S(1)} %get-tuple-element.99.y0), channel_id=1, source_target_pairs={{0,32},{16,48},{32,0},{48,16},{1,33},{17,49},{33,1},{49,17},{2,34}... | collective-permute-start | bytes 196616 | tf_op jit(solution)/shard_map/ppermute | solution.py:341
  9.7 7.7 %collective-permute-start.4 = (f32[16,1024]{1,0:T(8,128)S(1)}, f32[16,1024]{1,0:T(8,128)S(1)}, u32[]{:S(2)}, u32[]{:S(2)}) collective-permute-start(f32[16,1024]{1,0:T(8,128)S(1)} %get-tuple-element.99.y0), channel_id=1, source_target_pairs={{0,48},{16,0},{32,16},{48,32},{1,49},{17,1},{33,17},{49,33},{2,50}... | collective-permute-start | bytes 196616 | tf_op jit(solution)/shard_map/ppermute | solution.py:341
  11.7 5.7 %collective-permute-start.3 = (f32[16,1024]{1,0:T(8,128)S(1)}, f32[16,1024]{1,0:T(8,128)S(1)}, u32[]{:S(2)}, u32[]{:S(2)}) collective-permute-start(f32[16,1024]{1,0:T(8,128)S(1)} %get-tuple-element.99.y0), channel_id=1, source_target_pairs={{0,16},{16,32},{32,48},{48,0},{1,17},{17,33},{33,49},{49,1},{2,18}... | collective-permute-start | bytes 196616 | tf_op jit(solution)/shard_map/ppermute | solution.py:341
  18.1 7.0 %collective-permute-start.10 = (f32[64,1024]{1,0:T(8,128)S(1)}, f32[64,1024]{1,0:T(8,128)S(1)}, u32[]{:S(2)}, u32[]{:S(2)}) collective-permute-start(f32[64,1024]{1,0:T(8,128)S(1)} %get-tuple-element.103), channel_id=1, source_target_pairs={{0,48},{16,0},{32,16},{48,32},{1,49},{17,1},{33,17},{49,33},{2,50}... | collective-permute-start | bytes 786440 | tf_op jit(solution)/shard_map/ppermute | solution.py:341
  19.6 6.4 %collective-permute-start.6 = (f32[64,1024]{1,0:T(8,128)S(1)}, f32[64,1024]{1,0:T(8,128)S(1)}, u32[]{:S(2)}, u32[]{:S(2)}) collective-permute-start(f32[64,1024]{1,0:T(8,128)S(1)} %get-tuple-element.101), channel_id=1, source_target_pairs={{0,4},{4,8},{8,12},{12,0},{1,5},{5,9},{9,13},{13,1},{2,6},{6,10},{... | collective-permute-start | bytes 786440 | tf_op jit(solution)/shard_map/ppermute | solution.py:341
  22.4 5.9 %collective-permute-start.7 = (f32[64,1024]{1,0:T(8,128)S(1)}, f32[64,1024]{1,0:T(8,128)S(1)}, u32[]{:S(2)}, u32[]{:S(2)}) collective-permute-start(f32[64,1024]{1,0:T(8,128)S(1)} %get-tuple-element.101), channel_id=1, source_target_pairs={{0,12},{4,0},{8,4},{12,8},{1,13},{5,1},{9,5},{13,9},{2,14},{6,2},{... | collective-permute-start | bytes 786440 | tf_op jit(solution)/shard_map/ppermute | solution.py:341
  25.0 6.4 %collective-permute-start.9 = (f32[64,1024]{1,0:T(8,128)S(1)}, f32[64,1024]{1,0:T(8,128)S(1)}, u32[]{:S(2)}, u32[]{:S(2)}) collective-permute-start(f32[64,1024]{1,0:T(8,128)S(1)} %get-tuple-element.103), channel_id=1, source_target_pairs={{0,16},{16,32},{32,48},{48,0},{1,17},{17,33},{33,49},{49,1},{2,18}... | collective-permute-start | bytes 786440 | tf_op jit(solution)/shard_map/ppermute | solution.py:341
  26.0 6.4 %collective-permute-start.8 = (f32[64,1024]{1,0:T(8,128)S(1)}, f32[64,1024]{1,0:T(8,128)S(1)}, u32[]{:S(2)}, u32[]{:S(2)}) collective-permute-start(f32[64,1024]{1,0:T(8,128)S(1)} %collective-permute-done.6.dx1), channel_id=1, source_target_pairs={{0,4},{4,8},{8,12},{12,0},{1,5},{5,9},{9,13},{13,1},{2,6},{6,10},{... | collective-permute-start | bytes 786440 | tf_op jit(solution)/shard_map/ppermute | solution.py:341
  26.0 6.4 %collective-permute-start.11 = (f32[64,1024]{1,0:T(8,128)S(1)}, f32[64,1024]{1,0:T(8,128)S(1)}, u32[]{:S(2)}, u32[]{:S(2)}) collective-permute-start(f32[64,1024]{1,0:T(8,128)S(1)} %collective-permute-done.10.dy3), channel_id=1, source_target_pairs={{0,48},{16,0},{32,16},{48,32},{1,49},{17,1},{33,17},{49,33},{2,50}... | collective-permute-start | bytes 786440 | tf_op jit(solution)/shard_map/ppermute | solution.py:341
  34.4 6.2 %collective-permute-start.12 = (f32[192,128]{1,0:T(8,128)S(1)}, f32[192,128]{1,0:T(8,128)S(1)}, u32[]{:S(2)}, u32[]{:S(2)}) collective-permute-start(f32[192,128]{1,0:T(8,128)S(1)} %get-tuple-element.112), channel_id=1, source_target_pairs={{0,64},{64,0},{1,65},{65,1},{2,66},{66,2},{3,67},{67,3},{4,68},{68... | collective-permute-start | bytes 294920 | tf_op jit(solution)/shard_map/ppermute | solution.py:341
  41.1 5.0 %collective-permute-start.13 = (f32[192,128]{1,0:T(8,128)S(1)}, f32[192,128]{1,0:T(8,128)S(1)}, u32[]{:S(2)}, u32[]{:S(2)}) collective-permute-start(f32[192,128]{1,0:T(8,128)S(1)} %pair_gram.1.a), channel_id=1, source_target_pairs={{0,128},{128,0},{1,129},{129,1},{2,130},{130,2},{3,131},{131,3},{4... | collective-permute-start | bytes 294920 | tf_op jit(solution)/shard_map/ppermute | solution.py:341
  46.7 3.9 %collective-permute-start.14 = (f32[2,128,512]{2,1,0:T(8,128)S(1)}, f32[2,128,512]{2,1,0:T(8,128)S(1)}, u32[]{:S(2)}, u32[]{:S(2)}) collective-permute-start(f32[2,128,512]{2,1,0:T(8,128)S(1)} %get-tuple-element.118), channel_id=1, source_target_pairs={{0,64},{64,0},{1,65},{65,1},{2,66},{66,2},{3,67},{67,3},{4,68},{68... | collective-permute-start | bytes 1572872 | tf_op jit(solution)/shard_map/ppermute | solution.py:341
  47.4 7.9 %collective-permute-start.17 = (f32[192,128]{1,0:T(8,128)S(1)}, f32[192,128]{1,0:T(8,128)S(1)}, u32[]{:S(2)}, u32[]{:S(2)}) collective-permute-start(f32[192,128]{1,0:T(8,128)S(1)} %row_gram.1.a), channel_id=1, source_target_pairs={{0,32},{16,48},{32,0},{48,16},{1,33},{17,49},{33,1},{49,17},{2,34}... | collective-permute-start | bytes 294920 | tf_op jit(solution)/shard_map/ppermute | solution.py:341
  49.2 6.1 %collective-permute-start.16 = (f32[192,128]{1,0:T(8,128)S(1)}, f32[192,128]{1,0:T(8,128)S(1)}, u32[]{:S(2)}, u32[]{:S(2)}) collective-permute-start(f32[192,128]{1,0:T(8,128)S(1)} %row_gram.1.a), channel_id=1, source_target_pairs={{0,48},{16,0},{32,16},{48,32},{1,49},{17,1},{33,17},{49,33},{2,50}... | collective-permute-start | bytes 294920 | tf_op jit(solution)/shard_map/ppermute | solution.py:341
  49.9 5.4 %collective-permute-start.15 = (f32[192,128]{1,0:T(8,128)S(1)}, f32[192,128]{1,0:T(8,128)S(1)}, u32[]{:S(2)}, u32[]{:S(2)}) collective-permute-start(f32[192,128]{1,0:T(8,128)S(1)} %row_gram.1.a), channel_id=1, source_target_pairs={{0,16},{16,32},{32,48},{48,0},{1,17},{17,33},{33,49},{49,1},{2,18}... | collective-permute-start | bytes 294920 | tf_op jit(solution)/shard_map/ppermute | solution.py:341
  55.9 2.7 %collective-permute-start.18 = (f32[4,192,128]{2,1,0:T(8,128)S(1)}, f32[4,192,128]{2,1,0:T(8,128)S(1)}, u32[]{:S(2)}, u32[]{:S(2)}) collective-permute-start(f32[4,192,128]{2,1,0:T(8,128)S(1)} %stack.21.mine), channel_id=1, source_target_pairs={{0,64},{64,0},{1,65},{65,1},{2,66},{66,2},{3,67},{67,3},{4,68},{68... | collective-permute-start | bytes 1179656 | tf_op jit(solution)/shard_map/ppermute | solution.py:341
  57.2 7.6 %collective-permute-start.19 = (f32[128,512]{1,0:T(8,128)S(1)}, f32[128,512]{1,0:T(8,128)S(1)}, u32[]{:S(2)}, u32[]{:S(2)}) collective-permute-start(f32[128,512]{1,0:T(8,128)S(1)} %get-tuple-element.119), channel_id=1, source_target_pairs={{0,128},{128,0},{1,129},{129,1},{2,130},{130,2},{3,131},{131,3},{4... | collective-permute-start | bytes 786440 | tf_op jit(solution)/shard_map/ppermute | solution.py:341

commit v4 on v3

--- a/solution.py
+++ b/solution.py
@@ -51,7 +51,7 @@
         scratch_shapes=list(scratch),
         compiler_params=pltpu.CompilerParams(vmem_limit_bytes=20 * 2**20),
         cost_estimate=pl.CostEstimate(
-            flops=int(micros * 1e7), transcendentals=0, bytes_accessed=int(micros * 3e4)
+            flops=int(micros * 1e9), transcendentals=0, bytes_accessed=int(micros * 3e6)
         ),
         name=name,
     )(operands[0], *held, *far)
@@ -397,8 +397,8 @@
         (),
         2.7,
     )
-    dxs.append(shifted(after(dxs[:1], w_hi)[0], "x", 1))
-    dys.append(shifted(after(dys[1:2], w_hi)[0], "y", 3))
+    dxs.append(shifted(dxs[0], "x", 1))
+    dys.append(shifted(dys[1], "y", 3))
     half = near(6 * n // 8, n // 2)
     (x0,) = after((along_x,), w_hi)
     hi, lo, keep, send = call(

time: 66.2 us -> 64.9 us (0.980)
  waiting for transfers between devices: 8.81 us -> 7.32 us
    ppermute x20, waiting for transfers between devices: 8.81 us -> 7.32 us  [shifted(): lax.ppermute(value, axis, [(i, (i + by) % count) for i in range(count)])]
  transfers between devices with their start and end apart: 20 -> 20, of which waited for: 8 -> 8; matrix products, arithmetic and copies ran while one was open for 0% -> 0% of each run, Pallas kernels for 31% -> 32%
where the time goes in v4:
time: 64.9 us; the launch traced here: 64.7 us
  starting transfers between devices  29.7 us (46%)
  Pallas kernels  26.8 us (41%)
  waiting for transfers between devices  7.32 us (11%)
  between operations  0.81 us (1%)
    ppermute x20, starting transfers between devices, shifted(): lax.ppermute(value, axis, [(i, (i + by) % count) for i in range(count)])  29.7 us
    pallas_call x13, Pallas kernels, call(): pl.pallas_call(kernel, out_shape=tuple(outs), in_specs=[SMEM] + [VMEM] *...  26.8 us
    ppermute x20, waiting for transfers between devices, shifted(): lax.ppermute(value, axis, [(i, (i + by) % count) for i in range(count)])  7.32 us
  transfers between devices with their start and end apart: 20, of which 8 were waited for; matrix products, arithmetic and copies ran while one was open for 0% of the time, Pallas kernels for 32%

profile of v4, /device:TPU:1, one launch (start us, length us, event | category | flops | bytes accessed | tf_op | source)
XLA Modules:
  0.0 64.7 jit_solution(11381581723384791104)
XLA Ops:
  0.6 0.1 pad_add_fusion.place
  0.7 1.0 %first.1 = (f32[48,1024]{1,0:T(8,128)S(1)}, f32[16,1024]{1,0:T(8,128)S(1)}) custom-call(s32[4]{0:T(128)S(1)} %pad_add_fusion.place, f32[16,1024]{1,0:T(8,128)} %bitcast.10, f32[16,1024]{1,0:T(8,128)} %bitcast.11, f32[16,1024]{1,0:T(8,128)} %bitcast.12, f32[16,1024]{1,0:T(8,128)} %bitcast.13), custom_call_target="tpu_custom_call" | custom-call | flops 1000000000 | bytes 3000000 | tf_op jit(solution)/shard_map/first/pallas_call | solution.py:46
  1.7 2.2 %collective-permute-start.3 = (f32[16,1024]{1,0:T(8,128)S(1)}, f32[16,1024]{1,0:T(8,128)S(1)}, u32[]{:S(2)}, u32[]{:S(2)}) collective-permute-start(f32[16,1024]{1,0:T(8,128)S(1)} %get-tuple-element.97.y0), channel_id=1, source_target_pairs={{0,16},{16,32},{32,48},{48,0},{1,17},{17,33},{33,49},{49,1},{2,18}... | collective-permute-start | bytes 196616 | tf_op jit(solution)/shard_map/ppermute | solution.py:341
  3.9 1.2 %collective-permute-start = (f32[48,1024]{1,0:T(8,128)S(1)}, f32[48,1024]{1,0:T(8,128)S(1)}, u32[]{:S(2)}, u32[]{:S(2)}) collective-permute-start(f32[48,1024]{1,0:T(8,128)S(1)} %get-tuple-element.98.x0), channel_id=1, source_target_pairs={{0,4},{4,8},{8,12},{12,0},{1,5},{5,9},{9,13},{13,1},{2,6},{6,10},{... | collective-permute-start | bytes 589832 | tf_op jit(solution)/shard_map/ppermute | solution.py:341
  5.1 1.5 %collective-permute-start.1 = (f32[48,1024]{1,0:T(8,128)S(1)}, f32[48,1024]{1,0:T(8,128)S(1)}, u32[]{:S(2)}, u32[]{:S(2)}) collective-permute-start(f32[48,1024]{1,0:T(8,128)S(1)} %get-tuple-element.98.x0), channel_id=1, source_target_pairs={{0,12},{4,0},{8,4},{12,8},{1,13},{5,1},{9,5},{13,9},{2,14},{6,2},{... | collective-permute-start | bytes 589832 | tf_op jit(solution)/shard_map/ppermute | solution.py:341
  6.6 1.5 %collective-permute-start.2 = (f32[48,1024]{1,0:T(8,128)S(1)}, f32[48,1024]{1,0:T(8,128)S(1)}, u32[]{:S(2)}, u32[]{:S(2)}) collective-permute-start(f32[48,1024]{1,0:T(8,128)S(1)} %get-tuple-element.98.x0), channel_id=1, source_target_pairs={{0,8},{4,12},{8,0},{12,4},{1,9},{5,13},{9,1},{13,5},{2,10},{6,14},... | collective-permute-start | bytes 589832 | tf_op jit(solution)/shard_map/ppermute | solution.py:341
  8.1 1.5 %collective-permute-start.4 = (f32[16,1024]{1,0:T(8,128)S(1)}, f32[16,1024]{1,0:T(8,128)S(1)}, u32[]{:S(2)}, u32[]{:S(2)}) collective-permute-start(f32[16,1024]{1,0:T(8,128)S(1)} %get-tuple-element.97.y0), channel_id=1, source_target_pairs={{0,48},{16,0},{32,16},{48,32},{1,49},{17,1},{33,17},{49,33},{2,50}... | collective-permute-start | bytes 196616 | tf_op jit(solution)/shard_map/ppermute | solution.py:341
  9.6 0.0 collective-permute-done.3.y1
  9.6 1.6 %collective-permute-start.5 = (f32[16,1024]{1,0:T(8,128)S(1)}, f32[16,1024]{1,0:T(8,128)S(1)}, u32[]{:S(2)}, u32[]{:S(2)}) collective-permute-start(f32[16,1024]{1,0:T(8,128)S(1)} %get-tuple-element.97.y0), channel_id=1, source_target_pairs={{0,32},{16,48},{32,0},{48,16},{1,33},{17,49},{33,1},{49,17},{2,34}... | collective-permute-start | bytes 196616 | tf_op jit(solution)/shard_map/ppermute | solution.py:341
  11.2 4.4 %inverses.1 = (f32[256,256]{1,0:T(8,128)S(1)}, f32[256,256]{1,0:T(8,128)S(1)}, f32[256,256]{1,0:T(8,128)S(1)}, f32[256,256]{1,0:T(8,128)S(1)}, f32[256,256]{1,0:...) custom-call(s32[4]{0:T(128)S(1)} %pad_add_fusion.place, ...), custom_call_target="tpu_custom_call" | custom-call | flops 4000000000 | bytes 12000000 | tf_op jit(solution)/shard_map/inverses/pallas_call | solution.py:46
  15.6 0.0 collective-permute-done.4.y3
  15.6 0.0 collective-permute-done.5.y2
  15.6 0.0 collective-permute-done.x1
  15.6 0.0 collective-permute-done.1.x3
  15.6 0.1 collective-permute-done.2.x2
  15.8 0.6 far.1
  16.3 1.7 %collective-permute-start.10 = (f32[64,1024]{1,0:T(8,128)S(1)}, f32[64,1024]{1,0:T(8,128)S(1)}, u32[]{:S(2)}, u32[]{:S(2)}) collective-permute-start(f32[64,1024]{1,0:T(8,128)S(1)} %get-tuple-element.100), channel_id=1, source_target_pairs={{0,48},{16,0},{32,16},{48,32},{1,49},{17,1},{33,17},{49,33},{2,50}... | collective-permute-start | bytes 786440 | tf_op jit(solution)/shard_map/ppermute | solution.py:341
  18.0 0.5 collective-permute-start.6
  18.5 2.2 %collective-permute-start.7 = (f32[64,1024]{1,0:T(8,128)S(1)}, f32[64,1024]{1,0:T(8,128)S(1)}, u32[]{:S(2)}, u32[]{:S(2)}) collective-permute-start(f32[64,1024]{1,0:T(8,128)S(1)} %get-tuple-element.99), channel_id=1, source_target_pairs={{0,12},{4,0},{8,4},{12,8},{1,13},{5,1},{9,5},{13,9},{2,14},{6,2},{... | collective-permute-start | bytes 786440 | tf_op jit(solution)/shard_map/ppermute | solution.py:341
  20.7 0.0 collective-permute-start.9
  20.7 1.3 %collective-permute-done.10.dy3 = f32[64,1024]{1,0:T(8,128)S(1)} collective-permute-done((f32[64,1024]{1,0:T(8,128)S(1)}, f32[64,1024]{1,0:T(8,128)S(1)}, u32[]{:S(2)}, u32[]{:S(2)}) %collective-permute-start.10) | collective-permute-done | bytes 262176 | tf_op jit(solution)/shard_map/ppermute | solution.py:341
  22.0 3.2 %collective-permute-start.11 = (f32[64,1024]{1,0:T(8,128)S(1)}, f32[64,1024]{1,0:T(8,128)S(1)}, u32[]{:S(2)}, u32[]{:S(2)}) collective-permute-start(f32[64,1024]{1,0:T(8,128)S(1)} %collective-permute-done.10.dy3), channel_id=1, source_target_pairs={{0,48},{16,0},{32,16},{48,32},{1,49},{17,1},{33,17},{49,33},{2,50}... | collective-permute-start | bytes 786440 | tf_op jit(solution)/shard_map/ppermute | solution.py:341
  25.2 0.0 collective-permute-done.6.dx1
  25.2 0.1 collective-permute-start.8
  25.3 2.7 %weights.1 = (f32[256,256]{1,0:T(8,128)S(1)}, f32[256,256]{1,0:T(8,128)S(1)}, f32[2,256,512]{2,1,0:T(8,128)S(1)}, bf16[512,512]{1,0:T(8,128)(2,1)S(1)}, bf16[512...) custom-call(s32[4]{0:T(128)S(1)} %pad_add_fusion.place, ...), custom_call_target="tpu_custom_call" | custom-call | flops 2700000000 | bytes 8100000 | tf_op jit(solution)/shard_map/weights/pallas_call | solution.py:46
  28.0 0.0 collective-permute-done.7.dx3
  28.0 0.0 collective-permute-done.9.dy1
  28.0 0.5 collective-permute-done.11.dy2
  28.5 3.1 %collective-permute-done.8.dx2 = f32[64,1024]{1,0:T(8,128)S(1)} collective-permute-done((f32[64,1024]{1,0:T(8,128)S(1)}, f32[64,1024]{1,0:T(8,128)S(1)}, u32[]{:S(2)}, u32[]{:S(2)}) %collective-permute-start.8) | collective-permute-done | bytes 262176 | tf_op jit(solution)/shard_map/ppermute | solution.py:341
  31.7 1.9 %grams.1 = (bf16[512,1024]{1,0:T(8,128)(2,1)S(1)}, bf16[512,1024]{1,0:T(8,128)(2,1)S(1)}, f32[192,128]{1,0:T(8,128)S(1)}, f32[192,128]{1,0:T(8,128)S(1)}) custom-call(s32[4]{0:T(128)S(1)} %pad_add_fusion.place, f32[48,1024]{1,0:T(8,128)S(1)} %get-tuple-element.98.x0, f32[16,1024]{1,0:T(8,128)S(1)} %get-tuple-element.97.y0, ...), custom_call_target="tpu_custom_call" | custom-call | flops 2000000000 | bytes 6000000 | tf_op jit(solution)/shard_map/grams/pallas_call | solution.py:46
  33.6 4.2 %collective-permute-start.12 = (f32[192,128]{1,0:T(8,128)S(1)}, f32[192,128]{1,0:T(8,128)S(1)}, u32[]{:S(2)}, u32[]{:S(2)}) collective-permute-start(f32[192,128]{1,0:T(8,128)S(1)} %get-tuple-element.108), channel_id=1, source_target_pairs={{0,64},{64,0},{1,65},{65,1},{2,66},{66,2},{3,67},{67,3},{4,68},{68... | collective-permute-start | bytes 294920 | tf_op jit(solution)/shard_map/ppermute | solution.py:341
  37.8 0.9 %collective-permute-done.12.b = f32[192,128]{1,0:T(8,128)S(1)} collective-permute-done((f32[192,128]{1,0:T(8,128)S(1)}, f32[192,128]{1,0:T(8,128)S(1)}, u32[]{:S(2)}, u32[]{:S(2)}) %collective-permute-start.12) | collective-permute-done | bytes 98336 | tf_op jit(solution)/shard_map/ppermute | solution.py:341
  38.7 0.6 pair_gram.1.a
  39.3 1.8 %collective-permute-start.13 = (f32[192,128]{1,0:T(8,128)S(1)}, f32[192,128]{1,0:T(8,128)S(1)}, u32[]{:S(2)}, u32[]{:S(2)}) collective-permute-start(f32[192,128]{1,0:T(8,128)S(1)} %pair_gram.1.a), channel_id=1, source_target_pairs={{0,128},{128,0},{1,129},{129,1},{2,130},{130,2},{3,131},{131,3},{4... | collective-permute-start | bytes 294920 | tf_op jit(solution)/shard_map/ppermute | solution.py:341
  41.1 3.3 %below_sums.1 = (f32[2,128,512]{2,1,0:T(8,128)S(1)}, f32[2,128,512]{2,1,0:T(8,128)S(1)}) custom-call(s32[4]{0:T(128)S(1)} %pad_add_fusion.place, bf16[512,1024]{1,0:T(8,128)(2,1)S(1)} %get-tuple-element.101.hi, bf16[512,1024]{1,0:T(8,128)(2,1)S(1)} %get-tuple-element.102.lo, bf16[1024,512]{1,0:T(8,128)(2,1)S(1)} %get-tuple-element.109.bl_hi, ...), custom_call_target="tpu_custom_call" | custom-call | flops 3000000000 | bytes 9000000 | tf_op jit(solution)/shard_map/below_sums/pallas_call | solution.py:46
  44.5 0.0 collective-permute-done.13.b
  44.5 0.6 row_gram.1.a
  45.0 0.7 %collective-permute-start.14 = (f32[2,128,512]{2,1,0:T(8,128)S(1)}, f32[2,128,512]{2,1,0:T(8,128)S(1)}, u32[]{:S(2)}, u32[]{:S(2)}) collective-permute-start(f32[2,128,512]{2,1,0:T(8,128)S(1)} %get-tuple-element.114), channel_id=1, source_target_pairs={{0,64},{64,0},{1,65},{65,1},{2,66},{66,2},{3,67},{67,3},{4,68},{68... | collective-permute-start | bytes 1572872 | tf_op jit(solution)/shard_map/ppermute | solution.py:341
  45.8 0.0 collective-permute-start.15
  45.8 2.7 %collective-permute-start.16 = (f32[192,128]{1,0:T(8,128)S(1)}, f32[192,128]{1,0:T(8,128)S(1)}, u32[]{:S(2)}, u32[]{:S(2)}) collective-permute-start(f32[192,128]{1,0:T(8,128)S(1)} %row_gram.1.a), channel_id=1, source_target_pairs={{0,48},{16,0},{32,16},{48,32},{1,49},{17,1},{33,17},{49,33},{2,50}... | collective-permute-start | bytes 294920 | tf_op jit(solution)/shard_map/ppermute | solution.py:341
  48.4 0.0 collective-permute-start.17
  48.5 0.0 collective-permute-done.14.got
  48.5 0.6 pair_sums.1
  49.1 4.1 %below_outputs.1 = (f32[1024,512]{1,0:T(8,128)}, f32[16,1024]{1,0:T(8,128)}, f32[16,1024]{1,0:T(8,128)}) custom-call(s32[4]{0:T(128)S(1)} %pad_add_fusion.place, bf16[512,1024]{1,0:T(8,128)(2,1)S(1)} %get-tuple-element.101.hi, bf16[512,1024]{1,0:T(8,128)(2,1)S(1)} %get-tuple-element.102.lo, bf16[512,512]{1,0:T(8,128)(2,1)S(1)} %get-tuple-element.95.w_hi, ...), custom_call_target="tpu_custom_call" | custom-call | flops 3800000000 | bytes 11400000 | tf_op jit(solution)/shard_map/below_outputs/pallas_call | solution.py:46
  53.2 0.0 collective-permute-done.15.b
  53.2 0.0 collective-permute-done.16.c
  53.2 0.2 collective-permute-done.17.d
  53.4 0.6 stack.21.mine
  54.0 1.9 %collective-permute-start.18 = (f32[4,192,128]{2,1,0:T(8,128)S(1)}, f32[4,192,128]{2,1,0:T(8,128)S(1)}, u32[]{:S(2)}, u32[]{:S(2)}) collective-permute-start(f32[4,192,128]{2,1,0:T(8,128)S(1)} %stack.21.mine), channel_id=1, source_target_pairs={{0,64},{64,0},{1,65},{65,1},{2,66},{66,2},{3,67},{67,3},{4,68},{68... | collective-permute-start | bytes 1179656 | tf_op jit(solution)/shard_map/ppermute | solution.py:341
  55.9 1.2 %collective-permute-start.19 = (f32[128,512]{1,0:T(8,128)S(1)}, f32[128,512]{1,0:T(8,128)S(1)}, u32[]{:S(2)}, u32[]{:S(2)}) collective-permute-start(f32[128,512]{1,0:T(8,128)S(1)} %get-tuple-element.115), channel_id=1, source_target_pairs={{0,128},{128,0},{1,129},{129,1},{2,130},{130,2},{3,131},{131,3},{4... | collective-permute-start | bytes 786440 | tf_op jit(solution)/shard_map/ppermute | solution.py:341
  57.1 0.1 collective-permute-done.18.other
  57.2 5.3 %chain.1 = (f32[64,512]{1,0:T(8,128)S(1)}, f32[64,512]{1,0:T(8,128)S(1)}, f32[256,256]{1,0:T(8,128)}, f32[256,256]{1,0:T(8,128)}, f32[256,256]{1,0:T(8,128)}) custom-call(s32[4]{0:T(128)S(1)} %pad_add_fusion.place, f32[4,192,128]{2,1,0:T(8,128)S(1)} %stack.21.mine, f32[4,192,128]{2,1,0:T(8,128)S(1)} %collective-permute-done.18.other, ...), custom_call_target="tpu_custom_call" | custom-call | flops 5200000000 | bytes 15600000 | tf_op jit(solution)/shard_map/chain/pallas_call | solution.py:46
  62.5 0.9 %collective-permute-done.19.got = f32[128,512]{1,0:T(8,128)S(1)} collective-permute-done((f32[128,512]{1,0:T(8,128)S(1)}, f32[128,512]{1,0:T(8,128)S(1)}, u32[]{:S(2)}, u32[]{:S(2)}) %collective-permute-start.19) | collective-permute-done | bytes 262176 | tf_op jit(solution)/shard_map/ppermute | solution.py:341
  63.4 1.3 %left.1 = (f32[64,512]{1,0:T(8,128)}, f32[64,512]{1,0:T(8,128)}) custom-call(s32[4]{0:T(128)S(1)} %pad_add_fusion.place, f32[64,512]{1,0:T(8,128)S(1)} %get-tuple-element.127.left2, f32[64,512]{1,0:T(8,128)S(1)} %get-tuple-element.128.left1, f32[128,512]{1,0:T(8,128)S(1)} %get-tuple-element.129.part, f32[128,512]{1,0:T(8,128)S(1)} %collective-permute-done.19.got), custom_call_target="tpu_custom_call" | custom-call | flops 1000000000 | bytes 3000000 | tf_op jit(solution)/shard_map/left/pallas_call | solution.py:46
Async XLA Ops:
  1.7 7.9 %collective-permute-start.3 = (f32[16,1024]{1,0:T(8,128)S(1)}, f32[16,1024]{1,0:T(8,128)S(1)}, u32[]{:S(2)}, u32[]{:S(2)}) collective-permute-start(f32[16,1024]{1,0:T(8,128)S(1)} %get-tuple-element.97.y0), channel_id=1, source_target_pairs={{0,16},{16,32},{32,48},{48,0},{1,17},{17,33},{33,49},{49,1},{2,18}... | collective-permute-start | bytes 196616 | tf_op jit(solution)/shard_map/ppermute | solution.py:341
  3.9 11.7 %collective-permute-start = (f32[48,1024]{1,0:T(8,128)S(1)}, f32[48,1024]{1,0:T(8,128)S(1)}, u32[]{:S(2)}, u32[]{:S(2)}) collective-permute-start(f32[48,1024]{1,0:T(8,128)S(1)} %get-tuple-element.98.x0), channel_id=1, source_target_pairs={{0,4},{4,8},{8,12},{12,0},{1,5},{5,9},{9,13},{13,1},{2,6},{6,10},{... | collective-permute-start | bytes 589832 | tf_op jit(solution)/shard_map/ppermute | solution.py:341
  5.1 10.5 %collective-permute-start.1 = (f32[48,1024]{1,0:T(8,128)S(1)}, f32[48,1024]{1,0:T(8,128)S(1)}, u32[]{:S(2)}, u32[]{:S(2)}) collective-permute-start(f32[48,1024]{1,0:T(8,128)S(1)} %get-tuple-element.98.x0), channel_id=1, source_target_pairs={{0,12},{4,0},{8,4},{12,8},{1,13},{5,1},{9,5},{13,9},{2,14},{6,2},{... | collective-permute-start | bytes 589832 | tf_op jit(solution)/shard_map/ppermute | solution.py:341
  6.6 9.2 %collective-permute-start.2 = (f32[48,1024]{1,0:T(8,128)S(1)}, f32[48,1024]{1,0:T(8,128)S(1)}, u32[]{:S(2)}, u32[]{:S(2)}) collective-permute-start(f32[48,1024]{1,0:T(8,128)S(1)} %get-tuple-element.98.x0), channel_id=1, source_target_pairs={{0,8},{4,12},{8,0},{12,4},{1,9},{5,13},{9,1},{13,5},{2,10},{6,14},... | collective-permute-start | bytes 589832 | tf_op jit(solution)/shard_map/ppermute | solution.py:341
  8.1 7.5 %collective-permute-start.4 = (f32[16,1024]{1,0:T(8,128)S(1)}, f32[16,1024]{1,0:T(8,128)S(1)}, u32[]{:S(2)}, u32[]{:S(2)}) collective-permute-start(f32[16,1024]{1,0:T(8,128)S(1)} %get-tuple-element.97.y0), channel_id=1, source_target_pairs={{0,48},{16,0},{32,16},{48,32},{1,49},{17,1},{33,17},{49,33},{2,50}... | collective-permute-start | bytes 196616 | tf_op jit(solution)/shard_map/ppermute | solution.py:341
  9.6 6.0 %collective-permute-start.5 = (f32[16,1024]{1,0:T(8,128)S(1)}, f32[16,1024]{1,0:T(8,128)S(1)}, u32[]{:S(2)}, u32[]{:S(2)}) collective-permute-start(f32[16,1024]{1,0:T(8,128)S(1)} %get-tuple-element.97.y0), channel_id=1, source_target_pairs={{0,32},{16,48},{32,0},{48,16},{1,33},{17,49},{33,1},{49,17},{2,34}... | collective-permute-start | bytes 196616 | tf_op jit(solution)/shard_map/ppermute | solution.py:341
  16.3 5.6 %collective-permute-start.10 = (f32[64,1024]{1,0:T(8,128)S(1)}, f32[64,1024]{1,0:T(8,128)S(1)}, u32[]{:S(2)}, u32[]{:S(2)}) collective-permute-start(f32[64,1024]{1,0:T(8,128)S(1)} %get-tuple-element.100), channel_id=1, source_target_pairs={{0,48},{16,0},{32,16},{48,32},{1,49},{17,1},{33,17},{49,33},{2,50}... | collective-permute-start | bytes 786440 | tf_op jit(solution)/shard_map/ppermute | solution.py:341
  18.0 7.2 %collective-permute-start.6 = (f32[64,1024]{1,0:T(8,128)S(1)}, f32[64,1024]{1,0:T(8,128)S(1)}, u32[]{:S(2)}, u32[]{:S(2)}) collective-permute-start(f32[64,1024]{1,0:T(8,128)S(1)} %get-tuple-element.99), channel_id=1, source_target_pairs={{0,4},{4,8},{8,12},{12,0},{1,5},{5,9},{9,13},{13,1},{2,6},{6,10},{... | collective-permute-start | bytes 786440 | tf_op jit(solution)/shard_map/ppermute | solution.py:341
  18.5 9.5 %collective-permute-start.7 = (f32[64,1024]{1,0:T(8,128)S(1)}, f32[64,1024]{1,0:T(8,128)S(1)}, u32[]{:S(2)}, u32[]{:S(2)}) collective-permute-start(f32[64,1024]{1,0:T(8,128)S(1)} %get-tuple-element.99), channel_id=1, source_target_pairs={{0,12},{4,0},{8,4},{12,8},{1,13},{5,1},{9,5},{13,9},{2,14},{6,2},{... | collective-permute-start | bytes 786440 | tf_op jit(solution)/shard_map/ppermute | solution.py:341
  20.7 7.3 %collective-permute-start.9 = (f32[64,1024]{1,0:T(8,128)S(1)}, f32[64,1024]{1,0:T(8,128)S(1)}, u32[]{:S(2)}, u32[]{:S(2)}) collective-permute-start(f32[64,1024]{1,0:T(8,128)S(1)} %get-tuple-element.100), channel_id=1, source_target_pairs={{0,16},{16,32},{32,48},{48,0},{1,17},{17,33},{33,49},{49,1},{2,18}... | collective-permute-start | bytes 786440 | tf_op jit(solution)/shard_map/ppermute | solution.py:341
  22.0 6.6 %collective-permute-start.11 = (f32[64,1024]{1,0:T(8,128)S(1)}, f32[64,1024]{1,0:T(8,128)S(1)}, u32[]{:S(2)}, u32[]{:S(2)}) collective-permute-start(f32[64,1024]{1,0:T(8,128)S(1)} %collective-permute-done.10.dy3), channel_id=1, source_target_pairs={{0,48},{16,0},{32,16},{48,32},{1,49},{17,1},{33,17},{49,33},{2,50}... | collective-permute-start | bytes 786440 | tf_op jit(solution)/shard_map/ppermute | solution.py:341
  25.2 6.4 %collective-permute-start.8 = (f32[64,1024]{1,0:T(8,128)S(1)}, f32[64,1024]{1,0:T(8,128)S(1)}, u32[]{:S(2)}, u32[]{:S(2)}) collective-permute-start(f32[64,1024]{1,0:T(8,128)S(1)} %collective-permute-done.6.dx1), channel_id=1, source_target_pairs={{0,4},{4,8},{8,12},{12,0},{1,5},{5,9},{9,13},{13,1},{2,6},{6,10},{... | collective-permute-start | bytes 786440 | tf_op jit(solution)/shard_map/ppermute | solution.py:341
  33.6 5.2 %collective-permute-start.12 = (f32[192,128]{1,0:T(8,128)S(1)}, f32[192,128]{1,0:T(8,128)S(1)}, u32[]{:S(2)}, u32[]{:S(2)}) collective-permute-start(f32[192,128]{1,0:T(8,128)S(1)} %get-tuple-element.108), channel_id=1, source_target_pairs={{0,64},{64,0},{1,65},{65,1},{2,66},{66,2},{3,67},{67,3},{4,68},{68... | collective-permute-start | bytes 294920 | tf_op jit(solution)/shard_map/ppermute | solution.py:341
  39.3 5.2 %collective-permute-start.13 = (f32[192,128]{1,0:T(8,128)S(1)}, f32[192,128]{1,0:T(8,128)S(1)}, u32[]{:S(2)}, u32[]{:S(2)}) collective-permute-start(f32[192,128]{1,0:T(8,128)S(1)} %pair_gram.1.a), channel_id=1, source_target_pairs={{0,128},{128,0},{1,129},{129,1},{2,130},{130,2},{3,131},{131,3},{4... | collective-permute-start | bytes 294920 | tf_op jit(solution)/shard_map/ppermute | solution.py:341
  45.0 3.4 %collective-permute-start.14 = (f32[2,128,512]{2,1,0:T(8,128)S(1)}, f32[2,128,512]{2,1,0:T(8,128)S(1)}, u32[]{:S(2)}, u32[]{:S(2)}) collective-permute-start(f32[2,128,512]{2,1,0:T(8,128)S(1)} %get-tuple-element.114), channel_id=1, source_target_pairs={{0,64},{64,0},{1,65},{65,1},{2,66},{66,2},{3,67},{67,3},{4,68},{68... | collective-permute-start | bytes 1572872 | tf_op jit(solution)/shard_map/ppermute | solution.py:341
  45.8 7.4 %collective-permute-start.15 = (f32[192,128]{1,0:T(8,128)S(1)}, f32[192,128]{1,0:T(8,128)S(1)}, u32[]{:S(2)}, u32[]{:S(2)}) collective-permute-start(f32[192,128]{1,0:T(8,128)S(1)} %row_gram.1.a), channel_id=1, source_target_pairs={{0,16},{16,32},{32,48},{48,0},{1,17},{17,33},{33,49},{49,1},{2,18}... | collective-permute-start | bytes 294920 | tf_op jit(solution)/shard_map/ppermute | solution.py:341
  45.8 7.4 %collective-permute-start.16 = (f32[192,128]{1,0:T(8,128)S(1)}, f32[192,128]{1,0:T(8,128)S(1)}, u32[]{:S(2)}, u32[]{:S(2)}) collective-permute-start(f32[192,128]{1,0:T(8,128)S(1)} %row_gram.1.a), channel_id=1, source_target_pairs={{0,48},{16,0},{32,16},{48,32},{1,49},{17,1},{33,17},{49,33},{2,50}... | collective-permute-start | bytes 294920 | tf_op jit(solution)/shard_map/ppermute | solution.py:341
  48.4 5.0 %collective-permute-start.17 = (f32[192,128]{1,0:T(8,128)S(1)}, f32[192,128]{1,0:T(8,128)S(1)}, u32[]{:S(2)}, u32[]{:S(2)}) collective-permute-start(f32[192,128]{1,0:T(8,128)S(1)} %row_gram.1.a), channel_id=1, source_target_pairs={{0,32},{16,48},{32,0},{48,16},{1,33},{17,49},{33,1},{49,17},{2,34}... | collective-permute-start | bytes 294920 | tf_op jit(solution)/shard_map/ppermute | solution.py:341
  54.0 3.2 %collective-permute-start.18 = (f32[4,192,128]{2,1,0:T(8,128)S(1)}, f32[4,192,128]{2,1,0:T(8,128)S(1)}, u32[]{:S(2)}, u32[]{:S(2)}) collective-permute-start(f32[4,192,128]{2,1,0:T(8,128)S(1)} %stack.21.mine), channel_id=1, source_target_pairs={{0,64},{64,0},{1,65},{65,1},{2,66},{66,2},{3,67},{67,3},{4,68},{68... | collective-permute-start | bytes 1179656 | tf_op jit(solution)/shard_map/ppermute | solution.py:341
  55.9 7.6 %collective-permute-start.19 = (f32[128,512]{1,0:T(8,128)S(1)}, f32[128,512]{1,0:T(8,128)S(1)}, u32[]{:S(2)}, u32[]{:S(2)}) collective-permute-start(f32[128,512]{1,0:T(8,128)S(1)} %get-tuple-element.115), channel_id=1, source_target_pairs={{0,128},{128,0},{1,129},{129,1},{2,130},{130,2},{3,131},{131,3},{4... | collective-permute-start | bytes 786440 | tf_op jit(solution)/shard_map/ppermute | solution.py:341

commit v5 on v4

--- a/solution.py
+++ b/solution.py
@@ -286,7 +286,7 @@
 
 
 def chain_kernel(
-    place, mine, other, a2, a2t, a1, a1t, d2t, d1t, c, gd2, gd1, gc, l2, l1, gl2, gl1,
+    place, mine, other, a2, a2t, a1, a1t, d2t, d1t, c, gd2, gd1, gc, l2, l1, gl2, gl1, part, got,
     left2, left1, o_diag2, o_diag1, o_cross, whole, tall, rows2, rows1, rowsx, rowsxt,
 ):
     n = a2.shape[0]
@@ -326,14 +326,18 @@
     share = gl2.shape[0]
     at = pl.ds(pl.multiple_of((place[3] * 2 + place[2]) * share, share), share)
     l2s, l1s = (split(l2[...]), split(l1[...]))
-    left2[...] = gl2[...] - dot3(split(rows2[at]), l2s) - dot3(split(rowsx[at]), l1s)
-    left1[...] = gl1[...] - dot3(split(rowsxt[at]), l2s) - dot3(split(rows1[at]), l1s)
-
-
-def left_kernel(place, left2, left1, part, got, o_left2, o_left1):
-    share = left2.shape[0]
-    o_left2[...] = left2[...] - (part[:share] + got[:share])
-    o_left1[...] = left1[...] - (part[share:] + got[share:])
+    left2[...] = (
+        gl2[...]
+        - (part[:share] + got[:share])
+        - dot3(split(rows2[at]), l2s)
+        - dot3(split(rowsx[at]), l1s)
+    )
+    left1[...] = (
+        gl1[...]
+        - dot3(split(rowsxt[at]), l2s)
+        - (part[share:] + got[share:])
+        - dot3(split(rows1[at]), l1s)
+    )
 
 
 def shifted(value, axis, by):
@@ -453,21 +457,18 @@
         stack_kernel,
         "stack",
         (near(4, *half.shape),),
-        (place, *after((gram,), s2t), *shifts(gram, "y")),
+        (place, *after((gram,), (s2t, got)), *shifts(gram, "y")),
         (),
         0.8,
     )
     left2, left1, diag2, diag1, cross = call(
         chain_kernel,
         "chain",
-        (near(*gl2.shape), near(*gl2.shape), shaped(n, n), shaped(n, n), shaped(n, n)),
-        (place, mine, shifted(mine, "core", 1), a2, a2t, a1, a1t, d2t, d1t, c, gd2, gd1, gc, l2, l1, gl2, gl1),
+        (shaped(*gl2.shape), shaped(*gl2.shape), shaped(n, n), shaped(n, n), shaped(n, n)),
+        (place, mine, shifted(mine, "core", 1), a2, a2t, a1, a1t, d2t, d1t, c, gd2, gd1, gc, l2, l1, gl2, gl1, part, got),
         (pltpu.VMEM((4, n, n // 2), F32), pltpu.VMEM((4, n, n // 4), F32))
         + (pltpu.VMEM((n, n), F32),) * 4,
         5.2,
-    )
-    left2, left1 = call(
-        left_kernel, "left", (shaped(*gl2.shape),) * 2, (place, left2, left1, part, got), (), 1.0
     )
     return out_below, left2, left1, diag2, diag1, cross, s2t.T, s1t.T
 

time: 64.9 us -> 65.7 us (1.012)
  waiting for transfers between devices: 7.32 us -> 9.1 us
  Pallas kernels: 26.8 us -> 25.6 us
    ppermute x20, waiting for transfers between devices: 7.32 us -> 9.1 us  [shifted(): lax.ppermute(value, axis, [(i, (i + by) % count) for i in range(count)])]
    pallas_call x13 -> x12, Pallas kernels: 26.8 us -> 25.6 us  [call(): pl.pallas_call(kernel, out_shape=tuple(outs), in_specs=[SMEM] + [VMEM] *...]
  transfers between devices with their start and end apart: 20 -> 20, of which waited for: 8 -> 7; matrix products, arithmetic and copies ran while one was open for 0% -> 0% of each run, Pallas kernels for 32% -> 23%
where the time goes in v5:
time: 65.7 us; the launch traced here: 65.5 us
  starting transfers between devices  29.9 us (46%)
  Pallas kernels  25.6 us (39%)
  waiting for transfers between devices  9.1 us (14%)
  between operations  0.8 us (1%)
    ppermute x20, starting transfers between devices, shifted(): lax.ppermute(value, axis, [(i, (i + by) % count) for i in range(count)])  29.9 us
    pallas_call x12, Pallas kernels, call(): pl.pallas_call(kernel, out_shape=tuple(outs), in_specs=[SMEM] + [VMEM] *...  25.6 us
    ppermute x20, waiting for transfers between devices, shifted(): lax.ppermute(value, axis, [(i, (i + by) % count) for i in range(count)])  9.1 us
  transfers between devices with their start and end apart: 20, of which 7 were waited for; matrix products, arithmetic and copies ran while one was open for 0% of the time, Pallas kernels for 23%

profile of v5, /device:TPU:1, one launch (start us, length us, event | category | flops | bytes accessed | tf_op | source)
XLA Modules:
  0.0 65.5 jit_solution(13548379280233879001)
XLA Ops:
  0.6 0.1 pad_add_fusion.place
  0.7 1.0 %first.1 = (f32[48,1024]{1,0:T(8,128)S(1)}, f32[16,1024]{1,0:T(8,128)S(1)}) custom-call(s32[4]{0:T(128)S(1)} %pad_add_fusion.place, f32[16,1024]{1,0:T(8,128)} %bitcast.10, f32[16,1024]{1,0:T(8,128)} %bitcast.11, f32[16,1024]{1,0:T(8,128)} %bitcast.12, f32[16,1024]{1,0:T(8,128)} %bitcast.13), custom_call_target="tpu_custom_call" | custom-call | flops 1000000000 | bytes 3000000 | tf_op jit(solution)/shard_map/first/pallas_call | solution.py:46
  1.7 2.2 %collective-permute-start.3 = (f32[16,1024]{1,0:T(8,128)S(1)}, f32[16,1024]{1,0:T(8,128)S(1)}, u32[]{:S(2)}, u32[]{:S(2)}) collective-permute-start(f32[16,1024]{1,0:T(8,128)S(1)} %get-tuple-element.95.y0), channel_id=1, source_target_pairs={{0,16},{16,32},{32,48},{48,0},{1,17},{17,33},{33,49},{49,1},{2,18}... | collective-permute-start | bytes 196616 | tf_op jit(solution)/shard_map/ppermute | solution.py:345
  3.9 1.2 %collective-permute-start = (f32[48,1024]{1,0:T(8,128)S(1)}, f32[48,1024]{1,0:T(8,128)S(1)}, u32[]{:S(2)}, u32[]{:S(2)}) collective-permute-start(f32[48,1024]{1,0:T(8,128)S(1)} %get-tuple-element.96.x0), channel_id=1, source_target_pairs={{0,4},{4,8},{8,12},{12,0},{1,5},{5,9},{9,13},{13,1},{2,6},{6,10},{... | collective-permute-start | bytes 589832 | tf_op jit(solution)/shard_map/ppermute | solution.py:345
  5.1 1.5 %collective-permute-start.1 = (f32[48,1024]{1,0:T(8,128)S(1)}, f32[48,1024]{1,0:T(8,128)S(1)}, u32[]{:S(2)}, u32[]{:S(2)}) collective-permute-start(f32[48,1024]{1,0:T(8,128)S(1)} %get-tuple-element.96.x0), channel_id=1, source_target_pairs={{0,12},{4,0},{8,4},{12,8},{1,13},{5,1},{9,5},{13,9},{2,14},{6,2},{... | collective-permute-start | bytes 589832 | tf_op jit(solution)/shard_map/ppermute | solution.py:345
  6.6 1.5 %collective-permute-start.2 = (f32[48,1024]{1,0:T(8,128)S(1)}, f32[48,1024]{1,0:T(8,128)S(1)}, u32[]{:S(2)}, u32[]{:S(2)}) collective-permute-start(f32[48,1024]{1,0:T(8,128)S(1)} %get-tuple-element.96.x0), channel_id=1, source_target_pairs={{0,8},{4,12},{8,0},{12,4},{1,9},{5,13},{9,1},{13,5},{2,10},{6,14},... | collective-permute-start | bytes 589832 | tf_op jit(solution)/shard_map/ppermute | solution.py:345
  8.1 1.5 %collective-permute-start.4 = (f32[16,1024]{1,0:T(8,128)S(1)}, f32[16,1024]{1,0:T(8,128)S(1)}, u32[]{:S(2)}, u32[]{:S(2)}) collective-permute-start(f32[16,1024]{1,0:T(8,128)S(1)} %get-tuple-element.95.y0), channel_id=1, source_target_pairs={{0,48},{16,0},{32,16},{48,32},{1,49},{17,1},{33,17},{49,33},{2,50}... | collective-permute-start | bytes 196616 | tf_op jit(solution)/shard_map/ppermute | solution.py:345
  9.6 0.0 collective-permute-done.3.y1
  9.6 1.6 %collective-permute-start.5 = (f32[16,1024]{1,0:T(8,128)S(1)}, f32[16,1024]{1,0:T(8,128)S(1)}, u32[]{:S(2)}, u32[]{:S(2)}) collective-permute-start(f32[16,1024]{1,0:T(8,128)S(1)} %get-tuple-element.95.y0), channel_id=1, source_target_pairs={{0,32},{16,48},{32,0},{48,16},{1,33},{17,49},{33,1},{49,17},{2,34}... | collective-permute-start | bytes 196616 | tf_op jit(solution)/shard_map/ppermute | solution.py:345
  11.2 4.4 %inverses.1 = (f32[256,256]{1,0:T(8,128)S(1)}, f32[256,256]{1,0:T(8,128)S(1)}, f32[256,256]{1,0:T(8,128)S(1)}, f32[256,256]{1,0:T(8,128)S(1)}, f32[256,256]{1,0:...) custom-call(s32[4]{0:T(128)S(1)} %pad_add_fusion.place, ...), custom_call_target="tpu_custom_call" | custom-call | flops 4000000000 | bytes 12000000 | tf_op jit(solution)/shard_map/inverses/pallas_call | solution.py:46
  15.6 0.0 collective-permute-done.4.y3
  15.6 0.0 collective-permute-done.5.y2
  15.6 0.0 collective-permute-done.x1
  15.6 0.0 collective-permute-done.1.x3
  15.6 0.1 collective-permute-done.2.x2
  15.8 0.6 far.1
  16.3 1.7 %collective-permute-start.10 = (f32[64,1024]{1,0:T(8,128)S(1)}, f32[64,1024]{1,0:T(8,128)S(1)}, u32[]{:S(2)}, u32[]{:S(2)}) collective-permute-start(f32[64,1024]{1,0:T(8,128)S(1)} %get-tuple-element.98), channel_id=1, source_target_pairs={{0,48},{16,0},{32,16},{48,32},{1,49},{17,1},{33,17},{49,33},{2,50}... | collective-permute-start | bytes 786440 | tf_op jit(solution)/shard_map/ppermute | solution.py:345
  18.0 0.5 collective-permute-start.6
  18.5 2.2 %collective-permute-start.7 = (f32[64,1024]{1,0:T(8,128)S(1)}, f32[64,1024]{1,0:T(8,128)S(1)}, u32[]{:S(2)}, u32[]{:S(2)}) collective-permute-start(f32[64,1024]{1,0:T(8,128)S(1)} %get-tuple-element.97), channel_id=1, source_target_pairs={{0,12},{4,0},{8,4},{12,8},{1,13},{5,1},{9,5},{13,9},{2,14},{6,2},{... | collective-permute-start | bytes 786440 | tf_op jit(solution)/shard_map/ppermute | solution.py:345
  20.7 0.0 collective-permute-start.9
  20.7 1.3 %collective-permute-done.10.dy3 = f32[64,1024]{1,0:T(8,128)S(1)} collective-permute-done((f32[64,1024]{1,0:T(8,128)S(1)}, f32[64,1024]{1,0:T(8,128)S(1)}, u32[]{:S(2)}, u32[]{:S(2)}) %collective-permute-start.10) | collective-permute-done | bytes 262176 | tf_op jit(solution)/shard_map/ppermute | solution.py:345
  22.0 3.2 %collective-permute-start.11 = (f32[64,1024]{1,0:T(8,128)S(1)}, f32[64,1024]{1,0:T(8,128)S(1)}, u32[]{:S(2)}, u32[]{:S(2)}) collective-permute-start(f32[64,1024]{1,0:T(8,128)S(1)} %collective-permute-done.10.dy3), channel_id=1, source_target_pairs={{0,48},{16,0},{32,16},{48,32},{1,49},{17,1},{33,17},{49,33},{2,50}... | collective-permute-start | bytes 786440 | tf_op jit(solution)/shard_map/ppermute | solution.py:345
  25.2 0.0 collective-permute-done.6.dx1
  25.2 0.1 collective-permute-start.8
  25.3 2.7 %weights.1 = (f32[256,256]{1,0:T(8,128)S(1)}, f32[256,256]{1,0:T(8,128)S(1)}, f32[2,256,512]{2,1,0:T(8,128)S(1)}, bf16[512,512]{1,0:T(8,128)(2,1)S(1)}, bf16[512...) custom-call(s32[4]{0:T(128)S(1)} %pad_add_fusion.place, ...), custom_call_target="tpu_custom_call" | custom-call | flops 2700000000 | bytes 8100000 | tf_op jit(solution)/shard_map/weights/pallas_call | solution.py:46
  28.0 0.0 collective-permute-done.7.dx3
  28.0 0.0 collective-permute-done.9.dy1
  28.0 0.5 collective-permute-done.11.dy2
  28.5 3.1 %collective-permute-done.8.dx2 = f32[64,1024]{1,0:T(8,128)S(1)} collective-permute-done((f32[64,1024]{1,0:T(8,128)S(1)}, f32[64,1024]{1,0:T(8,128)S(1)}, u32[]{:S(2)}, u32[]{:S(2)}) %collective-permute-start.8) | collective-permute-done | bytes 262176 | tf_op jit(solution)/shard_map/ppermute | solution.py:345
  31.7 1.9 %grams.1 = (bf16[512,1024]{1,0:T(8,128)(2,1)S(1)}, bf16[512,1024]{1,0:T(8,128)(2,1)S(1)}, f32[192,128]{1,0:T(8,128)S(1)}, f32[192,128]{1,0:T(8,128)S(1)}) custom-call(s32[4]{0:T(128)S(1)} %pad_add_fusion.place, f32[48,1024]{1,0:T(8,128)S(1)} %get-tuple-element.96.x0, f32[16,1024]{1,0:T(8,128)S(1)} %get-tuple-element.95.y0, ...), custom_call_target="tpu_custom_call" | custom-call | flops 2000000000 | bytes 6000000 | tf_op jit(solution)/shard_map/grams/pallas_call | solution.py:46
  33.6 4.2 %collective-permute-start.12 = (f32[192,128]{1,0:T(8,128)S(1)}, f32[192,128]{1,0:T(8,128)S(1)}, u32[]{:S(2)}, u32[]{:S(2)}) collective-permute-start(f32[192,128]{1,0:T(8,128)S(1)} %get-tuple-element.106), channel_id=1, source_target_pairs={{0,64},{64,0},{1,65},{65,1},{2,66},{66,2},{3,67},{67,3},{4,68},{68... | collective-permute-start | bytes 294920 | tf_op jit(solution)/shard_map/ppermute | solution.py:345
  37.8 0.9 %collective-permute-done.12.b = f32[192,128]{1,0:T(8,128)S(1)} collective-permute-done((f32[192,128]{1,0:T(8,128)S(1)}, f32[192,128]{1,0:T(8,128)S(1)}, u32[]{:S(2)}, u32[]{:S(2)}) %collective-permute-start.12) | collective-permute-done | bytes 98336 | tf_op jit(solution)/shard_map/ppermute | solution.py:345
  38.7 0.6 pair_gram.1.a
  39.3 1.8 %collective-permute-start.13 = (f32[192,128]{1,0:T(8,128)S(1)}, f32[192,128]{1,0:T(8,128)S(1)}, u32[]{:S(2)}, u32[]{:S(2)}) collective-permute-start(f32[192,128]{1,0:T(8,128)S(1)} %pair_gram.1.a), channel_id=1, source_target_pairs={{0,128},{128,0},{1,129},{129,1},{2,130},{130,2},{3,131},{131,3},{4... | collective-permute-start | bytes 294920 | tf_op jit(solution)/shard_map/ppermute | solution.py:345
  41.1 3.3 %below_sums.1 = (f32[2,128,512]{2,1,0:T(8,128)S(1)}, f32[2,128,512]{2,1,0:T(8,128)S(1)}) custom-call(s32[4]{0:T(128)S(1)} %pad_add_fusion.place, bf16[512,1024]{1,0:T(8,128)(2,1)S(1)} %get-tuple-element.99.hi, bf16[512,1024]{1,0:T(8,128)(2,1)S(1)} %get-tuple-element.100.lo, bf16[1024,512]{1,0:T(8,128)(2,1)S(1)} %get-tuple-element.107.bl_hi, ...), custom_call_target="tpu_custom_call" | custom-call | flops 3000000000 | bytes 9000000 | tf_op jit(solution)/shard_map/below_sums/pallas_call | solution.py:46
  44.5 0.0 collective-permute-done.13.b
  44.5 0.6 row_gram.1.a
  45.0 0.7 %collective-permute-start.14 = (f32[2,128,512]{2,1,0:T(8,128)S(1)}, f32[2,128,512]{2,1,0:T(8,128)S(1)}, u32[]{:S(2)}, u32[]{:S(2)}) collective-permute-start(f32[2,128,512]{2,1,0:T(8,128)S(1)} %get-tuple-element.112), channel_id=1, source_target_pairs={{0,64},{64,0},{1,65},{65,1},{2,66},{66,2},{3,67},{67,3},{4,68},{68... | collective-permute-start | bytes 1572872 | tf_op jit(solution)/shard_map/ppermute | solution.py:345
  45.8 0.0 collective-permute-start.16
  45.8 2.7 %collective-permute-start.17 = (f32[192,128]{1,0:T(8,128)S(1)}, f32[192,128]{1,0:T(8,128)S(1)}, u32[]{:S(2)}, u32[]{:S(2)}) collective-permute-start(f32[192,128]{1,0:T(8,128)S(1)} %row_gram.1.a), channel_id=1, source_target_pairs={{0,48},{16,0},{32,16},{48,32},{1,49},{17,1},{33,17},{49,33},{2,50}... | collective-permute-start | bytes 294920 | tf_op jit(solution)/shard_map/ppermute | solution.py:345
  48.4 0.0 collective-permute-start.18
  48.5 0.0 collective-permute-done.14.got
  48.5 0.6 pair_sums.1
  49.1 1.3 %collective-permute-start.15 = (f32[128,512]{1,0:T(8,128)S(1)}, f32[128,512]{1,0:T(8,128)S(1)}, u32[]{:S(2)}, u32[]{:S(2)}) collective-permute-start(f32[128,512]{1,0:T(8,128)S(1)} %get-tuple-element.113), channel_id=1, source_target_pairs={{0,128},{128,0},{1,129},{129,1},{2,130},{130,2},{3,131},{131,3},{4... | collective-permute-start | bytes 786440 | tf_op jit(solution)/shard_map/ppermute | solution.py:345
  50.4 4.1 %below_outputs.1 = (f32[1024,512]{1,0:T(8,128)}, f32[16,1024]{1,0:T(8,128)}, f32[16,1024]{1,0:T(8,128)}) custom-call(s32[4]{0:T(128)S(1)} %pad_add_fusion.place, bf16[512,1024]{1,0:T(8,128)(2,1)S(1)} %get-tuple-element.99.hi, bf16[512,1024]{1,0:T(8,128)(2,1)S(1)} %get-tuple-element.100.lo, bf16[512,512]{1,0:T(8,128)(2,1)S(1)} %get-tuple-element.93.w_hi, ...), custom_call_target="tpu_custom_call" | custom-call | flops 3800000000 | bytes 11400000 | tf_op jit(solution)/shard_map/below_outputs/pallas_call | solution.py:46
  54.5 1.7 %collective-permute-done.15.got = f32[128,512]{1,0:T(8,128)S(1)} collective-permute-done((f32[128,512]{1,0:T(8,128)S(1)}, f32[128,512]{1,0:T(8,128)S(1)}, u32[]{:S(2)}, u32[]{:S(2)}) %collective-permute-start.15) | collective-permute-done | bytes 262176 | tf_op jit(solution)/shard_map/ppermute | solution.py:345
  56.2 0.0 collective-permute-done.16.b
  56.2 0.0 collective-permute-done.17.c
  56.2 0.0 collective-permute-done.18.d
  56.2 0.6 stack.21.mine
  56.8 2.0 %collective-permute-start.19 = (f32[4,192,128]{2,1,0:T(8,128)S(1)}, f32[4,192,128]{2,1,0:T(8,128)S(1)}, u32[]{:S(2)}, u32[]{:S(2)}) collective-permute-start(f32[4,192,128]{2,1,0:T(8,128)S(1)} %stack.21.mine), channel_id=1, source_target_pairs={{0,64},{64,0},{1,65},{65,1},{2,66},{66,2},{3,67},{67,3},{4,68},{68... | collective-permute-start | bytes 1179656 | tf_op jit(solution)/shard_map/ppermute | solution.py:345
  58.8 1.3 %collective-permute-done.19.other = f32[4,192,128]{2,1,0:T(8,128)S(1)} collective-permute-done((f32[4,192,128]{2,1,0:T(8,128)S(1)}, f32[4,192,128]{2,1,0:T(8,128)S(1)}, u32[]{:S(2)}, u32[]{:S(2)}) %collective-permute-start.19) | collective-permute-done | bytes 393248 | tf_op jit(solution)/shard_map/ppermute | solution.py:345
  60.1 5.4 %chain.1 = (f32[64,512]{1,0:T(8,128)}, f32[64,512]{1,0:T(8,128)}, f32[256,256]{1,0:T(8,128)}, f32[256,256]{1,0:T(8,128)}, f32[256,256]{1,0:T(8,128)}) custom-call(s32[4]{0:T(128)S(1)} %pad_add_fusion.place, f32[4,192,128]{2,1,0:T(8,128)S(1)} %stack.21.mine, f32[4,192,128]{2,1,0:T(8,128)S(1)} %collective-permute-done.19.other, ...), custom_call_target="tpu_custom_call" | custom-call | flops 5200000000 | bytes 15600000 | tf_op jit(solution)/shard_map/chain/pallas_call | solution.py:46
Async XLA Ops:
  1.7 7.9 %collective-permute-start.3 = (f32[16,1024]{1,0:T(8,128)S(1)}, f32[16,1024]{1,0:T(8,128)S(1)}, u32[]{:S(2)}, u32[]{:S(2)}) collective-permute-start(f32[16,1024]{1,0:T(8,128)S(1)} %get-tuple-element.95.y0), channel_id=1, source_target_pairs={{0,16},{16,32},{32,48},{48,0},{1,17},{17,33},{33,49},{49,1},{2,18}... | collective-permute-start | bytes 196616 | tf_op jit(solution)/shard_map/ppermute | solution.py:345
  3.9 11.7 %collective-permute-start = (f32[48,1024]{1,0:T(8,128)S(1)}, f32[48,1024]{1,0:T(8,128)S(1)}, u32[]{:S(2)}, u32[]{:S(2)}) collective-permute-start(f32[48,1024]{1,0:T(8,128)S(1)} %get-tuple-element.96.x0), channel_id=1, source_target_pairs={{0,4},{4,8},{8,12},{12,0},{1,5},{5,9},{9,13},{13,1},{2,6},{6,10},{... | collective-permute-start | bytes 589832 | tf_op jit(solution)/shard_map/ppermute | solution.py:345
  5.1 10.5 %collective-permute-start.1 = (f32[48,1024]{1,0:T(8,128)S(1)}, f32[48,1024]{1,0:T(8,128)S(1)}, u32[]{:S(2)}, u32[]{:S(2)}) collective-permute-start(f32[48,1024]{1,0:T(8,128)S(1)} %get-tuple-element.96.x0), channel_id=1, source_target_pairs={{0,12},{4,0},{8,4},{12,8},{1,13},{5,1},{9,5},{13,9},{2,14},{6,2},{... | collective-permute-start | bytes 589832 | tf_op jit(solution)/shard_map/ppermute | solution.py:345
  6.6 9.2 %collective-permute-start.2 = (f32[48,1024]{1,0:T(8,128)S(1)}, f32[48,1024]{1,0:T(8,128)S(1)}, u32[]{:S(2)}, u32[]{:S(2)}) collective-permute-start(f32[48,1024]{1,0:T(8,128)S(1)} %get-tuple-element.96.x0), channel_id=1, source_target_pairs={{0,8},{4,12},{8,0},{12,4},{1,9},{5,13},{9,1},{13,5},{2,10},{6,14},... | collective-permute-start | bytes 589832 | tf_op jit(solution)/shard_map/ppermute | solution.py:345
  8.1 7.5 %collective-permute-start.4 = (f32[16,1024]{1,0:T(8,128)S(1)}, f32[16,1024]{1,0:T(8,128)S(1)}, u32[]{:S(2)}, u32[]{:S(2)}) collective-permute-start(f32[16,1024]{1,0:T(8,128)S(1)} %get-tuple-element.95.y0), channel_id=1, source_target_pairs={{0,48},{16,0},{32,16},{48,32},{1,49},{17,1},{33,17},{49,33},{2,50}... | collective-permute-start | bytes 196616 | tf_op jit(solution)/shard_map/ppermute | solution.py:345
  9.6 6.0 %collective-permute-start.5 = (f32[16,1024]{1,0:T(8,128)S(1)}, f32[16,1024]{1,0:T(8,128)S(1)}, u32[]{:S(2)}, u32[]{:S(2)}) collective-permute-start(f32[16,1024]{1,0:T(8,128)S(1)} %get-tuple-element.95.y0), channel_id=1, source_target_pairs={{0,32},{16,48},{32,0},{48,16},{1,33},{17,49},{33,1},{49,17},{2,34}... | collective-permute-start | bytes 196616 | tf_op jit(solution)/shard_map/ppermute | solution.py:345
  16.3 5.6 %collective-permute-start.10 = (f32[64,1024]{1,0:T(8,128)S(1)}, f32[64,1024]{1,0:T(8,128)S(1)}, u32[]{:S(2)}, u32[]{:S(2)}) collective-permute-start(f32[64,1024]{1,0:T(8,128)S(1)} %get-tuple-element.98), channel_id=1, source_target_pairs={{0,48},{16,0},{32,16},{48,32},{1,49},{17,1},{33,17},{49,33},{2,50}... | collective-permute-start | bytes 786440 | tf_op jit(solution)/shard_map/ppermute | solution.py:345
  18.0 7.2 %collective-permute-start.6 = (f32[64,1024]{1,0:T(8,128)S(1)}, f32[64,1024]{1,0:T(8,128)S(1)}, u32[]{:S(2)}, u32[]{:S(2)}) collective-permute-start(f32[64,1024]{1,0:T(8,128)S(1)} %get-tuple-element.97), channel_id=1, source_target_pairs={{0,4},{4,8},{8,12},{12,0},{1,5},{5,9},{9,13},{13,1},{2,6},{6,10},{... | collective-permute-start | bytes 786440 | tf_op jit(solution)/shard_map/ppermute | solution.py:345
  18.5 9.5 %collective-permute-start.7 = (f32[64,1024]{1,0:T(8,128)S(1)}, f32[64,1024]{1,0:T(8,128)S(1)}, u32[]{:S(2)}, u32[]{:S(2)}) collective-permute-start(f32[64,1024]{1,0:T(8,128)S(1)} %get-tuple-element.97), channel_id=1, source_target_pairs={{0,12},{4,0},{8,4},{12,8},{1,13},{5,1},{9,5},{13,9},{2,14},{6,2},{... | collective-permute-start | bytes 786440 | tf_op jit(solution)/shard_map/ppermute | solution.py:345
  20.7 7.3 %collective-permute-start.9 = (f32[64,1024]{1,0:T(8,128)S(1)}, f32[64,1024]{1,0:T(8,128)S(1)}, u32[]{:S(2)}, u32[]{:S(2)}) collective-permute-start(f32[64,1024]{1,0:T(8,128)S(1)} %get-tuple-element.98), channel_id=1, source_target_pairs={{0,16},{16,32},{32,48},{48,0},{1,17},{17,33},{33,49},{49,1},{2,18}... | collective-permute-start | bytes 786440 | tf_op jit(solution)/shard_map/ppermute | solution.py:345
  22.0 6.6 %collective-permute-start.11 = (f32[64,1024]{1,0:T(8,128)S(1)}, f32[64,1024]{1,0:T(8,128)S(1)}, u32[]{:S(2)}, u32[]{:S(2)}) collective-permute-start(f32[64,1024]{1,0:T(8,128)S(1)} %collective-permute-done.10.dy3), channel_id=1, source_target_pairs={{0,48},{16,0},{32,16},{48,32},{1,49},{17,1},{33,17},{49,33},{2,50}... | collective-permute-start | bytes 786440 | tf_op jit(solution)/shard_map/ppermute | solution.py:345
  25.2 6.4 %collective-permute-start.8 = (f32[64,1024]{1,0:T(8,128)S(1)}, f32[64,1024]{1,0:T(8,128)S(1)}, u32[]{:S(2)}, u32[]{:S(2)}) collective-permute-start(f32[64,1024]{1,0:T(8,128)S(1)} %collective-permute-done.6.dx1), channel_id=1, source_target_pairs={{0,4},{4,8},{8,12},{12,0},{1,5},{5,9},{9,13},{13,1},{2,6},{6,10},{... | collective-permute-start | bytes 786440 | tf_op jit(solution)/shard_map/ppermute | solution.py:345
  33.6 5.2 %collective-permute-start.12 = (f32[192,128]{1,0:T(8,128)S(1)}, f32[192,128]{1,0:T(8,128)S(1)}, u32[]{:S(2)}, u32[]{:S(2)}) collective-permute-start(f32[192,128]{1,0:T(8,128)S(1)} %get-tuple-element.106), channel_id=1, source_target_pairs={{0,64},{64,0},{1,65},{65,1},{2,66},{66,2},{3,67},{67,3},{4,68},{68... | collective-permute-start | bytes 294920 | tf_op jit(solution)/shard_map/ppermute | solution.py:345
  39.3 5.2 %collective-permute-start.13 = (f32[192,128]{1,0:T(8,128)S(1)}, f32[192,128]{1,0:T(8,128)S(1)}, u32[]{:S(2)}, u32[]{:S(2)}) collective-permute-start(f32[192,128]{1,0:T(8,128)S(1)} %pair_gram.1.a), channel_id=1, source_target_pairs={{0,128},{128,0},{1,129},{129,1},{2,130},{130,2},{3,131},{131,3},{4... | collective-permute-start | bytes 294920 | tf_op jit(solution)/shard_map/ppermute | solution.py:345
  45.0 3.4 %collective-permute-start.14 = (f32[2,128,512]{2,1,0:T(8,128)S(1)}, f32[2,128,512]{2,1,0:T(8,128)S(1)}, u32[]{:S(2)}, u32[]{:S(2)}) collective-permute-start(f32[2,128,512]{2,1,0:T(8,128)S(1)} %get-tuple-element.112), channel_id=1, source_target_pairs={{0,64},{64,0},{1,65},{65,1},{2,66},{66,2},{3,67},{67,3},{4,68},{68... | collective-permute-start | bytes 1572872 | tf_op jit(solution)/shard_map/ppermute | solution.py:345
  45.8 10.4 %collective-permute-start.16 = (f32[192,128]{1,0:T(8,128)S(1)}, f32[192,128]{1,0:T(8,128)S(1)}, u32[]{:S(2)}, u32[]{:S(2)}) collective-permute-start(f32[192,128]{1,0:T(8,128)S(1)} %row_gram.1.a), channel_id=1, source_target_pairs={{0,16},{16,32},{32,48},{48,0},{1,17},{17,33},{33,49},{49,1},{2,18}... | collective-permute-start | bytes 294920 | tf_op jit(solution)/shard_map/ppermute | solution.py:345
  45.8 10.4 %collective-permute-start.17 = (f32[192,128]{1,0:T(8,128)S(1)}, f32[192,128]{1,0:T(8,128)S(1)}, u32[]{:S(2)}, u32[]{:S(2)}) collective-permute-start(f32[192,128]{1,0:T(8,128)S(1)} %row_gram.1.a), channel_id=1, source_target_pairs={{0,48},{16,0},{32,16},{48,32},{1,49},{17,1},{33,17},{49,33},{2,50}... | collective-permute-start | bytes 294920 | tf_op jit(solution)/shard_map/ppermute | solution.py:345
  48.4 7.7 %collective-permute-start.18 = (f32[192,128]{1,0:T(8,128)S(1)}, f32[192,128]{1,0:T(8,128)S(1)}, u32[]{:S(2)}, u32[]{:S(2)}) collective-permute-start(f32[192,128]{1,0:T(8,128)S(1)} %row_gram.1.a), channel_id=1, source_target_pairs={{0,32},{16,48},{32,0},{48,16},{1,33},{17,49},{33,1},{49,17},{2,34}... | collective-permute-start | bytes 294920 | tf_op jit(solution)/shard_map/ppermute | solution.py:345
  49.1 7.1 %collective-permute-start.15 = (f32[128,512]{1,0:T(8,128)S(1)}, f32[128,512]{1,0:T(8,128)S(1)}, u32[]{:S(2)}, u32[]{:S(2)}) collective-permute-start(f32[128,512]{1,0:T(8,128)S(1)} %get-tuple-element.113), channel_id=1, source_target_pairs={{0,128},{128,0},{1,129},{129,1},{2,130},{130,2},{3,131},{131,3},{4... | collective-permute-start | bytes 786440 | tf_op jit(solution)/shard_map/ppermute | solution.py:345
  56.8 3.4 %collective-permute-start.19 = (f32[4,192,128]{2,1,0:T(8,128)S(1)}, f32[4,192,128]{2,1,0:T(8,128)S(1)}, u32[]{:S(2)}, u32[]{:S(2)}) collective-permute-start(f32[4,192,128]{2,1,0:T(8,128)S(1)} %stack.21.mine), channel_id=1, source_target_pairs={{0,64},{64,0},{1,65},{65,1},{2,66},{66,2},{3,67},{67,3},{4,68},{68... | collective-permute-start | bytes 1179656 | tf_op jit(solution)/shard_map/ppermute | solution.py:345
